TPU v7x, 32 devices: a whole 2x2x4 slice. The times are simulated.
32 devices in a mesh: gx: 2 (over y), gy: 16 (over z, x, core).
Axes of the slice: x: 2, y: 2, z: 4, core: 2. Of those that a mesh axis runs over, the one named last changes fastest.
Arguments:
- agents: bfloat16 [4, 64, 128, 256], P('gx', 'gy'), may hold values from -14 to 14
- block_fill: int32 [4, 64], replicated, may hold values from 64 to 96, as said below
- neighbours: int32 [4, 64, 4], P('gx', 'gy'), may hold values from 0 to 23, all different within a row
- target_slot: int32 [4, 64, 128], P('gx', 'gy'), may hold values from -1 to 1535, as said below
- attention_in: bfloat16 [256, 768], replicated, may hold values from -0.375 to 0.375
- attention_out: bfloat16 [256, 256], replicated, may hold values from -0.375 to 0.375
- policy_in: bfloat16 [512, 1024], replicated, may hold values from -0.25 to 0.25
- policy_mid: bfloat16 [2, 1024, 1024], replicated, may hold values from -0.1875 to 0.1875
- policy_out: bfloat16 [1024, 128], replicated, may hold values from -0.1875 to 0.1875
Outputs:
- actions: bfloat16 [4, 64, 128, 128], P('gx', 'gy')
- batch_obs: bfloat16 [2, 16, 768, 512], P('gx', 'gy')
Inputs may be any that keep to these rules, and one draw needn't show every extreme that they name: The live slots of a block are its first block_fill ones; a tile holds at most 768 live agents. `neighbours`: the 4 directions of a block are distinct; direction d numbers the offsets (dx, dy) with -2 <= dx, dy <= 2 other than (0, 0) in row-major order. `target_slot`: -1 exactly for the slots at or beyond their block's fill; a live slot in a block of x index i holds o * 768 + (i // 2) * 384 + r with an owner o and 0 <= r < 384, and no two slots of one tile hold the same value.
All inputs are finite; a program needn't handle non-finite values.
Results may differ from a plain program's by a relative error of at most 0.0079.
Values may be sent and summed in bfloat16 or wider, within the bound.
No kernel may reach another device: no remote copies, remote signals or barrier semaphores. Data moves between devices by JAX's collectives and lax.ppermute only.
A program may use at most 64 MiB of HBM per device.

v0:
```python
import math

import jax
import jax.numpy as jnp
from jax import lax
from jax.sharding import PartitionSpec as P

HEADS = 4


score_cap = 30.0
norm_eps = 1e-06


def extended(block, sides, width):
    for axis, dim in sides:
        count = lax.axis_size(axis)
        forward = [(i, i + 1) for i in range(count - 1)]
        backward = [(target, source) for source, target in forward]
        low = lax.ppermute(
            lax.slice_in_dim(block, block.shape[dim] - width, None, axis=dim), axis, forward
        )
        high = lax.ppermute(lax.slice_in_dim(block, 0, width, axis=dim), axis, backward)
        block = jnp.concatenate([low, block, high], axis=dim)
    return block


def direction_steps(chosen):
    cell_index = chosen + (chosen >= 12).astype(jnp.int32)
    return (cell_index // 5 - 2, cell_index % 5 - 2)


def attend(queries, key_rows, value_rows, key_count, attention_out):
    group_size, block_len, row_width = queries.shape
    key_blocks = key_rows.shape[1]
    head_size = row_width // HEADS
    key_flat = key_rows.reshape(group_size, key_blocks * block_len, row_width)
    value_flat = value_rows.reshape(group_size, key_blocks * block_len, row_width)
    slot_index = jnp.arange(block_len, dtype=jnp.int32)
    live_keys = (slot_index[None, None, :] < key_count[:, :, None]).reshape(
        group_size, 1, key_blocks * block_len
    )
    head_of_column = jnp.arange(row_width, dtype=jnp.int32) // head_size
    context = jnp.zeros((group_size, block_len, row_width), jnp.float32)
    for head_index in range(HEADS):
        head_mask = head_of_column == head_index
        masked_queries = jnp.where(head_mask[None, None, :], queries, jnp.zeros_like(queries))
        raw_scores = jnp.einsum(
            "cqf,ckf->cqk", masked_queries, key_flat, preferred_element_type=jnp.float32
        ) * (1.0 / math.sqrt(head_size))
        capped = score_cap * jnp.tanh(raw_scores / score_cap)
        exp_scores = jnp.where(live_keys, jnp.exp(capped), jnp.zeros_like(capped))
        weights = (exp_scores / jnp.sum(exp_scores, axis=-1, keepdims=True)).astype(jnp.bfloat16)
        head_context = jnp.einsum(
            "cqk,ckf->cqf", weights, value_flat, preferred_element_type=jnp.float32
        )
        context = context + jnp.where(
            head_mask[None, None, :], head_context, jnp.zeros_like(head_context)
        )
    context = context.astype(jnp.bfloat16)
    mixed_rows = jnp.dot(
        context.reshape(group_size * block_len, row_width),
        attention_out,
        preferred_element_type=jnp.float32,
    )
    inv_norm = lax.rsqrt(jnp.mean(mixed_rows * mixed_rows, axis=-1, keepdims=True) + norm_eps)
    return (mixed_rows * inv_norm).astype(jnp.bfloat16)


def policy(rows, policy_in, policy_mid, policy_out):
    hidden = jax.nn.silu(jnp.dot(rows, policy_in, preferred_element_type=jnp.float32)).astype(
        jnp.bfloat16
    )
    for level_index in range(policy_mid.shape[0]):
        hidden = jax.nn.silu(
            jnp.dot(hidden, policy_mid[level_index], preferred_element_type=jnp.float32)
        ).astype(jnp.bfloat16)
    return jnp.dot(hidden, policy_out, preferred_element_type=jnp.float32).astype(jnp.bfloat16)


def on_device(
    agents,
    block_fill,
    neighbours,
    target_slot,
    attention_in,
    attention_out,
    policy_in,
    policy_mid,
    policy_out,
):
    blocks_x, blocks_y, block_len, row_width = agents.shape
    all_blocks = blocks_x * blocks_y
    slot_count = all_blocks * block_len
    owners = lax.axis_size("gx")
    capacity = 3 * slot_count // (4 * owners)
    batch_rows = owners * capacity
    agent_rows = agents.reshape(slot_count, row_width)
    corner_x = lax.axis_index("gx") * blocks_x
    corner_y = lax.axis_index("gy") * blocks_y
    fill_near = lax.dynamic_slice(
        jnp.pad(block_fill, 2), (corner_x, corner_y), (blocks_x + 4, blocks_y + 4)
    )
    query_weight = attention_in[:, :row_width]
    key_weight = attention_in[:, row_width : 2 * row_width]
    value_weight = attention_in[:, 2 * row_width :]
    queries = jnp.dot(agent_rows, query_weight, preferred_element_type=jnp.float32).astype(
        jnp.bfloat16
    )
    near_blocks = (blocks_x + 4) * (blocks_y + 4)
    near_rows = extended(agents, (("gx", 0), ("gy", 1)), 2)
    near_flat = near_rows.reshape(-1, row_width)
    near_key = jnp.dot(near_flat, key_weight, preferred_element_type=jnp.float32).astype(
        jnp.bfloat16
    )
    near_value = jnp.dot(near_flat, value_weight, preferred_element_type=jnp.float32).astype(
        jnp.bfloat16
    )
    near_key = near_key.reshape(near_blocks, block_len, row_width)
    near_value = near_value.reshape(near_blocks, block_len, row_width)
    block_ids = jnp.arange(all_blocks, dtype=jnp.int32)
    step_x, step_y = direction_steps(neighbours.reshape(all_blocks, -1))
    home_x = (block_ids // blocks_y + 2)[:, None]
    home_y = (block_ids % blocks_y + 2)[:, None]
    near_x = jnp.concatenate([home_x, home_x + step_x], axis=1)
    near_y = jnp.concatenate([home_y, home_y + step_y], axis=1)
    key_index = near_x * (blocks_y + 4) + near_y
    key_count = jnp.take(fill_near.reshape(-1), key_index, axis=0)
    group_size = min(all_blocks, 8)
    groups = all_blocks // group_size

    def attend_group(group_args):
        group_queries, group_index, group_count = group_args
        group_keys = jnp.take(near_key, group_index, axis=0)
        group_values = jnp.take(near_value, group_index, axis=0)
        return attend(group_queries, group_keys, group_values, group_count, attention_out)

    summary = lax.map(
        attend_group,
        (
            queries.reshape(groups, group_size, block_len, row_width),
            key_index.reshape(groups, group_size, -1),
            key_count.reshape(groups, group_size, -1),
        ),
    )
    observed = jnp.concatenate([agent_rows, summary.reshape(slot_count, row_width)], axis=1)
    targets = target_slot.reshape(slot_count)
    live_slots = targets >= 0
    send_index = jnp.where(
        live_slots, targets // batch_rows * capacity + targets % capacity, batch_rows
    )
    packed = (
        jnp.zeros((batch_rows, 2 * row_width), jnp.bfloat16)
        .at[send_index]
        .set(observed, mode="drop")
    )
    outgoing = packed.reshape(owners, capacity, 2 * row_width)
    arrived = lax.all_to_all(outgoing, "gx", split_axis=0, concat_axis=0, tiled=True)
    owner_rows = policy(arrived.reshape(-1, 2 * row_width), policy_in, policy_mid, policy_out)
    owner_acts = owner_rows.reshape(arrived.shape[0], arrived.shape[1], -1)
    returned = lax.all_to_all(owner_acts, "gx", split_axis=0, concat_axis=0, tiled=True)
    gathered = jnp.take(
        returned.reshape(batch_rows, -1), jnp.where(live_slots, send_index, 0), axis=0
    )
    actions = jnp.where(live_slots[:, None], gathered, jnp.zeros_like(gathered))
    return (
        actions.reshape(blocks_x, blocks_y, block_len, -1),
        arrived.reshape(1, 1, batch_rows, 2 * row_width),
    )


def solution(mesh):
    return jax.shard_map(
        on_device,
        mesh=mesh,
        in_specs=(
            P("gx", "gy", None, None),
            P(),
            P("gx", "gy", None),
            P("gx", "gy", None),
            P(),
            P(),
            P(),
            P(),
            P(),
        ),
        out_specs=(P("gx", "gy", None, None), P("gx", "gy", None, None)),
        check_vma=False,
    )
```

profile of v0, /device:TPU:2, one launch (start us, length us, event | category | flops | bytes accessed | tf_op | source)
XLA Modules:
  0.0 116.2 jit_solution(66133145350414761)
XLA Ops:
  0.6 0.0 copy-start
  0.6 0.0 copy-start.1
  0.7 0.0 copy-start.4
  0.7 4.4 %collective-permute-start = (bf16[2,4,128,256]{3,2,1,0:T(8,128)(2,1)}, bf16[2,4,128,256]{3,2,1,0:T(8,128)(2,1)}, u32[]{:S(2)}, u32[]{:S(2)}) collective-permute-start(bf16[2,4,128,256]{3,2,1,0:T(8,128)(2,1)} %param.11), channel_id=1, source_target_pairs={{0,16},{1,17},{2,18},{3,19},{4,20},{5,21},{6,22},{7,23},{8,24},{9,... | collective-permute-start | bytes 1572872 | tf_op jit(solution)/shard_map/ppermute | solution.py:20
  5.0 1.3 %collective-permute-start.1 = (bf16[2,4,128,256]{3,2,1,0:T(8,128)(2,1)}, bf16[2,4,128,256]{3,2,1,0:T(8,128)(2,1)S(1)}, u32[]{:S(2)}, u32[]{:S(2)}) collective-permute-start(bf16[2,4,128,256]{3,2,1,0:T(8,128)(2,1)} %param.11), channel_id=1, source_target_pairs={{16,0},{17,1},{18,2},{19,3},{20,4},{21,5},{22,6},{23,7},{24,8},{25... | collective-permute-start | bytes 1572872 | tf_op jit(solution)/shard_map/ppermute | solution.py:23
  6.4 0.8 pad_dynamic-slice_fusion
  7.2 0.1 reshape.458
  7.2 0.8 copy.33
  8.1 0.1 copy.25
  8.1 0.1 reshape.488
  8.2 0.8 gather_fusion
  9.0 0.1 reshape.487
  9.1 0.1 copy.26
  9.2 0.1 copy.28
  9.3 0.1 reshape.515
  9.4 0.0 copy-done.4
  9.4 0.1 copy.27
  9.5 0.0 copy-done.1
  9.5 0.2 copy.32
  9.8 5.9 %collective-permute-done = bf16[2,4,128,256]{3,2,1,0:T(8,128)(2,1)} collective-permute-done((bf16[2,4,128,256]{3,2,1,0:T(8,128)(2,1)}, bf16[2,4,128,256]{3,2,1,0:T(8,128)(2,1)}, u32[]{:S(2)}, u32[]{:S(2)}) %collective-permute-start) | collective-permute-done | bytes 524320 | tf_op jit(solution)/shard_map/ppermute | solution.py:20
  15.7 1.1 constant_dynamic-update-slice_fusion.2
  16.8 0.0 copy-start.2
  16.8 3.6 %collective-permute-done.1 = bf16[2,4,128,256]{3,2,1,0:T(8,128)(2,1)S(1)} collective-permute-done((bf16[2,4,128,256]{3,2,1,0:T(8,128)(2,1)}, bf16[2,4,128,256]{3,2,1,0:T(8,128)(2,1)S(1)}, u32[]{:S(2)}, u32[]{:S(2)}) %collective-permute-start.1) | collective-permute-done | bytes 524320 | tf_op jit(solution)/shard_map/ppermute | solution.py:23
  20.5 0.1 fusion.95
  20.7 1.9 %collective-permute-start.2 = (bf16[6,2,128,256]{3,2,1,0:T(8,128)(2,1)S(1)}, bf16[6,2,128,256]{3,2,1,0:T(8,128)(2,1)S(1)}, u32[]{:S(2)}, u32[]{:S(2)}) collective-permute-start(bf16[6,2,128,256]{3,2,1,0:T(8,128)(2,1)S(1)} %get-tuple-element.39), channel_id=1, source_target_pairs={{0,1},{1,2},{2,3},{3,4},{4,5},{5,6},{6,7},{7,8},{8,9},{9,10},{10,1... | collective-permute-start | bytes 2359304 | tf_op jit(solution)/shard_map/ppermute | solution.py:20
  22.6 3.6 %collective-permute-start.3 = (bf16[6,2,128,256]{3,2,1,0:T(8,128)(2,1)S(1)}, bf16[6,2,128,256]{3,2,1,0:T(8,128)(2,1)S(1)}, u32[]{:S(2)}, u32[]{:S(2)}) collective-permute-start(bf16[6,2,128,256]{3,2,1,0:T(8,128)(2,1)S(1)} %get-tuple-element.40), channel_id=1, source_target_pairs={{1,0},{2,1},{3,2},{4,3},{5,4},{6,5},{7,6},{8,7},{9,8},{10,9},{11,1... | collective-permute-start | bytes 2359304 | tf_op jit(solution)/shard_map/ppermute | solution.py:23
  26.3 0.1 bitcast_compare_fusion
  26.4 0.0 copy-done.2
  26.4 0.3 convolution_convert_fusion.2
  26.7 15.7 %collective-permute-done.2 = bf16[6,2,128,256]{3,2,1,0:T(8,128)(2,1)S(1)} collective-permute-done((bf16[6,2,128,256]{3,2,1,0:T(8,128)(2,1)S(1)}, bf16[6,2,128,256]{3,2,1,0:T(8,128)(2,1)S(1)}, u32[]{:S(2)}, u32[]{:S(2)}) %collective-permute-start.2) | collective-permute-done | bytes 786464 | tf_op jit(solution)/shard_map/ppermute | solution.py:20
  42.4 0.0 collective-permute-done.3
  42.4 0.4 pad_maximum_fusion
  42.8 2.7 %convolution_convert_fusion = bf16[6144,256]{1,0:T(8,128)(2,1)} fusion(bf16[6144,256]{1,0:T(8,128)(2,1)S(1)} %bitcast.63, bf16[256,768]{1,0:T(8,128)(2,1)S(1)} %copy-done.2), kind=kOutput, calls=%fused_computation.5 | convolution fusion | flops 806879232 | bytes 6422528 | tf_op jit(solution)/shard_map/dot_general | solution.py:116
  45.5 2.6 %convolution_convert_fusion.1 = bf16[6144,256]{1,0:T(8,128)(2,1)} fusion(bf16[6144,256]{1,0:T(8,128)(2,1)S(1)} %bitcast.64, bf16[256,768]{1,0:T(8,128)(2,1)S(1)} %copy-done.2), kind=kOutput, calls=%fused_computation.6 | convolution fusion | flops 806879232 | bytes 6422528 | tf_op jit(solution)/shard_map/dot_general | solution.py:113
  48.1 4.3 %gather_fusion.3 = bf16[40,128,256]{2,1,0:T(8,128)(2,1)} fusion(bf16[48,128,256]{2,1,0:T(8,128)(2,1)} %bitcast.71, s32[1024]{0:T(1024)S(1)} %pad_clamp_fusion), kind=kCustom, calls=%fused_computation.1.clone | custom fusion | bytes 5243040 | tf_op jit(solution)/shard_map/while/body/eval_jaxpr/jit(_take)/gather | solution.py:135
  52.4 4.3 %gather_fusion.2 = bf16[40,128,256]{2,1,0:T(8,128)(2,1)} fusion(bf16[48,128,256]{2,1,0:T(8,128)(2,1)} %bitcast.70, s32[1024]{0:T(1024)S(1)} %pad_clamp_fusion), kind=kCustom, calls=%fused_computation.clone | custom fusion | bytes 5243040 | tf_op jit(solution)/shard_map/while/body/eval_jaxpr/jit(_take)/gather | solution.py:134
  56.7 3.1 %broadcast_select_fusion.1 = (bf16[8,5,128,256]{3,2,1,0:T(8,128)(2,1)S(1)}, bf16[8,5,128,256]{3,2,1,0:T(8,128)(2,1)S(1)}) fusion(bf16[8,5,128,256]{3,2,1,0:T(8,128)(2,1)} %bitcast.75, pred[8,5]{1,0:T(8,128)(4,1)S(1)} %copy.27, bf16[8,5,128,256]{3,2,1,0:T(8,128)(2,1)} %bitcast.74), kind=kLoop, calls=%fused_computation.20 | loop fusion | flops 2621440 | bytes 10485800 | tf_op jit(solution)/shard_map/while/body/eval_jaxpr/jit(_take)/select_n | solution.py:134
  59.8 0.9 fusion.36
  60.7 0.9 fusion.38
  61.6 0.9 fusion.40
  62.5 3.0 %fusion.6 = (f32[8,128]{1,0:T(8,128)S(1)}, f32[8,128]{1,0:T(8,128)S(1)}, f32[8,128]{1,0:T(8,128)S(1)}, f32[8,128]{1,0:T(8,128)S(1)}, f32[8,128,640]{2,1,0:T(8,128)S(1)}) fusion(pred[8,640]{1,0:T(8,128)(4,1)S(1)} %bitcast_compare_fusion, f32[8,128,640]{2,1,0:T(8,128)S(1)} %fusion.40, f32[8,128,640]{2,1,0:T(8,128)S(1)} %fusion.38, ...), kind=kOutput, calls=%fused_computation.27 | convolution fusion | flops 346288128 | bytes 13653248 | tf_op jit(solution)/shard_map/while/body/eval_jaxpr/cqf,ckf->cqk/dot_general | solution.py:48
  65.5 1.0 convolution_select_fusion.2
  66.5 1.0 convolution_select_fusion.1
  67.6 1.1 convolution_select_fusion
  68.6 0.0 copy-start.3
  68.6 1.1 fusion.34
  69.7 0.0 copy-done.3
  69.8 0.5 multiply_reduce_fusion
  70.3 0.1 multiply_convert_fusion.12
  70.4 0.1 pad_maximum_fusion.1
  70.5 1.3 %copy.31 = bf16[1024,512]{1,0:T(8,128)(2,1)} copy(bf16[1024,512]{0,1:T(8,128)(2,1)S(1)} %pad_maximum_fusion.1) | data formatting | bytes 2097152 | tf_op jit(solution)/shard_map/concatenate | solution.py:146
  71.8 5.7 %scatter_custom_fusion = bf16[768,512]{1,0:T(8,128)(2,1)S(1)} fusion(s32[1024]{0:T(1024)S(1)} %bitcast.95, bf16[1024,512]{1,0:T(8,128)(2,1)} %copy.31, bf16[]{:T(256)} %constant.184.clone.1), kind=kCustom, calls=%fused_computation.73 | custom fusion | bytes 786944 | tf_op jit(solution)/shard_map/scatter | solution.py:155
  77.6 10.4 %all_to_all.10 = bf16[2,384,512]{2,1,0:T(8,128)(2,1)S(1)} all-to-all(bf16[2,384,512]{2,1,0:T(8,128)(2,1)S(1)} %bitcast.82), channel_id=1, replica_groups=mesh['gx'=2,'gy'=16] {'gx'}, dimensions={0} | all-to-all | bytes 1572864 | tf_op jit(solution)/shard_map/all_to_all | solution.py:158
  88.0 0.0 copy-done
  88.0 2.6 %fusion.96 = f32[768,1024]{1,0:T(8,128)} fusion(bf16[768,512]{1,0:T(8,128)(2,1)S(1)} %bitcast.72, bf16[512,1024]{1,0:T(8,128)(2,1)S(1)} %copy-done), kind=kOutput, calls=%fused_computation.173 | convolution fusion | flops 805306368 | bytes 4980736 | tf_op jit(solution)/shard_map/dot_general | solution.py:71
  90.6 0.0 copy-start.5
  90.6 8.6 %fusion = f32[768,1024]{1,0:T(8,128)} fusion(bf16[2,1024,1024]{2,1,0:T(8,128)(2,1)} %param.18, f32[768,1024]{1,0:T(8,128)} %fusion.96), kind=kOutput, calls=%fused_computation.21 | convolution fusion | flops 3229089792 | bytes 10485760 | tf_op jit(solution)/shard_map/dot_general | solution.py:76
  99.2 0.0 copy-done.5
  99.2 3.5 %fusion.35 = bf16[768,128]{1,0:T(8,128)(2,1)} fusion(bf16[1024,128]{1,0:T(8,128)(2,1)S(1)} %copy-done.5, f32[768,1024]{1,0:T(8,128)} %fusion), kind=kOutput, calls=%fused_computation.57 | convolution fusion | flops 205357056 | bytes 3604480 | tf_op jit(solution)/shard_map/dot_general | solution.py:78
  102.8 3.4 %all-to-all-start.1 = ((bf16[2,384,128]{2,1,0:T(8,128)(2,1)}), bf16[2,384,128]{2,1,0:T(8,128)(2,1)S(1)}, u32[]{:S(2)}, u32[]{:S(2)}) async-start(bf16[2,384,128]{2,1,0:T(8,128)(2,1)} %bitcast.26), calls=%async_computation.1 | async-start | bytes 393216 | tf_op jit(solution)/shard_map/all_to_all | solution.py:161
  106.2 4.8 %all-to-all-done.1 = bf16[2,384,128]{2,1,0:T(8,128)(2,1)S(1)} async-done(((bf16[2,384,128]{2,1,0:T(8,128)(2,1)}), bf16[2,384,128]{2,1,0:T(8,128)(2,1)S(1)}, u32[]{:S(2)}, u32[]{:S(2)}) %all-to-all-start.1) | async-done | bytes 196640 | tf_op jit(solution)/shard_map/all_to_all | solution.py:161
  111.0 3.2 %gather_fusion.1 = bf16[1024,128]{1,0:T(8,128)(2,1)S(1)} fusion(bf16[768,128]{1,0:T(8,128)(2,1)S(1)} %bitcast.69, s32[1024]{0:T(1024)S(1)} %broadcast_clamp_fusion), kind=kCustom, calls=%fused_computation.3 | custom fusion | bytes 528384 | tf_op jit(solution)/shard_map/jit(_take)/gather | solution.py:162
  114.2 1.0 select_select_fusion
  115.3 0.9 copy.37
  (23 shorter events, 0.3 us)
Async XLA Ops:
  0.6 87.4 %copy-start = (bf16[512,1024]{1,0:T(8,128)(2,1)S(1)}, bf16[512,1024]{1,0:T(8,128)(2,1)}, u32[]{:S(2)}) copy-start(bf16[512,1024]{1,0:T(8,128)(2,1)} %param.17) | copy-start | bytes 3145732
  0.6 8.9 %copy-start.1 = (bf16[2,4,128,256]{3,2,1,0:T(8,128)(2,1)S(1)}, bf16[2,4,128,256]{3,2,1,0:T(8,128)(2,1)}, u32[]{:S(2)}) copy-start(bf16[2,4,128,256]{3,2,1,0:T(8,128)(2,1)} %param.11) | copy-start | bytes 1572868
  0.7 8.7 %copy-start.4 = (s32[2,4,128]{2,1,0:T(4,128)S(1)}, s32[2,4,128]{2,1,0:T(4,128)}, u32[]{:S(2)}) copy-start(s32[2,4,128]{2,1,0:T(4,128)} %param.14) | copy-start | bytes 12292
  0.7 15.0 %collective-permute-start = (bf16[2,4,128,256]{3,2,1,0:T(8,128)(2,1)}, bf16[2,4,128,256]{3,2,1,0:T(8,128)(2,1)}, u32[]{:S(2)}, u32[]{:S(2)}) collective-permute-start(bf16[2,4,128,256]{3,2,1,0:T(8,128)(2,1)} %param.11), channel_id=1, source_target_pairs={{0,16},{1,17},{2,18},{3,19},{4,20},{5,21},{6,22},{7,23},{8,24},{9,... | collective-permute-start | bytes 1572872 | tf_op jit(solution)/shard_map/ppermute | solution.py:20
  5.0 15.5 %collective-permute-start.1 = (bf16[2,4,128,256]{3,2,1,0:T(8,128)(2,1)}, bf16[2,4,128,256]{3,2,1,0:T(8,128)(2,1)S(1)}, u32[]{:S(2)}, u32[]{:S(2)}) collective-permute-start(bf16[2,4,128,256]{3,2,1,0:T(8,128)(2,1)} %param.11), channel_id=1, source_target_pairs={{16,0},{17,1},{18,2},{19,3},{20,4},{21,5},{22,6},{23,7},{24,8},{25... | collective-permute-start | bytes 1572872 | tf_op jit(solution)/shard_map/ppermute | solution.py:23
  16.8 9.6 %copy-start.2 = (bf16[256,768]{1,0:T(8,128)(2,1)S(1)}, bf16[256,768]{1,0:T(8,128)(2,1)}, u32[]{:S(2)}) copy-start(bf16[256,768]{1,0:T(8,128)(2,1)} %param.15) | copy-start | bytes 1179652
  20.7 21.7 %collective-permute-start.2 = (bf16[6,2,128,256]{3,2,1,0:T(8,128)(2,1)S(1)}, bf16[6,2,128,256]{3,2,1,0:T(8,128)(2,1)S(1)}, u32[]{:S(2)}, u32[]{:S(2)}) collective-permute-start(bf16[6,2,128,256]{3,2,1,0:T(8,128)(2,1)S(1)} %get-tuple-element.39), channel_id=1, source_target_pairs={{0,1},{1,2},{2,3},{3,4},{4,5},{5,6},{6,7},{7,8},{8,9},{9,10},{10,1... | collective-permute-start | bytes 2359304 | tf_op jit(solution)/shard_map/ppermute | solution.py:20
  22.6 19.8 %collective-permute-start.3 = (bf16[6,2,128,256]{3,2,1,0:T(8,128)(2,1)S(1)}, bf16[6,2,128,256]{3,2,1,0:T(8,128)(2,1)S(1)}, u32[]{:S(2)}, u32[]{:S(2)}) collective-permute-start(bf16[6,2,128,256]{3,2,1,0:T(8,128)(2,1)S(1)} %get-tuple-element.40), channel_id=1, source_target_pairs={{1,0},{2,1},{3,2},{4,3},{5,4},{6,5},{7,6},{8,7},{9,8},{10,9},{11,1... | collective-permute-start | bytes 2359304 | tf_op jit(solution)/shard_map/ppermute | solution.py:23
  68.6 1.1 copy-start.3
  90.6 8.6 %copy-start.5 = (bf16[1024,128]{1,0:T(8,128)(2,1)S(1)}, bf16[1024,128]{1,0:T(8,128)(2,1)}, u32[]{:S(2)}) copy-start(bf16[1024,128]{1,0:T(8,128)(2,1)} %param.19) | copy-start | bytes 786436
  102.8 8.2 %all-to-all-start.1 = ((bf16[2,384,128]{2,1,0:T(8,128)(2,1)}), bf16[2,384,128]{2,1,0:T(8,128)(2,1)S(1)}, u32[]{:S(2)}, u32[]{:S(2)}) async-start(bf16[2,384,128]{2,1,0:T(8,128)(2,1)} %bitcast.26), calls=%async_computation.1 | async-start | bytes 393216 | tf_op jit(solution)/shard_map/all_to_all | solution.py:161
where the time goes:
time: 117 us; the launch traced here: 116 us
  matrix products  30.8 us (26%)
  waiting for transfers between devices  30.1 us (26%)
  local copies, waits for them, and re-layouts  24.3 us (21%)
  starting transfers between devices  14.6 us (12%)
  blocking collectives  10.4 us (9%)
  other arithmetic  4.93 us (4%)
    ppermute x2, waiting for transfers between devices, extended(): lax.ppermute(lax.slice_in_dim(block, block.shape[dim] - width, None, axis...  21.6 us
    all_to_all x1, blocking collectives, on_device(): lax.all_to_all(outgoing, 'gx', split_axis=0, concat_axis=0, tiled=True)  10.4 us
    dot_general x1, matrix products, policy(): jnp.dot(hidden, policy_mid[level_index], preferred_element_type=jnp.float32)  8.63 us
    ppermute x2, starting transfers between devices, extended(): lax.ppermute(lax.slice_in_dim(block, block.shape[dim] - width, None, axis...  6.27 us
    dot_general x4, matrix products, attend(): jnp.einsum('cqf,ckf->cqk', masked_queries, key_flat, preferred_element_ty...  5.74 us
    scatter x1, local copies, waits for them, and re-layouts, on_device(): packed = jnp.zeros((batch_rows, 2 * row_width), jnp.bfloat16).at[send_ind...  5.73 us
    ppermute x2, starting transfers between devices, extended(): lax.ppermute(lax.slice_in_dim(block, 0, width, axis=dim), axis, backward)  4.92 us
    all_to_all x1, waiting for transfers between devices, on_device(): lax.all_to_all(owner_acts, 'gx', split_axis=0, concat_axis=0, tiled=True)  4.8 us
  transfers between devices with their start and end apart: 5, of which 4 were waited for; matrix products, arithmetic and copies ran while one was open for 4% of the time, Pallas kernels for 0%

commit v1 on v0

v1 whole, which is shorter than its diff:
```python
import functools
import math

import jax
import jax.numpy as jnp
from jax import lax
from jax.experimental import pallas as pl
from jax.experimental.pallas import tpu as pltpu
from jax.sharding import PartitionSpec as P

HEADS = 4
LIVE = 96
REACH = 2
SCORE_CAP = 30.0
NORM_EPS = 1e-06
MIB = 1 << 20
BF16 = jnp.bfloat16
F32 = jnp.float32


def nt_dot(a, b):
    return lax.dot_general(a, b, (((1,), (1,)), ((), ())), preferred_element_type=F32)


def key_tables(fill_ref, near_ref, lx, ly, blocks_x, blocks_y, row_x, row_y):
    rows_x, rows_y = fill_ref.shape
    columns = blocks_y + 2 * REACH
    home_x = row_x * blocks_x + lx
    home_y = row_y * blocks_y + ly
    where_to = [lx * columns + ly + REACH]
    counts = [fill_ref[home_x, home_y]]
    for d in range(near_ref.shape[2]):
        direction = near_ref[lx, ly, d]
        cell = direction + jnp.where(direction >= 12, 1, 0)
        cell_x = (cell * 13) >> 6
        step_x = cell_x - REACH
        step_y = cell - cell_x * 5 - REACH
        at_x = home_x + step_x
        at_y = home_y + step_y
        inside = (at_x >= 0) & (at_x < rows_x) & (at_y >= 0) & (at_y < rows_y)
        safe_x = jnp.clip(at_x, 0, rows_x - 1)
        safe_y = jnp.clip(at_y, 0, rows_y - 1)
        counts.append(jnp.where(inside, fill_ref[safe_x, safe_y], 0))
        tile_x = jnp.where(safe_x >= blocks_x, 1, 0)
        other = jnp.where(tile_x == row_x, 0, 1)
        in_x = safe_x - tile_x * blocks_x
        where_to.append((other * blocks_x + in_x) * columns + ly + step_y + REACH)
    return where_to, counts


def attention_kernel(
    fill_ref,
    near_ref,
    place_ref,
    target_ref,
    own_ref,
    other_ref,
    low_ref,
    high_ref,
    other_low_ref,
    other_high_ref,
    weight_in_ref,
    weight_out_ref,
    summary_ref,
    packed_ref,
    keys_ref,
    values_ref,
    padded_ref,
):
    blocks_x, blocks_y = own_ref.shape[:2]
    width = own_ref.shape[-1]
    head = width // HEADS
    columns = blocks_y + 2 * REACH
    row_x = place_ref[0]
    row_y = place_ref[1]
    capacity = packed_ref.shape[0]
    weight_kv = weight_in_ref[:, width:]
    weight_q = weight_in_ref[:, :width]
    sources = ((low_ref, own_ref, high_ref), (other_low_ref, other_ref, other_high_ref))
    for o in range(2):
        for x in range(blocks_x):
            first = (o * blocks_x + x) * columns
            for part in sources[o]:
                count = part.shape[1]
                rows = part[x].reshape(count * LIVE, width)
                both = jnp.dot(rows, weight_kv, preferred_element_type=F32).astype(BF16)
                both = both.reshape(count, LIVE, 2 * width)
                keys_ref[first : first + count] = both[:, :, :width]
                values_ref[first : first + count] = both[:, :, width:]
                first += count

    key_blocks = near_ref.shape[2] + 1
    lane = lax.broadcasted_iota(jnp.int32, (1, key_blocks * LIVE), 1)
    head_of = lax.broadcasted_iota(jnp.int32, (1, width), 1) // head
    padded_ref[...] = jnp.zeros_like(padded_ref)
    for lx in range(blocks_x):
        for ly in range(blocks_y):
            b = lx * blocks_y + ly
            where_to, counts = key_tables(
                fill_ref, near_ref, lx, ly, blocks_x, blocks_y, row_x, row_y
            )
            query = jnp.dot(own_ref[lx, ly], weight_q, preferred_element_type=F32).astype(BF16)
            split = jnp.concatenate(
                [jnp.where(head_of == h, query, jnp.zeros_like(query)) for h in range(HEADS)],
                axis=0,
            )
            keys = jnp.concatenate([keys_ref[i] for i in where_to], axis=0)
            values = jnp.concatenate([values_ref[i] for i in where_to], axis=0)
            end = jnp.full(lane.shape, counts[0], jnp.int32)
            for j in range(1, key_blocks):
                end = jnp.where(lane >= j * LIVE, counts[j] + j * LIVE, end)
            raw = nt_dot(split, keys)
            capped = jnp.tanh(raw * (1.0 / (math.sqrt(head) * SCORE_CAP)))
            weight = jnp.exp(capped * SCORE_CAP)
            weight = jnp.where(lane < end, weight, 0.0)
            total = jnp.sum(weight, axis=-1, keepdims=True)
            mixed = jnp.dot(weight.astype(BF16), values, preferred_element_type=F32)
            mixed = mixed * (1.0 / total)
            context = mixed[:LIVE]
            for h in range(1, HEADS):
                context = jnp.where(head_of == h, mixed[h * LIVE : (h + 1) * LIVE], context)
            out = jnp.dot(
                context.astype(BF16), weight_out_ref[...], preferred_element_type=F32
            )
            scale = lax.rsqrt(jnp.mean(out * out, axis=-1, keepdims=True) + NORM_EPS)
            out = (out * scale).astype(BF16)
            summary_ref[lx, ly] = out
            padded_ref[b, :LIVE] = out

    block_len = padded_ref.shape[1]
    base = ((1 - row_x) * 2 + row_x) * capacity
    row = lax.broadcasted_iota(jnp.int32, (capacity, block_len), 0) + base
    pick = jnp.concatenate(
        [
            jnp.where(row == target_ref[lx, ly : ly + 1, :], 1.0, 0.0).astype(BF16)
            for lx in range(blocks_x)
            for ly in range(blocks_y)
        ],
        axis=1,
    )
    flat = padded_ref[...].reshape(blocks_x * blocks_y * block_len, width)
    packed_ref[...] = jnp.dot(pick, flat, preferred_element_type=F32).astype(BF16)


def silu(v):
    half = 0.5 * v
    return half + half * jnp.tanh(half)


def policy_kernel(
    fill_ref,
    place_ref,
    target_ref,
    other_target_ref,
    own_ref,
    other_ref,
    summary_ref,
    policy_in_ref,
    policy_mid_ref,
    policy_out_ref,
    actions_ref,
    batch_ref,
    x_ref,
    h_ref,
    g_ref,
    own_pad_ref,
    other_pad_ref,
):
    blocks_x, blocks_y = own_ref.shape[:2]
    width = own_ref.shape[-1]
    slots = blocks_x * blocks_y * LIVE
    block_len = actions_ref.shape[2]
    row_x = place_ref[0]
    row_y = place_ref[1]
    capacity = batch_ref.shape[0] // 2
    own = own_ref[...].reshape(slots, width)
    x_ref[:, :width] = own
    x_ref[:, width:] = summary_ref[...].reshape(slots, width)
    chunk = 256
    hidden = policy_in_ref.shape[1]
    for n in range(0, hidden, chunk):
        v = jnp.dot(x_ref[...], policy_in_ref[:, n : n + chunk], preferred_element_type=F32)
        h_ref[:, n : n + chunk] = silu(v).astype(BF16)
    now, later = h_ref, g_ref
    for m in range(policy_mid_ref.shape[0]):
        for n in range(0, hidden, chunk):
            v = jnp.dot(
                now[...], policy_mid_ref[m, :, n : n + chunk], preferred_element_type=F32
            )
            later[:, n : n + chunk] = silu(v).astype(BF16)
        now, later = later, now
    acts = jnp.dot(now[...], policy_out_ref[...], preferred_element_type=F32)
    slot = lax.broadcasted_iota(jnp.int32, (LIVE, 1), 0)
    for lx in range(blocks_x):
        for ly in range(blocks_y):
            b = lx * blocks_y + ly
            fill = fill_ref[row_x * blocks_x + lx, row_y * blocks_y + ly]
            act = jnp.where(slot < fill, acts[b * LIVE : (b + 1) * LIVE], 0.0)
            actions_ref[lx, ly, :LIVE] = act.astype(BF16)
            actions_ref[lx, ly, LIVE:] = jnp.zeros(
                (block_len - LIVE, act.shape[1]), BF16
            )

    own_pad_ref[...] = jnp.zeros_like(own_pad_ref)
    other_pad_ref[...] = jnp.zeros_like(other_pad_ref)
    for lx in range(blocks_x):
        for ly in range(blocks_y):
            b = lx * blocks_y + ly
            own_pad_ref[b, :LIVE] = x_ref[b * LIVE : (b + 1) * LIVE]
            other_pad_ref[b, :LIVE] = other_ref[lx, ly]
    count = blocks_x * blocks_y * block_len

    def picked(which_ref, source, rows):
        base = (row_x * 2 + source) * capacity
        row = lax.broadcasted_iota(jnp.int32, (capacity, block_len), 0) + base
        pick = jnp.concatenate(
            [
                jnp.where(row == which_ref[lx, ly : ly + 1, :], 1.0, 0.0).astype(BF16)
                for lx in range(blocks_x)
                for ly in range(blocks_y)
            ],
            axis=1,
        )
        return jnp.dot(pick, rows, preferred_element_type=F32).astype(BF16)

    mine = pl.ds(pl.multiple_of(row_x * capacity, capacity), capacity)
    theirs = pl.ds(pl.multiple_of((1 - row_x) * capacity, capacity), capacity)
    batch_ref[mine, :] = picked(target_ref, row_x, own_pad_ref[...].reshape(count, 2 * width))
    batch_ref[theirs, :width] = picked(
        other_target_ref, 1 - row_x, other_pad_ref[...].reshape(count, width)
    )
    batch_ref[theirs, width:] = jnp.zeros((capacity, width), BF16)


VMEM = pl.BlockSpec(memory_space=pltpu.VMEM)
SMEM = pl.BlockSpec(memory_space=pltpu.SMEM)


def on_device(
    agents,
    block_fill,
    neighbours,
    target_slot,
    attention_in,
    attention_out,
    policy_in,
    policy_mid,
    policy_out,
):
    blocks_x, blocks_y, block_len, width = agents.shape
    all_blocks = blocks_x * blocks_y
    owners = lax.axis_size("gx")
    count_y = lax.axis_size("gy")
    row_x = lax.axis_index("gx")
    capacity = 3 * all_blocks * block_len // (4 * owners)
    hidden = policy_in.shape[1]
    acts = policy_out.shape[1]
    place = jnp.stack([row_x, lax.axis_index("gy")]).astype(jnp.int32)

    swap = [(0, 1), (1, 0)]
    up = [(i, i + 1) for i in range(count_y - 1)]
    down = [(b, a) for a, b in up]
    own = agents[:, :, :LIVE]
    other = lax.ppermute(own, "gx", swap)
    low = lax.ppermute(own[:, blocks_y - REACH :], "gy", up)
    high = lax.ppermute(own[:, :REACH], "gy", down)
    other_low = lax.ppermute(other[:, blocks_y - REACH :], "gy", up)
    other_high = lax.ppermute(other[:, :REACH], "gy", down)
    other_target = lax.ppermute(target_slot, "gx", swap)

    window = blocks_x * owners * (blocks_y + 2 * REACH)
    summary, packed = pl.pallas_call(
        attention_kernel,
        out_shape=(
            jax.ShapeDtypeStruct((blocks_x, blocks_y, LIVE, width), BF16),
            jax.ShapeDtypeStruct((capacity, width), BF16),
        ),
        in_specs=[SMEM, SMEM, SMEM] + [VMEM] * 9,
        out_specs=(VMEM, VMEM),
        scratch_shapes=[
            pltpu.VMEM((window, LIVE, width), BF16),
            pltpu.VMEM((window, LIVE, width), BF16),
            pltpu.VMEM((all_blocks, block_len, width), BF16),
        ],
        compiler_params=pltpu.CompilerParams(vmem_limit_bytes=32 * MIB),
        name="attention",
    )(
        block_fill,
        neighbours,
        place,
        target_slot,
        own,
        other,
        low,
        high,
        other_low,
        other_high,
        attention_in,
        attention_out,
    )
    arrived = lax.ppermute(packed, "gx", swap)
    slots = all_blocks * LIVE
    rows = owners * capacity
    actions, batch = pl.pallas_call(
        policy_kernel,
        out_shape=(
            jax.ShapeDtypeStruct((blocks_x, blocks_y, block_len, acts), BF16),
            jax.ShapeDtypeStruct((rows, 2 * width), BF16),
        ),
        in_specs=[SMEM, SMEM] + [VMEM] * 8,
        out_specs=(VMEM, VMEM),
        scratch_shapes=[
            pltpu.VMEM((slots, 2 * width), BF16),
            pltpu.VMEM((slots, hidden), BF16),
            pltpu.VMEM((slots, hidden), BF16),
            pltpu.VMEM((all_blocks, block_len, 2 * width), BF16),
            pltpu.VMEM((all_blocks, block_len, width), BF16),
        ],
        compiler_params=pltpu.CompilerParams(vmem_limit_bytes=40 * MIB),
        cost_estimate=pl.CostEstimate(
            flops=2 * slots * hidden * (2 * width + 2 * hidden + acts),
            bytes_accessed=12 * MIB,
            transcendentals=3 * slots * hidden,
        ),
        name="policy",
    )(
        block_fill,
        place,
        target_slot,
        other_target,
        own,
        other,
        summary,
        policy_in,
        policy_mid,
        policy_out,
    )
    batch = lax.dynamic_update_slice(batch, arrived, ((1 - row_x) * capacity, width))
    return actions, batch.reshape(1, 1, rows, 2 * width)


def solution(mesh):
    return jax.shard_map(
        on_device,
        mesh=mesh,
        in_specs=(
            P("gx", "gy", None, None),
            P(),
            P("gx", "gy", None),
            P("gx", "gy", None),
            P(),
            P(),
            P(),
            P(),
            P(),
        ),
        out_specs=(P("gx", "gy", None, None), P("gx", "gy", None, None)),
        check_vma=False,
    )
```

time: 117 us -> 46.5 us (0.40)
  matrix products: 30.8 us -> 0 us
  waiting for transfers between devices: 30.1 us -> 7.35 us
  local copies, waits for them, and re-layouts: 24.3 us -> 9.73 us
  Pallas kernels: 0 us -> 14.4 us
  blocking collectives: 10.4 us -> 0 us
  other arithmetic: 4.93 us -> 0.07 us
  starting transfers between devices: 14.6 us -> 13.4 us
    dot_general x15 -> x0, matrix products: 30.8 us -> none  [the longest x1 8.63 us: policy(): jnp.dot(hidden, policy_mid[level_index], preferred_element_type=jnp.float32)]
    ppermute x4 -> x7, waiting for transfers between devices: 25.3 us -> 7.35 us  [the longest x1 3.94 us: on_device(): other = lax.ppermute(own, 'gx', swap)]
    pallas_call x0 -> x2, Pallas kernels: none -> 14.4 us  [the longest x1 7.51 us: on_device(): pl.pallas_call(attention_kernel, out_shape=(jax.ShapeDtypeStruct((blocks_...]
    gather x6 -> x0, local copies, waits for them, and re-layouts: 12.7 us -> none  [the longest x1 4.32 us: attend_group(): group_values = jnp.take(near_value, group_index, axis=0)]
    all_to_all x1 -> x0, blocking collectives: 10.4 us -> none  [on_device(): lax.all_to_all(outgoing, 'gx', split_axis=0, concat_axis=0, tiled=True)]
    scatter x1 -> x0, local copies, waits for them, and re-layouts: 5.73 us -> none  [on_device(): packed = jnp.zeros((batch_rows, 2 * row_width), jnp.bfloat16).at[send_ind...]
    all_to_all x1 -> x0, waiting for transfers between devices: 4.8 us -> none  [on_device(): lax.all_to_all(owner_acts, 'gx', split_axis=0, concat_axis=0, tiled=True)]
    select_n x6 -> x0, other arithmetic: 4.17 us -> none  [the longest x1 3.06 us: attend_group(): group_keys = jnp.take(near_key, group_index, axis=0)]
  transfers between devices with their start and end apart: 5 -> 7, of which waited for: 4 -> 2; matrix products, arithmetic and copies ran while one was open for 4% -> 4% of each run, Pallas kernels for 0% -> 31%
where the time goes in v1:
time: 46.5 us; the launch traced here: 45.7 us
  Pallas kernels  14.4 us (31%)
  starting transfers between devices  13.4 us (29%)
  local copies, waits for them, and re-layouts  9.73 us (21%)
  waiting for transfers between devices  7.35 us (16%)
  between operations  0.75 us (2%)
    pallas_call x1, Pallas kernels, on_device(): pl.pallas_call(attention_kernel, out_shape=(jax.ShapeDtypeStruct((blocks_...  7.51 us
    pallas_call x1, Pallas kernels, on_device(): pl.pallas_call(policy_kernel, out_shape=(jax.ShapeDtypeStruct((blocks_x,...  6.84 us
    unnamed x20, local copies, waits for them, and re-layouts  6.16 us
    ppermute x1, waiting for transfers between devices, on_device(): other = lax.ppermute(own, 'gx', swap)  3.94 us
    ppermute x1, waiting for transfers between devices, on_device(): other_low = lax.ppermute(other[:, blocks_y - REACH:], 'gy', up)  3.4 us
    ppermute x1, starting transfers between devices, on_device(): low = lax.ppermute(own[:, blocks_y - REACH:], 'gy', up)  2.41 us
    ppermute x1, starting transfers between devices, on_device(): other_low = lax.ppermute(other[:, blocks_y - REACH:], 'gy', up)  2.41 us
    ppermute x1, starting transfers between devices, on_device(): high = lax.ppermute(own[:, :REACH], 'gy', down)  1.92 us
  transfers between devices with their start and end apart: 7, of which 2 were waited for; matrix products, arithmetic and copies ran while one was open for 4% of the time, Pallas kernels for 31%

profile of v1, /device:TPU:2, one launch (start us, length us, event | category | flops | bytes accessed | tf_op | source)
XLA Modules:
  0.0 45.7 jit_solution(14605393074416202832)
XLA Ops:
  0.6 0.0 copy-start.4
  0.6 0.0 copy-start.6
  0.7 0.0 copy-start.9
  0.7 0.0 copy-start.8
  0.7 1.1 %slice.17.own_ref = bf16[2,4,96,256]{3,2,1,0:T(8,128)(2,1)S(1)} slice(bf16[2,4,128,256]{3,2,1,0:T(8,128)(2,1)} %param.9), slice={[0:2], [0:4], [0:96], [0:256]} | slice | bytes 786432 | tf_op jit(solution)/shard_map/slice | solution.py:263
  1.8 1.6 %collective-permute-start.1 = (bf16[2,4,96,256]{3,2,1,0:T(8,128)(2,1)S(1)}, bf16[2,4,96,256]{3,2,1,0:T(8,128)(2,1)S(1)}, u32[]{:S(2)}, u32[]{:S(2)}) collective-permute-start(bf16[2,4,96,256]{3,2,1,0:T(8,128)(2,1)S(1)} %slice.17.own_ref), channel_id=1, source_target_pairs={{0,16},{16,0},{1,17},{17,1},{2,18},{18,2},{3,19},{19,3},{4,20},{20... | collective-permute-start | bytes 1179656 | tf_op jit(solution)/shard_map/ppermute | solution.py:264
  3.4 1.0 %fusion = (bf16[2,2,96,256]{3,2,1,0:T(8,128)(2,1)S(1)}, bf16[2,2,96,256]{3,2,1,0:T(8,128)(2,1)S(1)}) fusion(bf16[2,4,128,256]{3,2,1,0:T(8,128)(2,1)} %param.9), kind=kLoop, calls=%fused_computation.2 | loop fusion | bytes 786432 | tf_op jit(solution)/shard_map/slice | solution.py:266
  4.4 1.9 %collective-permute-start.3 = (bf16[2,2,96,256]{3,2,1,0:T(8,128)(2,1)S(1)}, bf16[2,2,96,256]{3,2,1,0:T(8,128)(2,1)S(1)}, u32[]{:S(2)}, u32[]{:S(2)}) collective-permute-start(bf16[2,2,96,256]{3,2,1,0:T(8,128)(2,1)S(1)} %get-tuple-element.10), channel_id=1, source_target_pairs={{1,0},{2,1},{3,2},{4,3},{5,4},{6,5},{7,6},{8,7},{9,8},{10,9},{11,1... | collective-permute-start | bytes 589832 | tf_op jit(solution)/shard_map/ppermute | solution.py:266
  6.4 2.4 %collective-permute-start.2 = (bf16[2,2,96,256]{3,2,1,0:T(8,128)(2,1)S(1)}, bf16[2,2,96,256]{3,2,1,0:T(8,128)(2,1)S(1)}, u32[]{:S(2)}, u32[]{:S(2)}) collective-permute-start(bf16[2,2,96,256]{3,2,1,0:T(8,128)(2,1)S(1)} %get-tuple-element.11), channel_id=1, source_target_pairs={{0,1},{1,2},{2,3},{3,4},{4,5},{5,6},{6,7},{7,8},{8,9},{9,10},{10,1... | collective-permute-start | bytes 589832 | tf_op jit(solution)/shard_map/ppermute | solution.py:265
  8.8 3.9 %collective-permute-done.1.other_ref = bf16[2,4,96,256]{3,2,1,0:T(8,128)(2,1)S(1)} collective-permute-done((bf16[2,4,96,256]{3,2,1,0:T(8,128)(2,1)S(1)}, bf16[2,4,96,256]{3,2,1,0:T(8,128)(2,1)S(1)}, u32[]{:S(2)}, u32[]{:S(2)}) %collective-permute-start.1) | collective-permute-done | bytes 393248 | tf_op jit(solution)/shard_map/ppermute | solution.py:264
  12.7 0.7 %fusion.1 = (bf16[2,2,96,256]{3,2,1,0:T(8,128)(2,1)}, bf16[2,2,96,256]{3,2,1,0:T(8,128)(2,1)S(1)}) fusion(bf16[2,4,96,256]{3,2,1,0:T(8,128)(2,1)S(1)} %collective-permute-done.1.other_ref), kind=kLoop, calls=%fused_computation.3 | loop fusion | bytes 786432 | tf_op jit(solution)/shard_map/slice | solution.py:268
  13.4 1.9 %collective-permute-start.5 = (bf16[2,2,96,256]{3,2,1,0:T(8,128)(2,1)}, bf16[2,2,96,256]{3,2,1,0:T(8,128)(2,1)S(1)}, u32[]{:S(2)}, u32[]{:S(2)}) collective-permute-start(bf16[2,2,96,256]{3,2,1,0:T(8,128)(2,1)} %get-tuple-element.12), channel_id=1, source_target_pairs={{1,0},{2,1},{3,2},{4,3},{5,4},{6,5},{7,6},{8,7},{9,8},{10,9},{11,1... | collective-permute-start | bytes 589832 | tf_op jit(solution)/shard_map/ppermute | solution.py:268
  15.3 2.4 %collective-permute-start.4 = (bf16[2,2,96,256]{3,2,1,0:T(8,128)(2,1)S(1)}, bf16[2,2,96,256]{3,2,1,0:T(8,128)(2,1)S(1)}, u32[]{:S(2)}, u32[]{:S(2)}) collective-permute-start(bf16[2,2,96,256]{3,2,1,0:T(8,128)(2,1)S(1)} %get-tuple-element.13), channel_id=1, source_target_pairs={{0,1},{1,2},{2,3},{3,4},{4,5},{5,6},{6,7},{7,8},{8,9},{9,10},{10,1... | collective-permute-start | bytes 589832 | tf_op jit(solution)/shard_map/ppermute | solution.py:267
  17.8 1.6 %collective-permute-start = (s32[2,4,128]{2,1,0:T(4,128)}, s32[2,4,128]{2,1,0:T(4,128)S(1)}, u32[]{:S(2)}, u32[]{:S(2)}) collective-permute-start(s32[2,4,128]{2,1,0:T(4,128)} %target_ref.3), channel_id=1, source_target_pairs={{0,16},{16,0},{1,17},{17,1},{2,18},{18,2},{3,19},{19,3},{4,20},{20... | collective-permute-start | bytes 12296 | tf_op jit(solution)/shard_map/ppermute | solution.py:269
  19.3 0.1 pad_add_fusion.place_ref
  19.4 0.0 collective-permute-done.3.high_ref
  19.4 0.0 collective-permute-done.2.low_ref
  19.4 0.0 collective-permute-done.5.other_high_ref
  19.4 3.4 %collective-permute-done.4.other_low_ref = bf16[2,2,96,256]{3,2,1,0:T(8,128)(2,1)S(1)} collective-permute-done((bf16[2,2,96,256]{3,2,1,0:T(8,128)(2,1)S(1)}, bf16[2,2,96,256]{3,2,1,0:T(8,128)(2,1)S(1)}, u32[]{:S(2)}, u32[]{:S(2)}) %collective-permute-start.4) | collective-permute-done | bytes 196640 | tf_op jit(solution)/shard_map/ppermute | solution.py:267
  22.8 0.0 copy-start
  22.8 1.0 %copy-done = bf16[256,768]{1,0:T(8,128)(2,1)S(1)} copy-done((bf16[256,768]{1,0:T(8,128)(2,1)S(1)}, bf16[256,768]{1,0:T(8,128)(2,1)}, u32[]{:S(2)}) %copy-start) | copy-done | bytes 393240
  23.8 0.0 copy-start.1
  23.8 0.9 %copy-done.1 = bf16[256,256]{1,0:T(8,128)(2,1)S(1)} copy-done((bf16[256,256]{1,0:T(8,128)(2,1)S(1)}, bf16[256,256]{1,0:T(8,128)(2,1)}, u32[]{:S(2)}) %copy-start.1) | copy-done | bytes 131096
  24.7 0.0 copy-start.2
  24.7 0.7 %copy-done.2 = s32[2,4,4]{2,1,0:T(4,128)S(1)} copy-done((s32[2,4,4]{2,1,0:T(4,128)S(1)}, s32[2,4,4]{2,1,0:T(4,128)}, u32[]{:S(2)}) %copy-start.2) | copy-done | bytes 152
  25.4 0.0 copy-start.3
  25.4 0.7 %copy-done.3 = s32[2,4,128]{2,1,0:T(4,128)S(1)} copy-done((s32[2,4,128]{2,1,0:T(4,128)S(1)}, s32[2,4,128]{2,1,0:T(4,128)}, u32[]{:S(2)}) %copy-start.3) | copy-done | bytes 4120
  26.1 0.0 copy-start.5
  26.1 0.7 %copy-done.5 = s32[4,64]{1,0:T(4,128)S(1)} copy-done((s32[4,64]{1,0:T(4,128)S(1)}, s32[4,64]{1,0:T(4,128)}, u32[]{:S(2)}) %copy-start.5) | copy-done | bytes 1048
  26.8 7.5 %attention.1 = (bf16[2,4,96,256]{3,2,1,0:T(8,128)(2,1)S(1)}, bf16[384,256]{1,0:T(8,128)(2,1)S(1)}) custom-call(s32[4,64]{1,0:T(4,128)S(1)} %copy-done.5, s32[2,4,4]{2,1,0:T(4,128)S(1)} %copy-done.2, s32[2]{0:T(128)S(1)} %pad_add_fusion.place_ref, s32[2,4,128]{2,1,0:T(4,128)S(1)} %copy-done.3, bf16[2,4,96,256]{3,2,1,0:T(8,128)(2,1)S(1)} %slice.17.own_ref, ...), custom_call_target="tpu_custom_call" | custom-call | tf_op jit(solution)/shard_map/attention/pallas_call | solution.py:272
  34.3 1.6 %collective-permute-start.6 = (bf16[384,256]{1,0:T(8,128)(2,1)S(1)}, bf16[384,256]{1,0:T(8,128)(2,1)S(1)}, u32[]{:S(2)}, u32[]{:S(2)}) collective-permute-start(bf16[384,256]{1,0:T(8,128)(2,1)S(1)} %get-tuple-element.9), channel_id=1, source_target_pairs={{0,16},{16,0},{1,17},{17,1},{2,18},{18,2},{3,19},{19,3},{4,20},{20... | collective-permute-start | bytes 589832 | tf_op jit(solution)/shard_map/ppermute | solution.py:301
  35.9 0.0 collective-permute-done.other_target_ref
  35.9 0.0 copy-done.4
  35.9 0.0 copy-done.6
  35.9 0.0 copy-done.9
  35.9 0.0 copy-done.8
  35.9 0.0 copy-start.7
  35.9 2.2 %copy-done.7 = bf16[2,1024,1024]{2,1,0:T(8,128)(2,1)S(1)} copy-done((bf16[2,1024,1024]{2,1,0:T(8,128)(2,1)S(1)}, bf16[2,1024,1024]{2,1,0:T(8,128)(2,1)}, u32[]{:S(2)}) %copy-start.7) | copy-done | bytes 4194328
  38.1 6.8 %policy.1 = (bf16[2,4,128,128]{3,2,1,0:T(8,128)(2,1)}, bf16[768,512]{1,0:T(8,128)(2,1)}) custom-call(s32[4,64]{1,0:T(4,128)S(1)} %copy-done.6, s32[2]{0:T(128)S(1)} %pad_add_fusion.place_ref, s32[2,4,128]{2,1,0:T(4,128)S(1)} %copy-done.4, s32[2,4,128]{2,1,0:T(4,128)S(1)} %collective-permute-done.other_target_ref, bf16[2,4,96,256]{3,2,1,0:T(8,128)(2,1)S(1)} %slice.17.own_ref, ...), custom_call_target="tpu_custom_call" | custom-call | flops 4227858432 | bytes 12582912 | tf_op jit(solution)/shard_map/policy/pallas_call | solution.py:304
  45.0 0.0 collective-permute-done.6
  45.0 0.7 %bitcast_dynamic-update-slice_fusion = bf16[1,1,768,512]{3,2,1,0:T(8,128)(2,1)} fusion(bf16[1,1,768,512]{3,2,1,0:T(8,128)(2,1)} %bitcast.5, s32[]{:T(128)S(6)} %select_n.3, bf16[384,256]{1,0:T(8,128)(2,1)S(1)} %collective-permute-done.6), kind=kLoop, calls=%fused_computation | loop fusion | bytes 393220 | tf_op jit(solution)/shard_map/dynamic_update_slice | solution.py:338
Async XLA Ops:
  0.6 35.3 %copy-start.4 = (s32[2,4,128]{2,1,0:T(4,128)S(1)}, s32[2,4,128]{2,1,0:T(4,128)}, u32[]{:S(2)}) copy-start(s32[2,4,128]{2,1,0:T(4,128)} %target_ref.3) | copy-start | bytes 12292
  0.6 35.3 %copy-start.6 = (s32[4,64]{1,0:T(4,128)S(1)}, s32[4,64]{1,0:T(4,128)}, u32[]{:S(2)}) copy-start(s32[4,64]{1,0:T(4,128)} %fill_ref.3) | copy-start | bytes 3076
  0.7 35.3 %copy-start.9 = (bf16[1024,128]{1,0:T(8,128)(2,1)S(1)}, bf16[1024,128]{1,0:T(8,128)(2,1)}, u32[]{:S(2)}) copy-start(bf16[1024,128]{1,0:T(8,128)(2,1)} %policy_out_ref.1) | copy-start | bytes 786436
  0.7 35.3 %copy-start.8 = (bf16[512,1024]{1,0:T(8,128)(2,1)S(1)}, bf16[512,1024]{1,0:T(8,128)(2,1)}, u32[]{:S(2)}) copy-start(bf16[512,1024]{1,0:T(8,128)(2,1)} %policy_in_ref.1) | copy-start | bytes 3145732
  1.8 10.9 %collective-permute-start.1 = (bf16[2,4,96,256]{3,2,1,0:T(8,128)(2,1)S(1)}, bf16[2,4,96,256]{3,2,1,0:T(8,128)(2,1)S(1)}, u32[]{:S(2)}, u32[]{:S(2)}) collective-permute-start(bf16[2,4,96,256]{3,2,1,0:T(8,128)(2,1)S(1)} %slice.17.own_ref), channel_id=1, source_target_pairs={{0,16},{16,0},{1,17},{17,1},{2,18},{18,2},{3,19},{19,3},{4,20},{20... | collective-permute-start | bytes 1179656 | tf_op jit(solution)/shard_map/ppermute | solution.py:264
  4.4 15.0 %collective-permute-start.3 = (bf16[2,2,96,256]{3,2,1,0:T(8,128)(2,1)S(1)}, bf16[2,2,96,256]{3,2,1,0:T(8,128)(2,1)S(1)}, u32[]{:S(2)}, u32[]{:S(2)}) collective-permute-start(bf16[2,2,96,256]{3,2,1,0:T(8,128)(2,1)S(1)} %get-tuple-element.10), channel_id=1, source_target_pairs={{1,0},{2,1},{3,2},{4,3},{5,4},{6,5},{7,6},{8,7},{9,8},{10,9},{11,1... | collective-permute-start | bytes 589832 | tf_op jit(solution)/shard_map/ppermute | solution.py:266
  6.4 13.1 %collective-permute-start.2 = (bf16[2,2,96,256]{3,2,1,0:T(8,128)(2,1)S(1)}, bf16[2,2,96,256]{3,2,1,0:T(8,128)(2,1)S(1)}, u32[]{:S(2)}, u32[]{:S(2)}) collective-permute-start(bf16[2,2,96,256]{3,2,1,0:T(8,128)(2,1)S(1)} %get-tuple-element.11), channel_id=1, source_target_pairs={{0,1},{1,2},{2,3},{3,4},{4,5},{5,6},{6,7},{7,8},{8,9},{9,10},{10,1... | collective-permute-start | bytes 589832 | tf_op jit(solution)/shard_map/ppermute | solution.py:265
  13.4 6.0 %collective-permute-start.5 = (bf16[2,2,96,256]{3,2,1,0:T(8,128)(2,1)}, bf16[2,2,96,256]{3,2,1,0:T(8,128)(2,1)S(1)}, u32[]{:S(2)}, u32[]{:S(2)}) collective-permute-start(bf16[2,2,96,256]{3,2,1,0:T(8,128)(2,1)} %get-tuple-element.12), channel_id=1, source_target_pairs={{1,0},{2,1},{3,2},{4,3},{5,4},{6,5},{7,6},{8,7},{9,8},{10,9},{11,1... | collective-permute-start | bytes 589832 | tf_op jit(solution)/shard_map/ppermute | solution.py:268
  15.3 7.5 %collective-permute-start.4 = (bf16[2,2,96,256]{3,2,1,0:T(8,128)(2,1)S(1)}, bf16[2,2,96,256]{3,2,1,0:T(8,128)(2,1)S(1)}, u32[]{:S(2)}, u32[]{:S(2)}) collective-permute-start(bf16[2,2,96,256]{3,2,1,0:T(8,128)(2,1)S(1)} %get-tuple-element.13), channel_id=1, source_target_pairs={{0,1},{1,2},{2,3},{3,4},{4,5},{5,6},{6,7},{7,8},{8,9},{9,10},{10,1... | collective-permute-start | bytes 589832 | tf_op jit(solution)/shard_map/ppermute | solution.py:267
  17.8 18.1 %collective-permute-start = (s32[2,4,128]{2,1,0:T(4,128)}, s32[2,4,128]{2,1,0:T(4,128)S(1)}, u32[]{:S(2)}, u32[]{:S(2)}) collective-permute-start(s32[2,4,128]{2,1,0:T(4,128)} %target_ref.3), channel_id=1, source_target_pairs={{0,16},{16,0},{1,17},{17,1},{2,18},{18,2},{3,19},{19,3},{4,20},{20... | collective-permute-start | bytes 12296 | tf_op jit(solution)/shard_map/ppermute | solution.py:269
  22.8 1.0 %copy-start = (bf16[256,768]{1,0:T(8,128)(2,1)S(1)}, bf16[256,768]{1,0:T(8,128)(2,1)}, u32[]{:S(2)}) copy-start(bf16[256,768]{1,0:T(8,128)(2,1)} %weight_in_ref.1) | copy-start | bytes 1179652
  23.8 0.9 %copy-start.1 = (bf16[256,256]{1,0:T(8,128)(2,1)S(1)}, bf16[256,256]{1,0:T(8,128)(2,1)}, u32[]{:S(2)}) copy-start(bf16[256,256]{1,0:T(8,128)(2,1)} %weight_out_ref.1) | copy-start | bytes 393220
  24.7 0.7 %copy-start.2 = (s32[2,4,4]{2,1,0:T(4,128)S(1)}, s32[2,4,4]{2,1,0:T(4,128)}, u32[]{:S(2)}) copy-start(s32[2,4,4]{2,1,0:T(4,128)} %near_ref.1) | copy-start | bytes 388
  25.4 0.7 %copy-start.3 = (s32[2,4,128]{2,1,0:T(4,128)S(1)}, s32[2,4,128]{2,1,0:T(4,128)}, u32[]{:S(2)}) copy-start(s32[2,4,128]{2,1,0:T(4,128)} %target_ref.3) | copy-start | bytes 12292
  26.1 0.7 %copy-start.5 = (s32[4,64]{1,0:T(4,128)S(1)}, s32[4,64]{1,0:T(4,128)}, u32[]{:S(2)}) copy-start(s32[4,64]{1,0:T(4,128)} %fill_ref.3) | copy-start | bytes 3076
  34.3 10.7 %collective-permute-start.6 = (bf16[384,256]{1,0:T(8,128)(2,1)S(1)}, bf16[384,256]{1,0:T(8,128)(2,1)S(1)}, u32[]{:S(2)}, u32[]{:S(2)}) collective-permute-start(bf16[384,256]{1,0:T(8,128)(2,1)S(1)} %get-tuple-element.9), channel_id=1, source_target_pairs={{0,16},{16,0},{1,17},{17,1},{2,18},{18,2},{3,19},{19,3},{4,20},{20... | collective-permute-start | bytes 589832 | tf_op jit(solution)/shard_map/ppermute | solution.py:301
  35.9 2.2 %copy-start.7 = (bf16[2,1024,1024]{2,1,0:T(8,128)(2,1)S(1)}, bf16[2,1024,1024]{2,1,0:T(8,128)(2,1)}, u32[]{:S(2)}) copy-start(bf16[2,1024,1024]{2,1,0:T(8,128)(2,1)} %policy_mid_ref.1) | copy-start | bytes 12582916

commit v2 on v1

v2 whole, which is shorter than its diff:
```python
import math

import jax
import jax.numpy as jnp
from jax import lax
from jax.experimental import pallas as pl
from jax.experimental.pallas import tpu as pltpu
from jax.sharding import PartitionSpec as P

HEADS = 4
LIVE = 96
REACH = 2
SCORE_CAP = 30.0
NORM_EPS = 1e-06
LOG2_E = math.log2(math.e)
TARGET_ROWS = 8
MIB = 1 << 20
BF16 = jnp.bfloat16
F32 = jnp.float32


def nt_dot(a, b):
    return lax.dot_general(a, b, (((1,), (1,)), ((), ())), preferred_element_type=F32)


def key_tables(fill_ref, near_ref, lx, ly, columns, first, place):
    row_x, row_y, blocks_x, blocks_y = place
    rows_x, rows_y = fill_ref.shape
    home_x = row_x * blocks_x + lx
    home_y = row_y * blocks_y + ly
    where_to = [lx * columns + ly - first + REACH]
    counts = [fill_ref[home_x, home_y]]
    for d in range(near_ref.shape[2]):
        direction = near_ref[lx, ly, d]
        cell = direction + jnp.where(direction >= 12, 1, 0)
        cell_x = (cell * 13) >> 6
        step_x = cell_x - REACH
        step_y = cell - cell_x * 5 - REACH
        at_x = home_x + step_x
        at_y = home_y + step_y
        inside = (at_x >= 0) & (at_x < rows_x) & (at_y >= 0) & (at_y < rows_y)
        safe_x = jnp.clip(at_x, 0, rows_x - 1)
        safe_y = jnp.clip(at_y, 0, rows_y - 1)
        counts.append(jnp.where(inside, fill_ref[safe_x, safe_y], 0))
        tile_x = jnp.where(safe_x >= blocks_x, 1, 0)
        other = jnp.where(tile_x == row_x, 0, 1)
        in_x = safe_x - tile_x * blocks_x
        where_to.append((other * blocks_x + in_x) * columns + ly - first + step_y + REACH)
    return where_to, counts


def one_hot(base, capacity, block_len, target_rows):
    row = lax.broadcasted_iota(jnp.int32, (capacity, block_len), 0) + base
    row = row.astype(F32)
    return jnp.concatenate(
        [jnp.where(row == target, 1.0, 0.0).astype(BF16) for target in target_rows], axis=1
    )


def place(pick, pad_ref):
    blocks, block_len, width = pad_ref.shape
    flat = pad_ref[...].reshape(blocks * block_len, width)
    return jnp.dot(pick, flat, preferred_element_type=F32)


def sent_targets(ref, first, count):
    start = ref.shape[0] - TARGET_ROWS
    half = ref.shape[1] // 2
    both = ref[start : start + TARGET_ROWS].astype(F32)
    rows = both[:, :half] * 256.0 + both[:, half:]
    return [rows[b : b + 1] for b in range(first, first + count)]


def spread(pad_ref, first, rows, blocks):
    _, block_len, width = pad_ref.shape
    for b in range(blocks):
        pad_ref[first + b, :LIVE] = rows[b * LIVE : (b + 1) * LIVE]
        pad_ref[first + b, LIVE:] = jnp.zeros((block_len - LIVE, width), pad_ref.dtype)


def stage_kernel(place_ref, target_hbm, agents_hbm, off_ref, inn_ref, target_ref, sems):
    blocks_x, _, _, _ = agents_hbm.shape
    core = place_ref[1] & 1
    rows = REACH * LIVE
    targets = pltpu.make_async_copy(target_hbm, target_ref, sems.at[2, 0])
    targets.start()
    copies = []
    for x in range(blocks_x):
        for ref, column, s in ((off_ref, core * REACH, 0), (inn_ref, REACH - core * REACH, 1)):
            for c in range(REACH):
                copies.append(
                    pltpu.make_async_copy(
                        agents_hbm.at[x, column + c, pl.ds(0, LIVE)],
                        ref.at[pl.ds(x * rows + c * LIVE, LIVE)],
                        sems.at[s, x * REACH + c],
                    )
                )
    for copy in copies:
        copy.start()
    targets.wait()
    halves = []
    for column in (core * REACH, REACH - core * REACH):
        for x in range(blocks_x):
            for c in range(REACH):
                halves.append(target_ref[x, pl.ds(column + c, 1), :])
    target = jnp.concatenate(halves, axis=0)
    high = target >> 8
    low = target - high * 256
    split = jnp.concatenate([high, low], axis=1).astype(F32).astype(BF16)
    inn_ref[blocks_x * rows :] = split
    for copy in copies:
        copy.wait()


def local_kernel(
    place_ref,
    off_ref,
    inn_ref,
    weight_in_hbm,
    weight_out_hbm,
    weight_in_ref,
    weight_out_ref,
    own_rows_ref,
    pad_ref,
    sems,
):
    copies = [
        pltpu.make_async_copy(weight_in_hbm, weight_in_ref, sems.at[0]),
        pltpu.make_async_copy(weight_out_hbm, weight_out_ref, sems.at[1]),
    ]
    for copy in copies:
        copy.start()
    capacity = own_rows_ref.shape[0]
    blocks, block_len, _ = pad_ref.shape
    row_x = place_ref[0]
    spread(pad_ref, 0, off_ref, blocks // 2)
    spread(pad_ref, blocks // 2, inn_ref, blocks // 2)
    pick = one_hot(
        (row_x * 2 + row_x) * capacity, capacity, block_len, sent_targets(inn_ref, 0, blocks)
    )
    own_rows_ref[...] = place(pick, pad_ref).astype(BF16)
    for copy in copies:
        copy.wait()


def attend(home_ref, first, sources, fill_ref, near_ref, place_ref, weights, window):
    weight_in_ref, weight_out_ref = weights
    keys_ref, values_ref, context_ref = window
    width = weight_out_ref.shape[0]
    head = width // HEADS
    half_rows = context_ref.shape[0]
    blocks_x = half_rows // (REACH * LIVE)
    blocks_y = 2 * REACH
    columns = 3 * REACH
    row_x = place_ref[0]
    row_y = place_ref[1]
    for o, column, ref in sources:
        rows = ref[:half_rows]
        both = jnp.dot(rows, weight_in_ref[:, width:], preferred_element_type=F32).astype(BF16)
        both = both.reshape(blocks_x * REACH, LIVE, 2 * width)
        for x in range(blocks_x):
            at = (o * blocks_x + x) * columns + column
            keys_ref[pl.ds(at, REACH)] = both[x * REACH : (x + 1) * REACH, :, :width]
            values_ref[pl.ds(at, REACH)] = both[x * REACH : (x + 1) * REACH, :, width:]

    key_blocks = near_ref.shape[2] + 1
    lane = lax.broadcasted_iota(jnp.int32, (1, key_blocks * LIVE), 1)
    head_of = lax.broadcasted_iota(jnp.int32, (1, width), 1) // head
    queries = jnp.dot(
        home_ref[:half_rows], weight_in_ref[:, :width], preferred_element_type=F32
    ).astype(BF16)
    for i in range(blocks_x * REACH):
        lx = i // REACH
        ly = first + i % REACH
        where_to, counts = key_tables(
            fill_ref, near_ref, lx, ly, columns, first, (row_x, row_y, blocks_x, blocks_y)
        )
        query = queries[i * LIVE : (i + 1) * LIVE]
        split = jnp.concatenate(
            [jnp.where(head_of == h, query, jnp.zeros_like(query)) for h in range(HEADS)],
            axis=0,
        )
        keys = jnp.concatenate([keys_ref[w] for w in where_to], axis=0)
        values = jnp.concatenate([values_ref[w] for w in where_to], axis=0)
        end = jnp.full(lane.shape, counts[0], jnp.int32)
        for j in range(1, key_blocks):
            end = jnp.where(lane >= j * LIVE, counts[j] + j * LIVE, end)
        raw = nt_dot(split, keys)
        capped = jnp.tanh(raw * (1.0 / (math.sqrt(head) * SCORE_CAP)))
        weight = jnp.exp2(capped * (SCORE_CAP * LOG2_E))
        weight = jnp.where(lane < end, weight, 0.0)
        total = jnp.sum(weight, axis=-1, keepdims=True)
        weight = (weight * (1.0 / total)).astype(BF16)
        mixed = jnp.dot(weight, values, preferred_element_type=F32)
        context = mixed[:LIVE]
        for h in range(1, HEADS):
            context = jnp.where(head_of == h, mixed[h * LIVE : (h + 1) * LIVE], context)
        context_ref[i * LIVE : (i + 1) * LIVE] = context.astype(BF16)
    out = jnp.dot(context_ref[...], weight_out_ref[...], preferred_element_type=F32)
    scale = lax.rsqrt(jnp.mean(out * out, axis=-1, keepdims=True) + NORM_EPS)
    return (out * scale).astype(BF16)


def inner_kernel(
    fill_ref,
    near_ref,
    place_ref,
    off_ref,
    inn_ref,
    other_off_ref,
    other_inn_ref,
    side_ref,
    other_side_ref,
    weight_in_ref,
    weight_out_ref,
    policy_in_hbm,
    policy_mid_hbm,
    policy_out_hbm,
    summary_ref,
    packed_ref,
    own_ref,
    other_rows_ref,
    policy_in_ref,
    policy_mid_ref,
    policy_out_ref,
    keys_ref,
    values_ref,
    context_ref,
    pad_ref,
    sems,
):
    pairs = (
        (policy_in_hbm, policy_in_ref),
        (policy_mid_hbm, policy_mid_ref),
        (policy_out_hbm, policy_out_ref),
    )
    copies = [pltpu.make_async_copy(a, b, sems.at[i]) for i, (a, b) in enumerate(pairs)]
    for copy in copies:
        copy.start()
    row_x = place_ref[0]
    core = place_ref[1] & 1
    at_inn = REACH
    at_off = 2 * REACH * core
    at_side = 2 * REACH - 2 * REACH * core
    sources = (
        (0, at_off, off_ref),
        (0, at_inn, inn_ref),
        (1, at_off, other_off_ref),
        (1, at_inn, other_inn_ref),
        (0, at_side, side_ref),
        (1, at_side, other_side_ref),
    )
    out = attend(
        inn_ref,
        REACH - core * REACH,
        sources,
        fill_ref,
        near_ref,
        place_ref,
        (weight_in_ref, weight_out_ref),
        (keys_ref, values_ref, context_ref),
    )
    summary_ref[...] = out
    capacity = packed_ref.shape[0]
    blocks, block_len, _ = pad_ref.shape
    each = blocks // 2
    spread(pad_ref, 0, out, each)
    rows = sent_targets(inn_ref, each, each)
    for ref, owner in ((packed_ref, 1 - row_x), (own_ref, row_x)):
        pick = one_hot((owner * 2 + row_x) * capacity, capacity, block_len, rows)
        ref[...] = place(pick, pad_ref.at[:each]).astype(BF16)
    spread(pad_ref, 0, other_off_ref, each)
    spread(pad_ref, each, other_inn_ref, each)
    pick = one_hot(
        (row_x * 2 + 1 - row_x) * capacity,
        capacity,
        block_len,
        sent_targets(other_inn_ref, 0, blocks),
    )
    other_rows_ref[...] = place(pick, pad_ref).astype(BF16)
    for copy in copies:
        copy.wait()


def outer_kernel(
    fill_ref,
    near_ref,
    place_ref,
    off_ref,
    inn_ref,
    other_off_ref,
    other_inn_ref,
    side_ref,
    other_side_ref,
    weight_in_ref,
    weight_out_ref,
    inner_packed_ref,
    summary_ref,
    packed_ref,
    keys_ref,
    values_ref,
    context_ref,
    pad_ref,
):
    row_x = place_ref[0]
    core = place_ref[1] & 1
    at_off = REACH
    at_inn = 2 * REACH - 2 * REACH * core
    at_side = 2 * REACH * core
    sources = (
        (0, at_off, off_ref),
        (0, at_inn, inn_ref),
        (1, at_off, other_off_ref),
        (1, at_inn, other_inn_ref),
        (0, at_side, side_ref),
        (1, at_side, other_side_ref),
    )
    out = attend(
        off_ref,
        core * REACH,
        sources,
        fill_ref,
        near_ref,
        place_ref,
        (weight_in_ref, weight_out_ref),
        (keys_ref, values_ref, context_ref),
    )
    summary_ref[...] = out
    capacity = packed_ref.shape[0]
    each, block_len, _ = pad_ref.shape
    spread(pad_ref, 0, out, each)
    rows = sent_targets(inn_ref, 0, each)
    pick = one_hot(((1 - row_x) * 2 + row_x) * capacity, capacity, block_len, rows)
    packed_ref[...] = (place(pick, pad_ref) + inner_packed_ref[...].astype(F32)).astype(BF16)


def silu(v):
    half = 0.5 * v
    return half + half * jnp.tanh(half)


def policy_kernel(
    fill_ref,
    place_ref,
    off_ref,
    inn_ref,
    off_summary_ref,
    inn_summary_ref,
    own_rows_ref,
    own_inner_ref,
    other_rows_ref,
    policy_in_ref,
    policy_mid_ref,
    policy_out_ref,
    actions_ref,
    batch_ref,
    x_ref,
    h_ref,
    g_ref,
    pad_ref,
):
    width = off_ref.shape[1]
    blocks_x, blocks_y, block_len, _ = actions_ref.shape
    row_x = place_ref[0]
    row_y = place_ref[1]
    core = row_y & 1
    capacity = batch_ref.shape[0] // 2
    half_rows = off_ref.shape[0]
    x_ref[:half_rows, :width] = off_ref[...]
    x_ref[half_rows:, :width] = inn_ref[:half_rows]
    x_ref[:half_rows, width:] = off_summary_ref[...]
    x_ref[half_rows:, width:] = inn_summary_ref[...]
    chunk = 256
    hidden = policy_in_ref.shape[1]
    for n in range(0, hidden, chunk):
        v = jnp.dot(x_ref[...], policy_in_ref[:, n : n + chunk], preferred_element_type=F32)
        h_ref[:, n : n + chunk] = silu(v).astype(BF16)
    now, later = h_ref, g_ref
    for m in range(policy_mid_ref.shape[0]):
        for n in range(0, hidden, chunk):
            v = jnp.dot(
                now[...], policy_mid_ref[m, :, n : n + chunk], preferred_element_type=F32
            )
            later[:, n : n + chunk] = silu(v).astype(BF16)
        now, later = later, now
    acts = jnp.dot(now[...], policy_out_ref[...], preferred_element_type=F32)
    slot = lax.broadcasted_iota(jnp.int32, (LIVE, 1), 0)
    for half, first in enumerate((core * REACH, REACH - core * REACH)):
        for i in range(blocks_x * REACH):
            lx = i // REACH
            ly = first + i % REACH
            b = half * blocks_x * REACH + i
            fill = fill_ref[row_x * blocks_x + lx, row_y * blocks_y + ly]
            act = jnp.where(slot < fill, acts[b * LIVE : (b + 1) * LIVE], 0.0)
            actions_ref[lx, ly, :LIVE] = act.astype(BF16)
            actions_ref[lx, ly, LIVE:] = jnp.zeros((block_len - LIVE, act.shape[1]), BF16)

    mine = pl.ds(pl.multiple_of(row_x * capacity, capacity), capacity)
    theirs = pl.ds(pl.multiple_of((1 - row_x) * capacity, capacity), capacity)
    each = pad_ref.shape[0]
    spread(pad_ref, 0, off_summary_ref, each)
    rows = sent_targets(inn_ref, 0, each)
    pick = one_hot((row_x * 2 + row_x) * capacity, capacity, block_len, rows)
    batch_ref[mine, :width] = own_rows_ref[...]
    batch_ref[mine, width:] = (place(pick, pad_ref) + own_inner_ref[...].astype(F32)).astype(BF16)
    batch_ref[theirs, :width] = other_rows_ref[...]
    batch_ref[theirs, width:] = jnp.zeros((capacity, width), BF16)


VMEM = pl.BlockSpec(memory_space=pltpu.VMEM)
SMEM = pl.BlockSpec(memory_space=pltpu.SMEM)
HBM = pl.BlockSpec(memory_space=pltpu.HBM)
SDS = jax.ShapeDtypeStruct


def in_hbm(*arrays):
    return tuple(pltpu.with_memory_space_constraint(a, pltpu.HBM) for a in arrays)


def on_device(
    agents,
    block_fill,
    neighbours,
    target_slot,
    attention_in,
    attention_out,
    policy_in,
    policy_mid,
    policy_out,
):
    blocks_x, blocks_y, block_len, width = agents.shape
    all_blocks = blocks_x * blocks_y
    owners = lax.axis_size("gx")
    count_y = lax.axis_size("gy")
    row_x = lax.axis_index("gx")
    capacity = 3 * all_blocks * block_len // (4 * owners)
    hidden = policy_in.shape[1]
    acts = policy_out.shape[1]
    slots = all_blocks * LIVE
    half_rows = slots // 2
    rows = owners * capacity
    where = jnp.stack([row_x, lax.axis_index("gy")]).astype(jnp.int32)

    swap = [(0, 1), (1, 0)]
    across = [(i, i - 1) for i in range(2, count_y, 2)]
    across += [(i, i + 1) for i in range(1, count_y - 1, 2)]
    beside = [(i, i ^ 1) for i in range(count_y)]
    diagonal = [
        (g * count_y + a, (1 - g) * count_y + b) for g in range(owners) for a, b in across
    ]

    off, inn = pl.pallas_call(
        stage_kernel,
        out_shape=(SDS((half_rows, width), BF16), SDS((half_rows + TARGET_ROWS, width), BF16)),
        in_specs=[SMEM, HBM, HBM],
        out_specs=(VMEM, VMEM),
        scratch_shapes=[
            pltpu.VMEM((blocks_x, blocks_y, block_len), jnp.int32),
            pltpu.SemaphoreType.DMA((3, all_blocks // 2)),
        ],
        compiler_params=pltpu.CompilerParams(vmem_limit_bytes=4 * MIB),
        name="stage",
    )(where, *in_hbm(target_slot, agents))
    other_inn = lax.ppermute(inn, "gx", swap)
    other_off = lax.ppermute(off, "gx", swap)
    side_off = lax.ppermute(off, "gy", across)
    side_inn = lax.ppermute(inn, "gy", beside)
    attention_in, attention_out, own_rows = pl.pallas_call(
        local_kernel,
        out_shape=(
            SDS(attention_in.shape, BF16),
            SDS(attention_out.shape, BF16),
            SDS((capacity, width), BF16),
        ),
        in_specs=[SMEM, VMEM, VMEM, HBM, HBM],
        out_specs=(VMEM,) * 3,
        scratch_shapes=[
            pltpu.VMEM((all_blocks, block_len, width), BF16),
            pltpu.SemaphoreType.DMA((2,)),
        ],
        compiler_params=pltpu.CompilerParams(vmem_limit_bytes=8 * MIB),
        cost_estimate=pl.CostEstimate(
            flops=2 * capacity * all_blocks * block_len * width,
            bytes_accessed=8 * MIB,
            transcendentals=0,
        ),
        name="local",
    )(where, off, inn, *in_hbm(attention_in, attention_out))
    own_rows, other_inn, off_late = lax.optimization_barrier((own_rows, other_inn, off))
    other_side_off = lax.ppermute(off_late, ("gx", "gy"), diagonal)
    other_side_inn = lax.ppermute(other_inn, "gy", beside)

    window = blocks_x * owners * 3 * REACH
    scratch = [
        pltpu.VMEM((window, LIVE, width), BF16),
        pltpu.VMEM((window, LIVE, width), BF16),
        pltpu.VMEM((half_rows, width), BF16),
    ]
    scores = all_blocks // 2 * HEADS * LIVE * 5 * LIVE
    cost = pl.CostEstimate(
        flops=2 * (2 * scores + window * LIVE * 2 * width) * width,
        bytes_accessed=8 * MIB,
        transcendentals=2 * scores,
    )
    inn_summary, packed, own_inner, other_rows, policy_in, policy_mid, policy_out = pl.pallas_call(
        inner_kernel,
        out_shape=(
            SDS((half_rows, width), BF16),
            SDS((capacity, width), BF16),
            SDS((capacity, width), BF16),
            SDS((capacity, width), BF16),
            SDS(policy_in.shape, BF16),
            SDS(policy_mid.shape, BF16),
            SDS(policy_out.shape, BF16),
        ),
        in_specs=[SMEM] * 3 + [VMEM] * 8 + [HBM] * 3,
        out_specs=(VMEM,) * 7,
        scratch_shapes=scratch
        + [
            pltpu.VMEM((all_blocks, block_len, width), BF16),
            pltpu.SemaphoreType.DMA((3,)),
        ],
        compiler_params=pltpu.CompilerParams(vmem_limit_bytes=14 * MIB),
        cost_estimate=cost,
        name="inner",
    )(
        block_fill,
        neighbours,
        where,
        off,
        inn,
        other_off,
        other_inn,
        side_inn,
        other_side_inn,
        attention_in,
        attention_out,
        *in_hbm(policy_in, policy_mid, policy_out),
    )
    off_summary, packed = pl.pallas_call(
        outer_kernel,
        out_shape=(SDS((half_rows, width), BF16), SDS((capacity, width), BF16)),
        in_specs=[SMEM] * 3 + [VMEM] * 9,
        out_specs=(VMEM, VMEM),
        scratch_shapes=scratch + [pltpu.VMEM((all_blocks // 2, block_len, width), BF16)],
        compiler_params=pltpu.CompilerParams(vmem_limit_bytes=14 * MIB),
        cost_estimate=cost,
        name="outer",
    )(
        block_fill,
        neighbours,
        where,
        off,
        inn,
        other_off,
        other_inn,
        side_off,
        other_side_off,
        attention_in,
        attention_out,
        packed,
    )
    arrived = lax.ppermute(packed, "gx", swap)
    actions, batch = pl.pallas_call(
        policy_kernel,
        out_shape=(
            SDS((blocks_x, blocks_y, block_len, acts), BF16),
            SDS((rows, 2 * width), BF16),
        ),
        in_specs=[SMEM] * 2 + [VMEM] * 10,
        out_specs=(VMEM, VMEM),
        scratch_shapes=[
            pltpu.VMEM((slots, 2 * width), BF16),
            pltpu.VMEM((slots, hidden), BF16),
            pltpu.VMEM((slots, hidden), BF16),
            pltpu.VMEM((all_blocks // 2, block_len, width), BF16),
        ],
        compiler_params=pltpu.CompilerParams(vmem_limit_bytes=16 * MIB),
        cost_estimate=pl.CostEstimate(
            flops=2 * slots * hidden * (2 * width + 2 * hidden + acts),
            bytes_accessed=12 * MIB,
            transcendentals=3 * slots * hidden,
        ),
        name="policy",
    )(
        block_fill,
        where,
        off,
        inn,
        off_summary,
        inn_summary,
        own_rows,
        own_inner,
        other_rows,
        policy_in,
        policy_mid,
        policy_out,
    )
    batch = lax.dynamic_update_slice(batch, arrived, ((1 - row_x) * capacity, width))
    return actions, batch.reshape(1, 1, rows, 2 * width)


def solution(mesh):
    return jax.shard_map(
        on_device,
        mesh=mesh,
        in_specs=(
            P("gx", "gy", None, None),
            P(),
            P("gx", "gy", None),
            P("gx", "gy", None),
            P(),
            P(),
            P(),
            P(),
            P(),
        ),
        out_specs=(P("gx", "gy", None, None), P("gx", "gy", None, None)),
        check_vma=False,
    )
```

time: 46.5 us -> 37.6 us (0.81)
  the two profiles are of different devices: /device:TPU:2 before, /device:TPU:0 now
where the time goes in v2:
time: 37.6 us; the launch traced here: 37.3 us
  Pallas kernels  18.9 us (50%)
  starting transfers between devices  7.92 us (21%)
  waiting for transfers between devices  7.61 us (20%)
  local copies, waits for them, and re-layouts  2.06 us (5%)
  between operations  0.72 us (2%)
    pallas_call x1, Pallas kernels, on_device(): pl.pallas_call(policy_kernel, out_shape=(SDS((blocks_x, blocks_y, block_l...  6.36 us
    pallas_call x1, Pallas kernels, on_device(): pl.pallas_call(inner_kernel, out_shape=(SDS((half_rows, width), BF16), SD...  6.11 us
    ppermute x1, waiting for transfers between devices, on_device(): other_off = lax.ppermute(off, 'gx', swap)  4.22 us
    ppermute x1, waiting for transfers between devices, on_device(): other_inn = lax.ppermute(inn, 'gx', swap)  3.38 us
    pallas_call x1, Pallas kernels, on_device(): pl.pallas_call(outer_kernel, out_shape=(SDS((half_rows, width), BF16), SD...  3.26 us
    ppermute x1, starting transfers between devices, on_device(): other_inn = lax.ppermute(inn, 'gx', swap)  3.03 us
    ppermute x1, starting transfers between devices, on_device(): arrived = lax.ppermute(packed, 'gx', swap)  1.81 us
    ppermute x1, starting transfers between devices, on_device(): other_off = lax.ppermute(off, 'gx', swap)  1.74 us
  transfers between devices with their start and end apart: 7, of which 2 were waited for; matrix products, arithmetic and copies ran while one was open for 0% of the time, Pallas kernels for 38%

profile of v2, /device:TPU:0, one launch (start us, length us, event | category | flops | bytes accessed | tf_op | source)
XLA Modules:
  0.0 37.3 jit_solution(6244639238570277341)
XLA Ops:
  0.6 0.1 pad_add_fusion.place_ref
  0.7 1.6 %stage.1 = (bf16[384,256]{1,0:T(8,128)(2,1)S(1)}, bf16[392,256]{1,0:T(8,128)(2,1)S(1)}) custom-call(s32[2]{0:T(128)S(1)} %pad_add_fusion.place_ref, s32[2,4,128]{2,1,0:T(4,128)} %target_hbm.1, bf16[2,4,128,256]{3,2,1,0:T(8,128)(2,1)} %agents_hbm.1), custom_call_target="tpu_custom_call" | custom-call | tf_op jit(solution)/shard_map/stage/pallas_call | solution.py:452
  2.3 3.0 %collective-permute-start.1 = (bf16[392,256]{1,0:T(8,128)(2,1)S(1)}, bf16[392,256]{1,0:T(8,128)(2,1)S(1)}, u32[]{:S(2)}, u32[]{:S(2)}) collective-permute-start(bf16[392,256]{1,0:T(8,128)(2,1)S(1)} %get-tuple-element.22.inn_ref), channel_id=1, source_target_pairs={{0,16},{16,0},{1,17},{17,1},{2,18},{18,2},{3,19},{19,3},{4,20},{20... | collective-permute-start | bytes 602120 | tf_op jit(solution)/shard_map/ppermute | solution.py:464
  5.4 0.0 collective-permute-start.4
  5.4 1.6 %local.1 = (bf16[256,768]{1,0:T(8,128)(2,1)S(1)}, bf16[256,256]{1,0:T(8,128)(2,1)S(1)}, bf16[384,256]{1,0:T(8,128)(2,1)S(1)}) custom-call(s32[2]{0:T(128)S(1)} %pad_add_fusion.place_ref, bf16[384,256]{1,0:T(8,128)(2,1)S(1)} %get-tuple-element.25.off_ref, bf16[392,256]{1,0:T(8,128)(2,1)S(1)} %get-tuple-element.22.inn_ref, bf16[256,768]{1,0:T(8,128)(2,1)} %weight_in_hbm.1, ...), custom_call_target="tpu_custom_call" | custom-call | flops 201326592 | bytes 8388608 | tf_op jit(solution)/shard_map/local/pallas_call | solution.py:468
  7.0 3.4 %collective-permute-done.1.other_inn_ref = bf16[392,256]{1,0:T(8,128)(2,1)S(1)} collective-permute-done((bf16[392,256]{1,0:T(8,128)(2,1)S(1)}, bf16[392,256]{1,0:T(8,128)(2,1)S(1)}, u32[]{:S(2)}, u32[]{:S(2)}) %collective-permute-start.1) | collective-permute-done | bytes 200736 | tf_op jit(solution)/shard_map/ppermute | solution.py:464
  10.4 0.0 collective-permute-start.5
  10.4 1.7 %collective-permute-start = (bf16[384,256]{1,0:T(8,128)(2,1)S(1)}, bf16[384,256]{1,0:T(8,128)(2,1)S(1)}, u32[]{:S(2)}, u32[]{:S(2)}) collective-permute-start(bf16[384,256]{1,0:T(8,128)(2,1)S(1)} %get-tuple-element.25.off_ref), channel_id=1, source_target_pairs={{0,16},{16,0},{1,17},{17,1},{2,18},{18,2},{3,19},{19,3},{4,20},{20... | collective-permute-start | bytes 589832 | tf_op jit(solution)/shard_map/ppermute | solution.py:465
  12.1 0.7 %collective-permute-start.2 = (bf16[384,256]{1,0:T(8,128)(2,1)S(1)}, bf16[384,256]{1,0:T(8,128)(2,1)S(1)}, u32[]{:S(2)}, u32[]{:S(2)}) collective-permute-start(bf16[384,256]{1,0:T(8,128)(2,1)S(1)} %get-tuple-element.25.off_ref), channel_id=1, source_target_pairs={{2,1},{4,3},{6,5},{8,7},{10,9},{12,11},{14,13},{1,2},{3,4},{5,6},{... | collective-permute-start | bytes 589832 | tf_op jit(solution)/shard_map/ppermute | solution.py:466
  12.8 0.7 %collective-permute-start.3 = (bf16[384,256]{1,0:T(8,128)(2,1)S(1)}, bf16[384,256]{1,0:T(8,128)(2,1)S(1)}, u32[]{:S(2)}, u32[]{:S(2)}) collective-permute-start(bf16[384,256]{1,0:T(8,128)(2,1)S(1)} %get-tuple-element.25.off_ref), channel_id=1, source_target_pairs={{2,17},{4,19},{6,21},{8,23},{10,25},{12,27},{14,29},{1,18},{3,20},... | collective-permute-start | bytes 589832 | tf_op jit(solution)/shard_map/ppermute | solution.py:490
  13.5 4.2 %collective-permute-done.other_off_ref = bf16[384,256]{1,0:T(8,128)(2,1)S(1)} collective-permute-done((bf16[384,256]{1,0:T(8,128)(2,1)S(1)}, bf16[384,256]{1,0:T(8,128)(2,1)S(1)}, u32[]{:S(2)}, u32[]{:S(2)}) %collective-permute-start) | collective-permute-done | bytes 196640 | tf_op jit(solution)/shard_map/ppermute | solution.py:465
  17.7 0.0 collective-permute-done.4.side_ref
  17.7 0.0 collective-permute-done.5.other_side_ref
  17.7 0.0 copy-start
  17.7 0.7 %copy-done = s32[2,4,4]{2,1,0:T(4,128)S(1)} copy-done((s32[2,4,4]{2,1,0:T(4,128)S(1)}, s32[2,4,4]{2,1,0:T(4,128)}, u32[]{:S(2)}) %copy-start) | copy-done | bytes 152
  18.4 0.0 copy-start.1
  18.4 0.7 %copy-done.1 = s32[4,64]{1,0:T(4,128)S(1)} copy-done((s32[4,64]{1,0:T(4,128)S(1)}, s32[4,64]{1,0:T(4,128)}, u32[]{:S(2)}) %copy-start.1) | copy-done | bytes 1048
  19.1 6.1 %inner.1 = (bf16[384,256]{1,0:T(8,128)(2,1)S(1)}, bf16[384,256]{1,0:T(8,128)(2,1)S(1)}, bf16[384,256]{1,0:T(8,128)(2,1)S(1)}, bf16[384,256]{1,0:T(8,128)(2,1)S(1...) custom-call(s32[4,64]{1,0:T(4,128)S(1)} %copy-done.1, ...), custom_call_target="tpu_custom_call" | custom-call | flops 1358954496 | bytes 8388608 | tf_op jit(solution)/shard_map/inner/pallas_call | solution.py:505
  25.2 0.0 copy-start.2
  25.2 0.0 collective-permute-done.2.side_ref
  25.2 0.0 collective-permute-done.3.other_side_ref
  25.2 3.3 %outer.1 = (bf16[384,256]{1,0:T(8,128)(2,1)S(1)}, bf16[384,256]{1,0:T(8,128)(2,1)S(1)}) custom-call(s32[4,64]{1,0:T(4,128)S(1)} %copy-done.1, s32[2,4,4]{2,1,0:T(4,128)S(1)} %copy-done, s32[2]{0:T(128)S(1)} %pad_add_fusion.place_ref, bf16[384,256]{1,0:T(8,128)(2,1)S(1)} %get-tuple-element.25.off_ref, bf16[392,256]{1,0:T(8,128)(2,1)S(1)} %get-tuple-element.22.inn_ref, ...), custom_call_target="tpu_custom_call" | custom-call | flops 1358954496 | bytes 8388608 | tf_op jit(solution)/shard_map/outer/pallas_call | solution.py:540
  28.5 1.8 %collective-permute-start.6 = (bf16[384,256]{1,0:T(8,128)(2,1)S(1)}, bf16[384,256]{1,0:T(8,128)(2,1)S(1)}, u32[]{:S(2)}, u32[]{:S(2)}) collective-permute-start(bf16[384,256]{1,0:T(8,128)(2,1)S(1)} %get-tuple-element.39), channel_id=1, source_target_pairs={{0,16},{16,0},{1,17},{17,1},{2,18},{18,2},{3,19},{19,3},{4,20},{20... | collective-permute-start | bytes 589832 | tf_op jit(solution)/shard_map/ppermute | solution.py:563
  30.3 0.0 copy-done.2
  30.3 6.4 %policy.1 = (bf16[2,4,128,128]{3,2,1,0:T(8,128)(2,1)}, bf16[768,512]{1,0:T(8,128)(2,1)}) custom-call(s32[4,64]{1,0:T(4,128)S(1)} %copy-done.2, s32[2]{0:T(128)S(1)} %pad_add_fusion.place_ref, bf16[384,256]{1,0:T(8,128)(2,1)S(1)} %get-tuple-element.25.off_ref, bf16[392,256]{1,0:T(8,128)(2,1)S(1)} %get-tuple-element.22.inn_ref, ...), custom_call_target="tpu_custom_call" | custom-call | flops 4227858432 | bytes 12582912 | tf_op jit(solution)/shard_map/policy/pallas_call | solution.py:564
  36.6 0.0 collective-permute-done.6
  36.7 0.7 %bitcast_dynamic-update-slice_fusion = bf16[1,1,768,512]{3,2,1,0:T(8,128)(2,1)} fusion(bf16[1,1,768,512]{3,2,1,0:T(8,128)(2,1)} %bitcast.5, s32[]{:T(128)S(6)} %select_n.3, bf16[384,256]{1,0:T(8,128)(2,1)S(1)} %collective-permute-done.6), kind=kLoop, calls=%fused_computation | loop fusion | bytes 393220 | tf_op jit(solution)/shard_map/dynamic_update_slice | solution.py:599
Async XLA Ops:
  2.3 8.0 %collective-permute-start.1 = (bf16[392,256]{1,0:T(8,128)(2,1)S(1)}, bf16[392,256]{1,0:T(8,128)(2,1)S(1)}, u32[]{:S(2)}, u32[]{:S(2)}) collective-permute-start(bf16[392,256]{1,0:T(8,128)(2,1)S(1)} %get-tuple-element.22.inn_ref), channel_id=1, source_target_pairs={{0,16},{16,0},{1,17},{17,1},{2,18},{18,2},{3,19},{19,3},{4,20},{20... | collective-permute-start | bytes 602120 | tf_op jit(solution)/shard_map/ppermute | solution.py:464
  5.4 12.3 %collective-permute-start.4 = (bf16[392,256]{1,0:T(8,128)(2,1)S(1)}, bf16[392,256]{1,0:T(8,128)(2,1)S(1)}, u32[]{:S(2)}, u32[]{:S(2)}) collective-permute-start(bf16[392,256]{1,0:T(8,128)(2,1)S(1)} %get-tuple-element.22.inn_ref), channel_id=1, source_target_pairs={{0,1},{1,0},{2,3},{3,2},{4,5},{5,4},{6,7},{7,6},{8,9},{9,8},{10,11... | collective-permute-start | bytes 602120 | tf_op jit(solution)/shard_map/ppermute | solution.py:467
  10.4 7.3 %collective-permute-start.5 = (bf16[392,256]{1,0:T(8,128)(2,1)S(1)}, bf16[392,256]{1,0:T(8,128)(2,1)S(1)}, u32[]{:S(2)}, u32[]{:S(2)}) collective-permute-start(bf16[392,256]{1,0:T(8,128)(2,1)S(1)} %collective-permute-done.1.other_inn_ref), channel_id=1, source_target_pairs={{0,1},{1,0},{2,3},{3,2},{4,5},{5,4},{6,7},{7,6},{8,9},{9,8},{10,11... | collective-permute-start | bytes 602120 | tf_op jit(solution)/shard_map/ppermute | solution.py:491
  10.4 7.3 %collective-permute-start = (bf16[384,256]{1,0:T(8,128)(2,1)S(1)}, bf16[384,256]{1,0:T(8,128)(2,1)S(1)}, u32[]{:S(2)}, u32[]{:S(2)}) collective-permute-start(bf16[384,256]{1,0:T(8,128)(2,1)S(1)} %get-tuple-element.25.off_ref), channel_id=1, source_target_pairs={{0,16},{16,0},{1,17},{17,1},{2,18},{18,2},{3,19},{19,3},{4,20},{20... | collective-permute-start | bytes 589832 | tf_op jit(solution)/shard_map/ppermute | solution.py:465
  12.1 13.1 %collective-permute-start.2 = (bf16[384,256]{1,0:T(8,128)(2,1)S(1)}, bf16[384,256]{1,0:T(8,128)(2,1)S(1)}, u32[]{:S(2)}, u32[]{:S(2)}) collective-permute-start(bf16[384,256]{1,0:T(8,128)(2,1)S(1)} %get-tuple-element.25.off_ref), channel_id=1, source_target_pairs={{2,1},{4,3},{6,5},{8,7},{10,9},{12,11},{14,13},{1,2},{3,4},{5,6},{... | collective-permute-start | bytes 589832 | tf_op jit(solution)/shard_map/ppermute | solution.py:466
  12.8 12.4 %collective-permute-start.3 = (bf16[384,256]{1,0:T(8,128)(2,1)S(1)}, bf16[384,256]{1,0:T(8,128)(2,1)S(1)}, u32[]{:S(2)}, u32[]{:S(2)}) collective-permute-start(bf16[384,256]{1,0:T(8,128)(2,1)S(1)} %get-tuple-element.25.off_ref), channel_id=1, source_target_pairs={{2,17},{4,19},{6,21},{8,23},{10,25},{12,27},{14,29},{1,18},{3,20},... | collective-permute-start | bytes 589832 | tf_op jit(solution)/shard_map/ppermute | solution.py:490
  17.7 0.7 %copy-start = (s32[2,4,4]{2,1,0:T(4,128)S(1)}, s32[2,4,4]{2,1,0:T(4,128)}, u32[]{:S(2)}) copy-start(s32[2,4,4]{2,1,0:T(4,128)} %near_ref.3) | copy-start | bytes 388
  18.4 0.7 %copy-start.1 = (s32[4,64]{1,0:T(4,128)S(1)}, s32[4,64]{1,0:T(4,128)}, u32[]{:S(2)}) copy-start(s32[4,64]{1,0:T(4,128)} %fill_ref.5) | copy-start | bytes 3076
  25.2 5.1 %copy-start.2 = (s32[4,64]{1,0:T(4,128)S(1)}, s32[4,64]{1,0:T(4,128)}, u32[]{:S(2)}) copy-start(s32[4,64]{1,0:T(4,128)} %fill_ref.5) | copy-start | bytes 3076
  28.5 8.2 %collective-permute-start.6 = (bf16[384,256]{1,0:T(8,128)(2,1)S(1)}, bf16[384,256]{1,0:T(8,128)(2,1)S(1)}, u32[]{:S(2)}, u32[]{:S(2)}) collective-permute-start(bf16[384,256]{1,0:T(8,128)(2,1)S(1)} %get-tuple-element.39), channel_id=1, source_target_pairs={{0,16},{16,0},{1,17},{17,1},{2,18},{18,2},{3,19},{19,3},{4,20},{20... | collective-permute-start | bytes 589832 | tf_op jit(solution)/shard_map/ppermute | solution.py:563

commit v3 on v2

v3 whole, which is shorter than its diff:
```python
import math

import jax
import jax.numpy as jnp
from jax import lax
from jax.experimental import pallas as pl
from jax.experimental.pallas import tpu as pltpu
from jax.sharding import PartitionSpec as P

HEADS = 4
LIVE = 96
REACH = 2
SCORE_CAP = 30.0
NORM_EPS = 1e-06
LOG2_E = math.log2(math.e)
TARGET_ROWS = 8
MIB = 1 << 20
BF16 = jnp.bfloat16
F32 = jnp.float32


def nt_dot(a, b):
    return lax.dot_general(a, b, (((1,), (1,)), ((), ())), preferred_element_type=F32)


def key_tables(table_ref, fill_ref, near_ref, b, lx, ly, place):
    row_x, row_y, blocks_x, blocks_y = place
    rows_x, rows_y = fill_ref.shape
    columns = blocks_y + 2 * REACH
    key_blocks = near_ref.shape[2] + 1
    home_x = row_x * blocks_x + lx
    home_y = row_y * blocks_y + ly
    table_ref[b, 0] = lx * columns + ly + REACH
    table_ref[b, key_blocks] = fill_ref[home_x, home_y]
    for d in range(key_blocks - 1):
        direction = near_ref[lx, ly, d]
        cell = direction + jnp.where(direction >= 12, 1, 0)
        cell_x = (cell * 13) >> 6
        step_x = cell_x - REACH
        step_y = cell - cell_x * 5 - REACH
        at_x = home_x + step_x
        at_y = home_y + step_y
        inside = (at_x >= 0) & (at_x < rows_x) & (at_y >= 0) & (at_y < rows_y)
        safe_x = jnp.clip(at_x, 0, rows_x - 1)
        safe_y = jnp.clip(at_y, 0, rows_y - 1)
        tile_x = jnp.where(safe_x >= blocks_x, 1, 0)
        other = jnp.where(tile_x == row_x, 0, 1)
        in_x = safe_x - tile_x * blocks_x
        table_ref[b, 1 + d] = (other * blocks_x + in_x) * columns + ly + step_y + REACH
        table_ref[b, key_blocks + 1 + d] = jnp.where(inside, fill_ref[safe_x, safe_y], 0)


def one_hot(base, capacity, block_len, target_rows):
    row = lax.broadcasted_iota(jnp.int32, (capacity, block_len), 0) + base
    row = row.astype(F32)
    return jnp.concatenate(
        [jnp.where(row == target, 1.0, 0.0).astype(BF16) for target in target_rows], axis=1
    )


def place(pick, pad_ref):
    blocks, block_len, width = pad_ref.shape
    flat = pad_ref[...].reshape(blocks * block_len, width)
    return jnp.dot(pick, flat, preferred_element_type=F32)


def sent_targets(ref, first, count):
    start = ref.shape[0] - TARGET_ROWS
    half = ref.shape[1] // 2
    both = ref[start : start + TARGET_ROWS].astype(F32)
    rows = both[:, :half] * 256.0 + both[:, half:]
    return [rows[b : b + 1] for b in range(first, first + count)]


def spread(pad_ref, first, rows, blocks):
    _, block_len, width = pad_ref.shape
    for b in range(blocks):
        pad_ref[first + b, :LIVE] = rows[b * LIVE : (b + 1) * LIVE]
        pad_ref[first + b, LIVE:] = jnp.zeros((block_len - LIVE, width), pad_ref.dtype)


def stage_kernel(place_ref, target_hbm, agents_hbm, off_ref, inn_ref, target_ref, sems):
    blocks_x, _, _, _ = agents_hbm.shape
    core = place_ref[1] & 1
    rows = REACH * LIVE
    targets = pltpu.make_async_copy(target_hbm, target_ref, sems.at[2, 0])
    targets.start()
    copies = []
    for x in range(blocks_x):
        for ref, column, s in ((off_ref, core * REACH, 0), (inn_ref, REACH - core * REACH, 1)):
            copies.append(
                pltpu.make_async_copy(
                    agents_hbm.at[x, pl.ds(column, REACH), pl.ds(0, LIVE)],
                    ref.at[pl.ds(x * rows, rows)].reshape(REACH, LIVE, ref.shape[1]),
                    sems.at[s, x],
                )
            )
    for copy in copies:
        copy.start()
    targets.wait()
    halves = []
    for column in (core * REACH, REACH - core * REACH):
        for x in range(blocks_x):
            for c in range(REACH):
                halves.append(target_ref[x, pl.ds(column + c, 1), :])
    target = jnp.concatenate(halves, axis=0)
    high = target >> 8
    low = target - high * 256
    split = jnp.concatenate([high, low], axis=1).astype(F32).astype(BF16)
    inn_ref[blocks_x * rows :] = split
    for copy in copies:
        copy.wait()


def local_kernel(
    fill_ref,
    near_ref,
    place_ref,
    off_ref,
    inn_ref,
    weight_in_hbm,
    weight_out_hbm,
    weight_in_ref,
    weight_out_ref,
    own_rows_ref,
    pick_out_ref,
    table_ref,
    token_ref,
    pad_ref,
    sems,
):
    copies = [
        pltpu.make_async_copy(weight_in_hbm, weight_in_ref, sems.at[0]),
        pltpu.make_async_copy(weight_out_hbm, weight_out_ref, sems.at[1]),
    ]
    for copy in copies:
        copy.start()
    capacity = own_rows_ref.shape[0]
    blocks, block_len, _ = pad_ref.shape
    row_x = place_ref[0]
    core = place_ref[1] & 1
    place_of = (row_x, place_ref[1], blocks // (2 * REACH), 2 * REACH)
    for half, first in enumerate((core * REACH, REACH - core * REACH)):
        for i in range(blocks // 2):
            b = half * (blocks // 2) + i
            at = (i // REACH, first + i % REACH)
            key_tables(table_ref, fill_ref, near_ref, b, *at, place_of)
    spread(pad_ref, 0, off_ref, blocks // 2)
    spread(pad_ref, blocks // 2, inn_ref, blocks // 2)
    targets = sent_targets(inn_ref, 0, blocks)
    pick_out_ref[...] = one_hot(
        ((1 - row_x) * 2 + row_x) * capacity, capacity, block_len, targets
    )
    pick = one_hot((row_x * 2 + row_x) * capacity, capacity, block_len, targets)
    own_rows_ref[...] = place(pick, pad_ref).astype(BF16)
    token_ref[...] = jnp.zeros_like(token_ref)
    for copy in copies:
        copy.wait()


def attention_kernel(
    table_ref,
    place_ref,
    off_ref,
    inn_ref,
    other_off_ref,
    other_inn_ref,
    side_off_ref,
    side_inn_ref,
    other_side_off_ref,
    other_side_inn_ref,
    weight_in_ref,
    weight_out_ref,
    pick_out_ref,
    token_ref,
    summary_ref,
    packed_ref,
    keys_ref,
    values_ref,
    context_ref,
    pad_ref,
):
    width = weight_out_ref.shape[0]
    head = width // HEADS
    half_rows = off_ref.shape[0]
    each = half_rows // LIVE
    blocks_x = each // REACH
    columns = 4 * REACH
    core = place_ref[1] & 1
    at_off = REACH + REACH * core
    at_inn = 2 * REACH - REACH * core
    at_side_off = 3 * REACH * core
    at_side_inn = 3 * REACH - 3 * REACH * core
    sources = (
        (0, at_off, off_ref),
        (0, at_inn, inn_ref),
        (1, at_off, other_off_ref),
        (1, at_inn, other_inn_ref),
        (0, at_side_off, side_off_ref),
        (0, at_side_inn, side_inn_ref),
        (1, at_side_off, other_side_off_ref),
        (1, at_side_inn, other_side_inn_ref),
    )
    for o, column, ref in sources:
        rows = ref[:half_rows]
        both = jnp.dot(rows, weight_in_ref[:, width:], preferred_element_type=F32).astype(BF16)
        both = both.reshape(each, LIVE, 2 * width)
        for x in range(blocks_x):
            at = (o * blocks_x + x) * columns + column
            keys_ref[pl.ds(at, REACH)] = both[x * REACH : (x + 1) * REACH, :, :width]
            values_ref[pl.ds(at, REACH)] = both[x * REACH : (x + 1) * REACH, :, width:]

    key_blocks = table_ref.shape[1] // 2
    lane = lax.broadcasted_iota(jnp.int32, (1, key_blocks * LIVE), 1)
    head_of = lax.broadcasted_iota(jnp.int32, (1, width), 1) // head
    queries = [
        jnp.dot(ref[:half_rows], weight_in_ref[:, :width], preferred_element_type=F32).astype(BF16)
        for ref in (off_ref, inn_ref)
    ]
    for b in range(2 * each):
        where_to = [table_ref[b, j] for j in range(key_blocks)]
        counts = [table_ref[b, key_blocks + j] for j in range(key_blocks)]
        i = b % each
        query = queries[b // each][i * LIVE : (i + 1) * LIVE]
        split = jnp.concatenate(
            [jnp.where(head_of == h, query, jnp.zeros_like(query)) for h in range(HEADS)],
            axis=0,
        )
        keys = jnp.concatenate([keys_ref[w] for w in where_to], axis=0)
        values = jnp.concatenate([values_ref[w] for w in where_to], axis=0)
        end = jnp.full(lane.shape, counts[0], jnp.int32)
        for j in range(1, key_blocks):
            end = jnp.where(lane >= j * LIVE, counts[j] + j * LIVE, end)
        raw = nt_dot(split, keys)
        capped = jnp.tanh(raw * (1.0 / (math.sqrt(head) * SCORE_CAP)))
        weight = jnp.exp2(capped * (SCORE_CAP * LOG2_E))
        weight = jnp.where(lane < end, weight, 0.0)
        total = jnp.sum(weight, axis=-1, keepdims=True)
        weight = (weight * (1.0 / total)).astype(BF16)
        mixed = jnp.dot(weight, values, preferred_element_type=F32)
        context = mixed[:LIVE]
        for h in range(1, HEADS):
            context = jnp.where(head_of == h, mixed[h * LIVE : (h + 1) * LIVE], context)
        context_ref[b * LIVE : (b + 1) * LIVE] = context.astype(BF16)
    out = jnp.dot(context_ref[...], weight_out_ref[...], preferred_element_type=F32)
    scale = lax.rsqrt(jnp.mean(out * out, axis=-1, keepdims=True) + NORM_EPS)
    out = (out * scale).astype(BF16)
    summary_ref[...] = out
    spread(pad_ref, 0, out, 2 * each)
    packed_ref[...] = place(pick_out_ref[...], pad_ref).astype(BF16)


def silu(v):
    half = 0.5 * v
    return half + half * jnp.tanh(half)


def policy_kernel(
    table_ref,
    place_ref,
    off_ref,
    inn_ref,
    other_off_ref,
    other_inn_ref,
    summary_ref,
    own_rows_ref,
    policy_in_ref,
    policy_mid_ref,
    policy_out_ref,
    actions_ref,
    batch_ref,
    x_ref,
    h_ref,
    g_ref,
    pad_ref,
):
    width = off_ref.shape[1]
    blocks_x, blocks_y, block_len, _ = actions_ref.shape
    row_x = place_ref[0]
    core = place_ref[1] & 1
    capacity = batch_ref.shape[0] // 2
    half_rows = off_ref.shape[0]
    x_ref[:half_rows, :width] = off_ref[...]
    x_ref[half_rows:, :width] = inn_ref[:half_rows]
    x_ref[:, width:] = summary_ref[...]
    chunk = 256
    hidden = policy_in_ref.shape[1]
    for n in range(0, hidden, chunk):
        v = jnp.dot(x_ref[...], policy_in_ref[:, n : n + chunk], preferred_element_type=F32)
        h_ref[:, n : n + chunk] = silu(v).astype(BF16)
    now, later = h_ref, g_ref
    for m in range(policy_mid_ref.shape[0]):
        for n in range(0, hidden, chunk):
            v = jnp.dot(
                now[...], policy_mid_ref[m, :, n : n + chunk], preferred_element_type=F32
            )
            later[:, n : n + chunk] = silu(v).astype(BF16)
        now, later = later, now
    acts = jnp.dot(now[...], policy_out_ref[...], preferred_element_type=F32)
    slot = lax.broadcasted_iota(jnp.int32, (LIVE, 1), 0)
    for half, first in enumerate((core * REACH, REACH - core * REACH)):
        for i in range(blocks_x * REACH):
            lx = i // REACH
            ly = first + i % REACH
            b = half * blocks_x * REACH + i
            fill = table_ref[b, table_ref.shape[1] // 2]
            act = jnp.where(slot < fill, acts[b * LIVE : (b + 1) * LIVE], 0.0)
            actions_ref[lx, ly, :LIVE] = act.astype(BF16)
            actions_ref[lx, ly, LIVE:] = jnp.zeros((block_len - LIVE, act.shape[1]), BF16)

    mine = pl.ds(pl.multiple_of(row_x * capacity, capacity), capacity)
    theirs = pl.ds(pl.multiple_of((1 - row_x) * capacity, capacity), capacity)
    blocks = pad_ref.shape[0]
    batch_ref[mine, :width] = own_rows_ref[...]
    spread(pad_ref, 0, summary_ref, blocks)
    pick = one_hot(
        (row_x * 2 + row_x) * capacity, capacity, block_len, sent_targets(inn_ref, 0, blocks)
    )
    batch_ref[mine, width:] = place(pick, pad_ref).astype(BF16)
    spread(pad_ref, 0, other_off_ref, blocks // 2)
    spread(pad_ref, blocks // 2, other_inn_ref, blocks // 2)
    pick = one_hot(
        (row_x * 2 + 1 - row_x) * capacity,
        capacity,
        block_len,
        sent_targets(other_inn_ref, 0, blocks),
    )
    batch_ref[theirs, :width] = place(pick, pad_ref).astype(BF16)
    batch_ref[theirs, width:] = jnp.zeros((capacity, width), BF16)


VMEM = pl.BlockSpec(memory_space=pltpu.VMEM)
SMEM = pl.BlockSpec(memory_space=pltpu.SMEM)
HBM = pl.BlockSpec(memory_space=pltpu.HBM)
SDS = jax.ShapeDtypeStruct


def in_hbm(*arrays):
    return tuple(pltpu.with_memory_space_constraint(a, pltpu.HBM) for a in arrays)


def on_device(
    agents,
    block_fill,
    neighbours,
    target_slot,
    attention_in,
    attention_out,
    policy_in,
    policy_mid,
    policy_out,
):
    blocks_x, blocks_y, block_len, width = agents.shape
    all_blocks = blocks_x * blocks_y
    owners = lax.axis_size("gx")
    count_y = lax.axis_size("gy")
    row_x = lax.axis_index("gx")
    capacity = 3 * all_blocks * block_len // (4 * owners)
    hidden = policy_in.shape[1]
    acts = policy_out.shape[1]
    slots = all_blocks * LIVE
    half_rows = slots // 2
    rows = owners * capacity
    block_fill, neighbours = in_hbm(block_fill, neighbours)
    where = jnp.stack([row_x, lax.axis_index("gy")]).astype(jnp.int32)

    swap = [(0, 1), (1, 0)]
    across = [(i, i - 1) for i in range(2, count_y, 2)]
    across += [(i, i + 1) for i in range(1, count_y - 1, 2)]
    beside = [(i, i ^ 1) for i in range(count_y)]
    diagonal = [
        (g * count_y + a, (1 - g) * count_y + b) for g in range(owners) for a, b in across
    ]

    off, inn = pl.pallas_call(
        stage_kernel,
        out_shape=(SDS((half_rows, width), BF16), SDS((half_rows + TARGET_ROWS, width), BF16)),
        in_specs=[SMEM, HBM, HBM],
        out_specs=(VMEM, VMEM),
        scratch_shapes=[
            pltpu.VMEM((blocks_x, blocks_y, block_len), jnp.int32),
            pltpu.SemaphoreType.DMA((3, blocks_x)),
        ],
        compiler_params=pltpu.CompilerParams(vmem_limit_bytes=4 * MIB),
        name="stage",
    )(where, *in_hbm(target_slot, agents))
    other_inn = lax.ppermute(inn, "gx", swap)
    other_off = lax.ppermute(off, "gx", swap)
    side_off = lax.ppermute(off, "gy", across)
    side_inn = lax.ppermute(inn, "gy", beside)
    attention_in, attention_out, own_rows, pick_out, table, token = pl.pallas_call(
        local_kernel,
        out_shape=(
            SDS(attention_in.shape, BF16),
            SDS(attention_out.shape, BF16),
            SDS((capacity, width), BF16),
            SDS((capacity, all_blocks * block_len), BF16),
            SDS((all_blocks, 2 * neighbours.shape[2] + 2), jnp.int32),
            SDS((8, 128), F32),
        ),
        in_specs=[SMEM] * 3 + [VMEM] * 2 + [HBM] * 2,
        out_specs=(VMEM,) * 4 + (SMEM, VMEM),
        scratch_shapes=[
            pltpu.VMEM((all_blocks, block_len, width), BF16),
            pltpu.SemaphoreType.DMA((3,)),
        ],
        compiler_params=pltpu.CompilerParams(vmem_limit_bytes=8 * MIB),
        cost_estimate=pl.CostEstimate(
            flops=2 * capacity * all_blocks * block_len * width,
            bytes_accessed=8 * MIB,
            transcendentals=0,
        ),
        name="local",
    )(block_fill, neighbours, where, off, inn, *in_hbm(attention_in, attention_out))
    other_side_off = lax.ppermute(off, ("gx", "gy"), diagonal)
    other_inn, other_off, side_off, side_inn, other_side_off, token = lax.optimization_barrier(
        (other_inn, other_off, side_off, side_inn, other_side_off, token)
    )
    other_side_inn = lax.ppermute(other_inn, "gy", beside)

    window = blocks_x * owners * (blocks_y + 2 * REACH)
    scores = all_blocks * HEADS * LIVE * 5 * LIVE
    summary, packed = pl.pallas_call(
        attention_kernel,
        out_shape=(SDS((slots, width), BF16), SDS((capacity, width), BF16)),
        in_specs=[SMEM] * 2 + [VMEM] * 12,
        out_specs=(VMEM, VMEM),
        scratch_shapes=[
            pltpu.VMEM((window, LIVE, width), BF16),
            pltpu.VMEM((window, LIVE, width), BF16),
            pltpu.VMEM((slots, width), BF16),
            pltpu.VMEM((all_blocks, block_len, width), BF16),
        ],
        compiler_params=pltpu.CompilerParams(vmem_limit_bytes=16 * MIB),
        cost_estimate=pl.CostEstimate(
            flops=2 * (2 * scores + window * LIVE * 2 * width) * width,
            bytes_accessed=8 * MIB,
            transcendentals=2 * scores,
        ),
        name="attention",
    )(
        table,
        where,
        off,
        inn,
        other_off,
        other_inn,
        side_off,
        side_inn,
        other_side_off,
        other_side_inn,
        attention_in,
        attention_out,
        pick_out,
        token,
    )
    arrived = lax.ppermute(packed, "gx", swap)
    actions, batch = pl.pallas_call(
        policy_kernel,
        out_shape=(
            SDS((blocks_x, blocks_y, block_len, acts), BF16),
            SDS((rows, 2 * width), BF16),
        ),
        in_specs=[SMEM] * 2 + [VMEM] * 9,
        out_specs=(VMEM, VMEM),
        scratch_shapes=[
            pltpu.VMEM((slots, 2 * width), BF16),
            pltpu.VMEM((slots, hidden), BF16),
            pltpu.VMEM((slots, hidden), BF16),
            pltpu.VMEM((all_blocks, block_len, width), BF16),
        ],
        compiler_params=pltpu.CompilerParams(vmem_limit_bytes=16 * MIB),
        cost_estimate=pl.CostEstimate(
            flops=2 * slots * hidden * (2 * width + 2 * hidden + acts),
            bytes_accessed=12 * MIB,
            transcendentals=3 * slots * hidden,
        ),
        name="policy",
    )(
        table,
        where,
        off,
        inn,
        other_off,
        other_inn,
        summary,
        own_rows,
        policy_in,
        policy_mid,
        policy_out,
    )
    batch = lax.dynamic_update_slice(batch, arrived, ((1 - row_x) * capacity, width))
    return actions, batch.reshape(1, 1, rows, 2 * width)


def solution(mesh):
    return jax.shard_map(
        on_device,
        mesh=mesh,
        in_specs=(
            P("gx", "gy", None, None),
            P(),
            P("gx", "gy", None),
            P("gx", "gy", None),
            P(),
            P(),
            P(),
            P(),
            P(),
        ),
        out_specs=(P("gx", "gy", None, None), P("gx", "gy", None, None)),
        check_vma=False,
    )
```

time: 37.6 us -> 33.9 us (0.902)
  the two profiles are of different devices: /device:TPU:0 before, /device:TPU:2 now
where the time goes in v3:
time: 33.9 us; the launch traced here: 33.6 us
  Pallas kernels  16.2 us (48%)
  starting transfers between devices  10.4 us (31%)
  waiting for transfers between devices  5.46 us (16%)
  local copies, waits for them, and re-layouts  0.7 us (2%)
  between operations  0.7 us (2%)
    pallas_call x1, Pallas kernels, on_device(): pl.pallas_call(policy_kernel, out_shape=(SDS((blocks_x, blocks_y, block_l...  6.97 us
    pallas_call x1, Pallas kernels, on_device(): pl.pallas_call(attention_kernel, out_shape=(SDS((slots, width), BF16), SD...  4.6 us
    ppermute x1, starting transfers between devices, on_device(): side_off = lax.ppermute(off, 'gy', across)  3.58 us
    ppermute x1, waiting for transfers between devices, on_device(): side_off = lax.ppermute(off, 'gy', across)  3.17 us
    pallas_call x1, Pallas kernels, on_device(): pl.pallas_call(local_kernel, out_shape=(SDS(attention_in.shape, BF16), SD...  3.01 us
    ppermute x1, starting transfers between devices, on_device(): other_side_off = lax.ppermute(off, ('gx', 'gy'), diagonal)  1.91 us
    pallas_call x1, Pallas kernels, on_device(): pl.pallas_call(stage_kernel, out_shape=(SDS((half_rows, width), BF16), SD...  1.64 us
    ppermute x1, starting transfers between devices, on_device(): arrived = lax.ppermute(packed, 'gx', swap)  1.59 us
  transfers between devices with their start and end apart: 7, of which 3 were waited for; matrix products, arithmetic and copies ran while one was open for 0% of the time, Pallas kernels for 30%

profile of v3, /device:TPU:2, one launch (start us, length us, event | category | flops | bytes accessed | tf_op | source)
XLA Modules:
  0.0 33.6 jit_solution(2017022729069191202)
XLA Ops:
  0.6 0.1 pad_add_fusion.place_ref
  0.7 1.6 %stage.1 = (bf16[384,256]{1,0:T(8,128)(2,1)S(1)}, bf16[392,256]{1,0:T(8,128)(2,1)S(1)}) custom-call(s32[2]{0:T(128)S(1)} %pad_add_fusion.place_ref, s32[2,4,128]{2,1,0:T(4,128)} %target_hbm.1, bf16[2,4,128,256]{3,2,1,0:T(8,128)(2,1)} %agents_hbm.1), custom_call_target="tpu_custom_call" | custom-call | tf_op jit(solution)/shard_map/stage/pallas_call | solution.py:375
  2.4 0.1 collective-permute-start.3
  2.4 1.6 %collective-permute-start = (bf16[392,256]{1,0:T(8,128)(2,1)S(1)}, bf16[392,256]{1,0:T(8,128)(2,1)S(1)}, u32[]{:S(2)}, u32[]{:S(2)}) collective-permute-start(bf16[392,256]{1,0:T(8,128)(2,1)S(1)} %get-tuple-element.21.inn_ref), channel_id=1, source_target_pairs={{0,16},{16,0},{1,17},{17,1},{2,18},{18,2},{3,19},{19,3},{4,20},{20... | collective-permute-start | bytes 602120 | tf_op jit(solution)/shard_map/ppermute | solution.py:387
  4.0 1.9 %collective-permute-start.4 = (bf16[384,256]{1,0:T(8,128)(2,1)S(1)}, bf16[384,256]{1,0:T(8,128)(2,1)S(1)}, u32[]{:S(2)}, u32[]{:S(2)}) collective-permute-start(bf16[384,256]{1,0:T(8,128)(2,1)S(1)} %get-tuple-element.20.off_ref), channel_id=1, source_target_pairs={{2,17},{4,19},{6,21},{8,23},{10,25},{12,27},{14,29},{1,18},{3,20},... | collective-permute-start | bytes 589832 | tf_op jit(solution)/shard_map/ppermute | solution.py:415
  5.9 3.6 %collective-permute-start.2 = (bf16[384,256]{1,0:T(8,128)(2,1)S(1)}, bf16[384,256]{1,0:T(8,128)(2,1)S(1)}, u32[]{:S(2)}, u32[]{:S(2)}) collective-permute-start(bf16[384,256]{1,0:T(8,128)(2,1)S(1)} %get-tuple-element.20.off_ref), channel_id=1, source_target_pairs={{2,1},{4,3},{6,5},{8,7},{10,9},{12,11},{14,13},{1,2},{3,4},{5,6},{... | collective-permute-start | bytes 589832 | tf_op jit(solution)/shard_map/ppermute | solution.py:389
  9.5 1.6 %collective-permute-start.1 = (bf16[384,256]{1,0:T(8,128)(2,1)S(1)}, bf16[384,256]{1,0:T(8,128)(2,1)S(1)}, u32[]{:S(2)}, u32[]{:S(2)}) collective-permute-start(bf16[384,256]{1,0:T(8,128)(2,1)S(1)} %get-tuple-element.20.off_ref), channel_id=1, source_target_pairs={{0,16},{16,0},{1,17},{17,1},{2,18},{18,2},{3,19},{19,3},{4,20},{20... | collective-permute-start | bytes 589832 | tf_op jit(solution)/shard_map/ppermute | solution.py:388
  11.1 3.0 %local.1 = (bf16[256,768]{1,0:T(8,128)(2,1)S(1)}, bf16[256,256]{1,0:T(8,128)(2,1)S(1)}, bf16[384,256]{1,0:T(8,128)(2,1)S(1)}, bf16[384,1024]{1,0:T(8,128)(2,1)S(...) custom-call(s32[4,64]{1,0:T(4,128)} %fill_ref.1, s32[2,4,4]{2,1,0:T(4,128)} %near_ref.1, s32[2]{0:T(128)S(1)} %pad_add_fusion.place_ref, ...), custom_call_target="tpu_custom_call" | custom-call | flops 201326592 | bytes 8388608 | tf_op jit(solution)/shard_map/local/pallas_call | solution.py:391
  14.1 0.0 collective-permute-done.4.other_side_off_ref
  14.1 3.2 %collective-permute-done.2.side_off_ref = bf16[384,256]{1,0:T(8,128)(2,1)S(1)} collective-permute-done((bf16[384,256]{1,0:T(8,128)(2,1)S(1)}, bf16[384,256]{1,0:T(8,128)(2,1)S(1)}, u32[]{:S(2)}, u32[]{:S(2)}) %collective-permute-start.2) | collective-permute-done | bytes 196640 | tf_op jit(solution)/shard_map/ppermute | solution.py:389
  17.3 1.0 %collective-permute-done.1.other_off_ref = bf16[384,256]{1,0:T(8,128)(2,1)S(1)} collective-permute-done((bf16[384,256]{1,0:T(8,128)(2,1)S(1)}, bf16[384,256]{1,0:T(8,128)(2,1)S(1)}, u32[]{:S(2)}, u32[]{:S(2)}) %collective-permute-start.1) | collective-permute-done | bytes 196640 | tf_op jit(solution)/shard_map/ppermute | solution.py:388
  18.3 0.0 collective-permute-done.3.side_inn_ref
  18.3 0.0 collective-permute-done.other_inn_ref
  18.3 0.1 collective-permute-start.5
  18.4 1.3 %collective-permute-done.5.other_side_inn_ref = bf16[392,256]{1,0:T(8,128)(2,1)S(1)} collective-permute-done((bf16[392,256]{1,0:T(8,128)(2,1)S(1)}, bf16[392,256]{1,0:T(8,128)(2,1)S(1)}, u32[]{:S(2)}, u32[]{:S(2)}) %collective-permute-start.5) | collective-permute-done | bytes 200736 | tf_op jit(solution)/shard_map/ppermute | solution.py:419
  19.7 0.0 copy-start
  19.7 0.0 copy-start.1
  19.7 0.0 copy-start.2
  19.7 4.6 %attention.1 = (bf16[768,256]{1,0:T(8,128)(2,1)S(1)}, bf16[384,256]{1,0:T(8,128)(2,1)S(1)}) custom-call(s32[8,10]{1,0:T(8,128)S(1)} %get-tuple-element.22.table_ref, s32[2]{0:T(128)S(1)} %pad_add_fusion.place_ref, bf16[384,256]{1,0:T(8,128)(2,1)S(1)} %get-tuple-element.20.off_ref, bf16[392,256]{1,0:T(8,128)(2,1)S(1)} %get-tuple-element.21.inn_ref, ...), custom_call_target="tpu_custom_call" | custom-call | flops 2315255808 | bytes 8388608 | tf_op jit(solution)/shard_map/attention/pallas_call | solution.py:423
  24.3 1.6 %collective-permute-start.6 = (bf16[384,256]{1,0:T(8,128)(2,1)S(1)}, bf16[384,256]{1,0:T(8,128)(2,1)S(1)}, u32[]{:S(2)}, u32[]{:S(2)}) collective-permute-start(bf16[384,256]{1,0:T(8,128)(2,1)S(1)} %get-tuple-element.37), channel_id=1, source_target_pairs={{0,16},{16,0},{1,17},{17,1},{2,18},{18,2},{3,19},{19,3},{4,20},{20... | collective-permute-start | bytes 589832 | tf_op jit(solution)/shard_map/ppermute | solution.py:457
  25.9 0.0 copy-done
  25.9 0.0 copy-done.1
  25.9 0.0 copy-done.2
  25.9 7.0 %policy.1 = (bf16[2,4,128,128]{3,2,1,0:T(8,128)(2,1)}, bf16[768,512]{1,0:T(8,128)(2,1)}) custom-call(s32[8,10]{1,0:T(8,128)S(1)} %get-tuple-element.22.table_ref, s32[2]{0:T(128)S(1)} %pad_add_fusion.place_ref, bf16[384,256]{1,0:T(8,128)(2,1)S(1)} %get-tuple-element.20.off_ref, bf16[392,256]{1,0:T(8,128)(2,1)S(1)} %get-tuple-element.21.inn_ref, ...), custom_call_target="tpu_custom_call" | custom-call | flops 4227858432 | bytes 12582912 | tf_op jit(solution)/shard_map/policy/pallas_call | solution.py:458
  32.9 0.0 collective-permute-done.6
  32.9 0.7 %bitcast_dynamic-update-slice_fusion = bf16[1,1,768,512]{3,2,1,0:T(8,128)(2,1)} fusion(bf16[1,1,768,512]{3,2,1,0:T(8,128)(2,1)} %bitcast.5, s32[]{:T(128)S(6)} %select_n.3, bf16[384,256]{1,0:T(8,128)(2,1)S(1)} %collective-permute-done.6), kind=kLoop, calls=%fused_computation | loop fusion | bytes 393220 | tf_op jit(solution)/shard_map/dynamic_update_slice | solution.py:492
Async XLA Ops:
  2.4 15.9 %collective-permute-start.3 = (bf16[392,256]{1,0:T(8,128)(2,1)S(1)}, bf16[392,256]{1,0:T(8,128)(2,1)S(1)}, u32[]{:S(2)}, u32[]{:S(2)}) collective-permute-start(bf16[392,256]{1,0:T(8,128)(2,1)S(1)} %get-tuple-element.21.inn_ref), channel_id=1, source_target_pairs={{0,1},{1,0},{2,3},{3,2},{4,5},{5,4},{6,7},{7,6},{8,9},{9,8},{10,11... | collective-permute-start | bytes 602120 | tf_op jit(solution)/shard_map/ppermute | solution.py:390
  2.4 15.8 %collective-permute-start = (bf16[392,256]{1,0:T(8,128)(2,1)S(1)}, bf16[392,256]{1,0:T(8,128)(2,1)S(1)}, u32[]{:S(2)}, u32[]{:S(2)}) collective-permute-start(bf16[392,256]{1,0:T(8,128)(2,1)S(1)} %get-tuple-element.21.inn_ref), channel_id=1, source_target_pairs={{0,16},{16,0},{1,17},{17,1},{2,18},{18,2},{3,19},{19,3},{4,20},{20... | collective-permute-start | bytes 602120 | tf_op jit(solution)/shard_map/ppermute | solution.py:387
  4.0 10.1 %collective-permute-start.4 = (bf16[384,256]{1,0:T(8,128)(2,1)S(1)}, bf16[384,256]{1,0:T(8,128)(2,1)S(1)}, u32[]{:S(2)}, u32[]{:S(2)}) collective-permute-start(bf16[384,256]{1,0:T(8,128)(2,1)S(1)} %get-tuple-element.20.off_ref), channel_id=1, source_target_pairs={{2,17},{4,19},{6,21},{8,23},{10,25},{12,27},{14,29},{1,18},{3,20},... | collective-permute-start | bytes 589832 | tf_op jit(solution)/shard_map/ppermute | solution.py:415
  5.9 11.4 %collective-permute-start.2 = (bf16[384,256]{1,0:T(8,128)(2,1)S(1)}, bf16[384,256]{1,0:T(8,128)(2,1)S(1)}, u32[]{:S(2)}, u32[]{:S(2)}) collective-permute-start(bf16[384,256]{1,0:T(8,128)(2,1)S(1)} %get-tuple-element.20.off_ref), channel_id=1, source_target_pairs={{2,1},{4,3},{6,5},{8,7},{10,9},{12,11},{14,13},{1,2},{3,4},{5,6},{... | collective-permute-start | bytes 589832 | tf_op jit(solution)/shard_map/ppermute | solution.py:389
  9.5 8.7 %collective-permute-start.1 = (bf16[384,256]{1,0:T(8,128)(2,1)S(1)}, bf16[384,256]{1,0:T(8,128)(2,1)S(1)}, u32[]{:S(2)}, u32[]{:S(2)}) collective-permute-start(bf16[384,256]{1,0:T(8,128)(2,1)S(1)} %get-tuple-element.20.off_ref), channel_id=1, source_target_pairs={{0,16},{16,0},{1,17},{17,1},{2,18},{18,2},{3,19},{19,3},{4,20},{20... | collective-permute-start | bytes 589832 | tf_op jit(solution)/shard_map/ppermute | solution.py:388
  18.3 1.4 %collective-permute-start.5 = (bf16[392,256]{1,0:T(8,128)(2,1)S(1)}, bf16[392,256]{1,0:T(8,128)(2,1)S(1)}, u32[]{:S(2)}, u32[]{:S(2)}) collective-permute-start(bf16[392,256]{1,0:T(8,128)(2,1)S(1)} %collective-permute-done.other_inn_ref), channel_id=1, source_target_pairs={{0,1},{1,0},{2,3},{3,2},{4,5},{5,4},{6,7},{7,6},{8,9},{9,8},{10,11... | collective-permute-start | bytes 602120 | tf_op jit(solution)/shard_map/ppermute | solution.py:419
  19.7 6.2 %copy-start = (bf16[2,1024,1024]{2,1,0:T(8,128)(2,1)S(1)}, bf16[2,1024,1024]{2,1,0:T(8,128)(2,1)}, u32[]{:S(2)}) copy-start(bf16[2,1024,1024]{2,1,0:T(8,128)(2,1)} %policy_mid_ref.1) | copy-start | bytes 12582916
  19.7 6.2 %copy-start.1 = (bf16[512,1024]{1,0:T(8,128)(2,1)S(1)}, bf16[512,1024]{1,0:T(8,128)(2,1)}, u32[]{:S(2)}) copy-start(bf16[512,1024]{1,0:T(8,128)(2,1)} %policy_in_ref.1) | copy-start | bytes 3145732
  19.7 6.2 %copy-start.2 = (bf16[1024,128]{1,0:T(8,128)(2,1)S(1)}, bf16[1024,128]{1,0:T(8,128)(2,1)}, u32[]{:S(2)}) copy-start(bf16[1024,128]{1,0:T(8,128)(2,1)} %policy_out_ref.1) | copy-start | bytes 786436
  24.3 8.6 %collective-permute-start.6 = (bf16[384,256]{1,0:T(8,128)(2,1)S(1)}, bf16[384,256]{1,0:T(8,128)(2,1)S(1)}, u32[]{:S(2)}, u32[]{:S(2)}) collective-permute-start(bf16[384,256]{1,0:T(8,128)(2,1)S(1)} %get-tuple-element.37), channel_id=1, source_target_pairs={{0,16},{16,0},{1,17},{17,1},{2,18},{18,2},{3,19},{19,3},{4,20},{20... | collective-permute-start | bytes 589832 | tf_op jit(solution)/shard_map/ppermute | solution.py:457

commit v4 on v3

--- a/solution.py
+++ b/solution.py
@@ -156,6 +156,21 @@
     token_ref[...] = jnp.zeros_like(token_ref)
     for copy in copies:
         copy.wait()
+
+
+def others_kernel(place_ref, other_off_ref, other_inn_ref, other_rows_ref, pad_ref):
+    capacity = other_rows_ref.shape[0]
+    blocks, block_len, _ = pad_ref.shape
+    row_x = place_ref[0]
+    spread(pad_ref, 0, other_off_ref, blocks // 2)
+    spread(pad_ref, blocks // 2, other_inn_ref, blocks // 2)
+    pick = one_hot(
+        (row_x * 2 + 1 - row_x) * capacity,
+        capacity,
+        block_len,
+        sent_targets(other_inn_ref, 0, blocks),
+    )
+    other_rows_ref[...] = place(pick, pad_ref).astype(BF16)
 
 
 def attention_kernel(
@@ -260,10 +275,9 @@
     place_ref,
     off_ref,
     inn_ref,
-    other_off_ref,
-    other_inn_ref,
     summary_ref,
     own_rows_ref,
+    other_rows_ref,
     policy_in_ref,
     policy_mid_ref,
     policy_out_ref,
@@ -317,15 +331,7 @@
         (row_x * 2 + row_x) * capacity, capacity, block_len, sent_targets(inn_ref, 0, blocks)
     )
     batch_ref[mine, width:] = place(pick, pad_ref).astype(BF16)
-    spread(pad_ref, 0, other_off_ref, blocks // 2)
-    spread(pad_ref, blocks // 2, other_inn_ref, blocks // 2)
-    pick = one_hot(
-        (row_x * 2 + 1 - row_x) * capacity,
-        capacity,
-        block_len,
-        sent_targets(other_inn_ref, 0, blocks),
-    )
-    batch_ref[theirs, :width] = place(pick, pad_ref).astype(BF16)
+    batch_ref[theirs, :width] = other_rows_ref[...]
     batch_ref[theirs, width:] = jnp.zeros((capacity, width), BF16)
 
 
@@ -388,6 +394,7 @@
     other_off = lax.ppermute(off, "gx", swap)
     side_off = lax.ppermute(off, "gy", across)
     side_inn = lax.ppermute(inn, "gy", beside)
+    other_side_off = lax.ppermute(off, ("gx", "gy"), diagonal)
     attention_in, attention_out, own_rows, pick_out, table, token = pl.pallas_call(
         local_kernel,
         out_shape=(
@@ -412,11 +419,25 @@
         ),
         name="local",
     )(block_fill, neighbours, where, off, inn, *in_hbm(attention_in, attention_out))
-    other_side_off = lax.ppermute(off, ("gx", "gy"), diagonal)
-    other_inn, other_off, side_off, side_inn, other_side_off, token = lax.optimization_barrier(
-        (other_inn, other_off, side_off, side_inn, other_side_off, token)
+    token, other_side_off, side_inn, side_off, other_off, other_inn = lax.optimization_barrier(
+        (token, other_side_off, side_inn, side_off, other_off, other_inn)
     )
     other_side_inn = lax.ppermute(other_inn, "gy", beside)
+    other_rows = pl.pallas_call(
+        others_kernel,
+        out_shape=SDS((capacity, width), BF16),
+        in_specs=[SMEM, VMEM, VMEM],
+        out_specs=VMEM,
+        scratch_shapes=[pltpu.VMEM((all_blocks, block_len, width), BF16)],
+        compiler_params=pltpu.CompilerParams(vmem_limit_bytes=8 * MIB),
+        cost_estimate=pl.CostEstimate(
+            flops=2 * capacity * all_blocks * block_len * width,
+            bytes_accessed=2 * MIB,
+            transcendentals=0,
+        ),
+        name="others",
+    )(where, other_off, other_inn)
+    other_rows, other_side_inn = lax.optimization_barrier((other_rows, other_side_inn))
 
     window = blocks_x * owners * (blocks_y + 2 * REACH)
     scores = all_blocks * HEADS * LIVE * 5 * LIVE
@@ -461,7 +482,7 @@
             SDS((blocks_x, blocks_y, block_len, acts), BF16),
             SDS((rows, 2 * width), BF16),
         ),
-        in_specs=[SMEM] * 2 + [VMEM] * 9,
+        in_specs=[SMEM] * 2 + [VMEM] * 8,
         out_specs=(VMEM, VMEM),
         scratch_shapes=[
             pltpu.VMEM((slots, 2 * width), BF16),
@@ -481,10 +502,9 @@
         where,
         off,
         inn,
-        other_off,
-        other_inn,
         summary,
         own_rows,
+        other_rows,
         policy_in,
         policy_mid,
         policy_out,

time: 33.9 us -> 33.1 us (0.976)
  starting transfers between devices: 10.4 us -> 9.17 us
  Pallas kernels: 16.2 us -> 16.8 us
    ppermute x1, waiting for transfers between devices: 0.01 us -> 4.69 us  [on_device(): other_side_off = lax.ppermute(off, ('gx', 'gy'), diagonal)]
    ppermute x1, waiting for transfers between devices: 3.17 us -> 0.01 us  [on_device(): side_off = lax.ppermute(off, 'gy', across)]
    ppermute x1, starting transfers between devices: 1.91 us -> 4.47 us  [on_device(): other_side_off = lax.ppermute(off, ('gx', 'gy'), diagonal)]
    ppermute x1, starting transfers between devices: 3.58 us -> 2.04 us  [on_device(): side_off = lax.ppermute(off, 'gy', across)]
    ppermute x1, starting transfers between devices: 1.58 us -> 0.51 us  [on_device(): other_off = lax.ppermute(off, 'gx', swap)]
    ppermute x1, starting transfers between devices: 1.59 us -> 0.57 us  [on_device(): arrived = lax.ppermute(packed, 'gx', swap)]
    ppermute x1, waiting for transfers between devices: 0.95 us -> 0.01 us  [on_device(): other_off = lax.ppermute(off, 'gx', swap)]
    pallas_call x0 -> x1, Pallas kernels: none -> 0.91 us  [on_device(): pl.pallas_call(others_kernel, out_shape=SDS((capacity, width), BF16), in_...]
  transfers between devices with their start and end apart: 7 -> 7, of which waited for: 3 -> 2; matrix products, arithmetic and copies ran while one was open for 0% -> 0% of each run, Pallas kernels for 30% -> 32%
where the time goes in v4:
time: 33.1 us; the launch traced here: 32.6 us
  Pallas kernels  16.8 us (51%)
  starting transfers between devices  9.17 us (28%)
  waiting for transfers between devices  5.22 us (16%)
  between operations  0.72 us (2%)
  local copies, waits for them, and re-layouts  0.7 us (2%)
    pallas_call x1, Pallas kernels, on_device(): pl.pallas_call(policy_kernel, out_shape=(SDS((blocks_x, blocks_y, block_l...  6.6 us
    ppermute x1, waiting for transfers between devices, on_device(): other_side_off = lax.ppermute(off, ('gx', 'gy'), diagonal)  4.69 us
    pallas_call x1, Pallas kernels, on_device(): pl.pallas_call(attention_kernel, out_shape=(SDS((slots, width), BF16), SD...  4.6 us
    ppermute x1, starting transfers between devices, on_device(): other_side_off = lax.ppermute(off, ('gx', 'gy'), diagonal)  4.47 us
    pallas_call x1, Pallas kernels, on_device(): pl.pallas_call(local_kernel, out_shape=(SDS(attention_in.shape, BF16), SD...  3.01 us
    ppermute x1, starting transfers between devices, on_device(): side_off = lax.ppermute(off, 'gy', across)  2.04 us
    pallas_call x1, Pallas kernels, on_device(): pl.pallas_call(stage_kernel, out_shape=(SDS((half_rows, width), BF16), SD...  1.64 us
    ppermute x1, starting transfers between devices, on_device(): other_inn = lax.ppermute(inn, 'gx', swap)  1.58 us
  transfers between devices with their start and end apart: 7, of which 2 were waited for; matrix products, arithmetic and copies ran while one was open for 0% of the time, Pallas kernels for 32%

profile of v4, /device:TPU:2, one launch (start us, length us, event | category | flops | bytes accessed | tf_op | source)
XLA Modules:
  0.0 32.6 jit_solution(15316105138705041905)
XLA Ops:
  0.6 0.1 pad_add_fusion.place_ref
  0.7 1.6 %stage.1 = (bf16[384,256]{1,0:T(8,128)(2,1)S(1)}, bf16[392,256]{1,0:T(8,128)(2,1)S(1)}) custom-call(s32[2]{0:T(128)S(1)} %pad_add_fusion.place_ref, s32[2,4,128]{2,1,0:T(4,128)} %target_hbm.1, bf16[2,4,128,256]{3,2,1,0:T(8,128)(2,1)} %agents_hbm.1), custom_call_target="tpu_custom_call" | custom-call | tf_op jit(solution)/shard_map/stage/pallas_call | solution.py:381
  2.4 1.6 %collective-permute-start.4 = (bf16[392,256]{1,0:T(8,128)(2,1)S(1)}, bf16[392,256]{1,0:T(8,128)(2,1)S(1)}, u32[]{:S(2)}, u32[]{:S(2)}) collective-permute-start(bf16[392,256]{1,0:T(8,128)(2,1)S(1)} %get-tuple-element.23.inn_ref), channel_id=1, source_target_pairs={{0,16},{16,0},{1,17},{17,1},{2,18},{18,2},{3,19},{19,3},{4,20},{20... | collective-permute-start | bytes 602120 | tf_op jit(solution)/shard_map/ppermute | solution.py:393
  3.9 0.0 collective-permute-start.1
  3.9 0.5 %collective-permute-start.3 = (bf16[384,256]{1,0:T(8,128)(2,1)S(1)}, bf16[384,256]{1,0:T(8,128)(2,1)S(1)}, u32[]{:S(2)}, u32[]{:S(2)}) collective-permute-start(bf16[384,256]{1,0:T(8,128)(2,1)S(1)} %get-tuple-element.22.off_ref), channel_id=1, source_target_pairs={{0,16},{16,0},{1,17},{17,1},{2,18},{18,2},{3,19},{19,3},{4,20},{20... | collective-permute-start | bytes 589832 | tf_op jit(solution)/shard_map/ppermute | solution.py:394
  4.5 2.0 %collective-permute-start.2 = (bf16[384,256]{1,0:T(8,128)(2,1)S(1)}, bf16[384,256]{1,0:T(8,128)(2,1)S(1)}, u32[]{:S(2)}, u32[]{:S(2)}) collective-permute-start(bf16[384,256]{1,0:T(8,128)(2,1)S(1)} %get-tuple-element.22.off_ref), channel_id=1, source_target_pairs={{2,1},{4,3},{6,5},{8,7},{10,9},{12,11},{14,13},{1,2},{3,4},{5,6},{... | collective-permute-start | bytes 589832 | tf_op jit(solution)/shard_map/ppermute | solution.py:395
  6.5 4.5 %collective-permute-start = (bf16[384,256]{1,0:T(8,128)(2,1)S(1)}, bf16[384,256]{1,0:T(8,128)(2,1)S(1)}, u32[]{:S(2)}, u32[]{:S(2)}) collective-permute-start(bf16[384,256]{1,0:T(8,128)(2,1)S(1)} %get-tuple-element.22.off_ref), channel_id=1, source_target_pairs={{2,17},{4,19},{6,21},{8,23},{10,25},{12,27},{14,29},{1,18},{3,20},... | collective-permute-start | bytes 589832 | tf_op jit(solution)/shard_map/ppermute | solution.py:397
  11.0 3.0 %local.1 = (bf16[256,768]{1,0:T(8,128)(2,1)S(1)}, bf16[256,256]{1,0:T(8,128)(2,1)S(1)}, bf16[384,256]{1,0:T(8,128)(2,1)S(1)}, bf16[384,1024]{1,0:T(8,128)(2,1)S(...) custom-call(s32[4,64]{1,0:T(4,128)} %fill_ref.1, s32[2,4,4]{2,1,0:T(4,128)} %near_ref.1, s32[2]{0:T(128)S(1)} %pad_add_fusion.place_ref, ...), custom_call_target="tpu_custom_call" | custom-call | flops 201326592 | bytes 8388608 | tf_op jit(solution)/shard_map/local/pallas_call | solution.py:398
  14.0 0.0 collective-permute-done.3.other_off_ref
  14.0 0.0 collective-permute-done.2.side_off_ref
  14.0 4.7 %collective-permute-done.other_side_off_ref = bf16[384,256]{1,0:T(8,128)(2,1)S(1)} collective-permute-done((bf16[384,256]{1,0:T(8,128)(2,1)S(1)}, bf16[384,256]{1,0:T(8,128)(2,1)S(1)}, u32[]{:S(2)}, u32[]{:S(2)}) %collective-permute-start) | collective-permute-done | bytes 196640 | tf_op jit(solution)/shard_map/ppermute | solution.py:397
  18.7 0.0 collective-permute-done.4.other_inn_ref
  18.7 0.0 collective-permute-done.1.side_inn_ref
  18.7 0.0 collective-permute-start.5
  18.7 0.9 %others.1.other_rows_ref = bf16[384,256]{1,0:T(8,128)(2,1)S(1)} custom-call(s32[2]{0:T(128)S(1)} %pad_add_fusion.place_ref, bf16[384,256]{1,0:T(8,128)(2,1)S(1)} %collective-permute-done.3.other_off_ref, bf16[392,256]{1,0:T(8,128)(2,1)S(1)} %collective-permute-done.4.other_inn_ref), custom_call_target="tpu_custom_call" | custom-call | flops 201326592 | bytes 2097152 | tf_op jit(solution)/shard_map/others/pallas_call | solution.py:426
  19.6 0.5 %collective-permute-done.5.other_side_inn_ref = bf16[392,256]{1,0:T(8,128)(2,1)S(1)} collective-permute-done((bf16[392,256]{1,0:T(8,128)(2,1)S(1)}, bf16[392,256]{1,0:T(8,128)(2,1)S(1)}, u32[]{:S(2)}, u32[]{:S(2)}) %collective-permute-start.5) | collective-permute-done | bytes 200736 | tf_op jit(solution)/shard_map/ppermute | solution.py:425
  20.2 0.0 copy-start
  20.2 0.0 copy-start.1
  20.2 0.0 copy-start.2
  20.2 4.6 %attention.1 = (bf16[768,256]{1,0:T(8,128)(2,1)S(1)}, bf16[384,256]{1,0:T(8,128)(2,1)S(1)}) custom-call(s32[8,10]{1,0:T(8,128)S(1)} %get-tuple-element.24.table_ref, s32[2]{0:T(128)S(1)} %pad_add_fusion.place_ref, bf16[384,256]{1,0:T(8,128)(2,1)S(1)} %get-tuple-element.22.off_ref, bf16[392,256]{1,0:T(8,128)(2,1)S(1)} %get-tuple-element.23.inn_ref, ...), custom_call_target="tpu_custom_call" | custom-call | flops 2315255808 | bytes 8388608 | tf_op jit(solution)/shard_map/attention/pallas_call | solution.py:444
  24.8 0.6 %collective-permute-start.6 = (bf16[384,256]{1,0:T(8,128)(2,1)S(1)}, bf16[384,256]{1,0:T(8,128)(2,1)S(1)}, u32[]{:S(2)}, u32[]{:S(2)}) collective-permute-start(bf16[384,256]{1,0:T(8,128)(2,1)S(1)} %get-tuple-element.41), channel_id=1, source_target_pairs={{0,16},{16,0},{1,17},{17,1},{2,18},{18,2},{3,19},{19,3},{4,20},{20... | collective-permute-start | bytes 589832 | tf_op jit(solution)/shard_map/ppermute | solution.py:478
  25.4 0.0 copy-done
  25.4 0.0 copy-done.1
  25.4 0.0 copy-done.2
  25.4 6.6 %policy.1 = (bf16[2,4,128,128]{3,2,1,0:T(8,128)(2,1)}, bf16[768,512]{1,0:T(8,128)(2,1)}) custom-call(s32[8,10]{1,0:T(8,128)S(1)} %get-tuple-element.24.table_ref, s32[2]{0:T(128)S(1)} %pad_add_fusion.place_ref, bf16[384,256]{1,0:T(8,128)(2,1)S(1)} %get-tuple-element.22.off_ref, bf16[392,256]{1,0:T(8,128)(2,1)S(1)} %get-tuple-element.23.inn_ref, ...), custom_call_target="tpu_custom_call" | custom-call | flops 4227858432 | bytes 12582912 | tf_op jit(solution)/shard_map/policy/pallas_call | solution.py:479
  32.0 0.0 collective-permute-done.6
  32.0 0.7 %bitcast_dynamic-update-slice_fusion = bf16[1,1,768,512]{3,2,1,0:T(8,128)(2,1)} fusion(bf16[1,1,768,512]{3,2,1,0:T(8,128)(2,1)} %bitcast.5, s32[]{:T(128)S(6)} %select_n.3, bf16[384,256]{1,0:T(8,128)(2,1)S(1)} %collective-permute-done.6), kind=kLoop, calls=%fused_computation | loop fusion | bytes 393220 | tf_op jit(solution)/shard_map/dynamic_update_slice | solution.py:512
Async XLA Ops:
  2.4 16.4 %collective-permute-start.4 = (bf16[392,256]{1,0:T(8,128)(2,1)S(1)}, bf16[392,256]{1,0:T(8,128)(2,1)S(1)}, u32[]{:S(2)}, u32[]{:S(2)}) collective-permute-start(bf16[392,256]{1,0:T(8,128)(2,1)S(1)} %get-tuple-element.23.inn_ref), channel_id=1, source_target_pairs={{0,16},{16,0},{1,17},{17,1},{2,18},{18,2},{3,19},{19,3},{4,20},{20... | collective-permute-start | bytes 602120 | tf_op jit(solution)/shard_map/ppermute | solution.py:393
  3.9 14.8 %collective-permute-start.1 = (bf16[392,256]{1,0:T(8,128)(2,1)S(1)}, bf16[392,256]{1,0:T(8,128)(2,1)S(1)}, u32[]{:S(2)}, u32[]{:S(2)}) collective-permute-start(bf16[392,256]{1,0:T(8,128)(2,1)S(1)} %get-tuple-element.23.inn_ref), channel_id=1, source_target_pairs={{0,1},{1,0},{2,3},{3,2},{4,5},{5,4},{6,7},{7,6},{8,9},{9,8},{10,11... | collective-permute-start | bytes 602120 | tf_op jit(solution)/shard_map/ppermute | solution.py:396
  3.9 10.1 %collective-permute-start.3 = (bf16[384,256]{1,0:T(8,128)(2,1)S(1)}, bf16[384,256]{1,0:T(8,128)(2,1)S(1)}, u32[]{:S(2)}, u32[]{:S(2)}) collective-permute-start(bf16[384,256]{1,0:T(8,128)(2,1)S(1)} %get-tuple-element.22.off_ref), channel_id=1, source_target_pairs={{0,16},{16,0},{1,17},{17,1},{2,18},{18,2},{3,19},{19,3},{4,20},{20... | collective-permute-start | bytes 589832 | tf_op jit(solution)/shard_map/ppermute | solution.py:394
  4.5 9.6 %collective-permute-start.2 = (bf16[384,256]{1,0:T(8,128)(2,1)S(1)}, bf16[384,256]{1,0:T(8,128)(2,1)S(1)}, u32[]{:S(2)}, u32[]{:S(2)}) collective-permute-start(bf16[384,256]{1,0:T(8,128)(2,1)S(1)} %get-tuple-element.22.off_ref), channel_id=1, source_target_pairs={{2,1},{4,3},{6,5},{8,7},{10,9},{12,11},{14,13},{1,2},{3,4},{5,6},{... | collective-permute-start | bytes 589832 | tf_op jit(solution)/shard_map/ppermute | solution.py:395
  6.5 12.2 %collective-permute-start = (bf16[384,256]{1,0:T(8,128)(2,1)S(1)}, bf16[384,256]{1,0:T(8,128)(2,1)S(1)}, u32[]{:S(2)}, u32[]{:S(2)}) collective-permute-start(bf16[384,256]{1,0:T(8,128)(2,1)S(1)} %get-tuple-element.22.off_ref), channel_id=1, source_target_pairs={{2,17},{4,19},{6,21},{8,23},{10,25},{12,27},{14,29},{1,18},{3,20},... | collective-permute-start | bytes 589832 | tf_op jit(solution)/shard_map/ppermute | solution.py:397
  18.7 1.4 %collective-permute-start.5 = (bf16[392,256]{1,0:T(8,128)(2,1)S(1)}, bf16[392,256]{1,0:T(8,128)(2,1)S(1)}, u32[]{:S(2)}, u32[]{:S(2)}) collective-permute-start(bf16[392,256]{1,0:T(8,128)(2,1)S(1)} %collective-permute-done.4.other_inn_ref), channel_id=1, source_target_pairs={{0,1},{1,0},{2,3},{3,2},{4,5},{5,4},{6,7},{7,6},{8,9},{9,8},{10,11... | collective-permute-start | bytes 602120 | tf_op jit(solution)/shard_map/ppermute | solution.py:425
  20.2 5.2 %copy-start = (bf16[2,1024,1024]{2,1,0:T(8,128)(2,1)S(1)}, bf16[2,1024,1024]{2,1,0:T(8,128)(2,1)}, u32[]{:S(2)}) copy-start(bf16[2,1024,1024]{2,1,0:T(8,128)(2,1)} %policy_mid_ref.1) | copy-start | bytes 12582916
  20.2 5.2 %copy-start.1 = (bf16[512,1024]{1,0:T(8,128)(2,1)S(1)}, bf16[512,1024]{1,0:T(8,128)(2,1)}, u32[]{:S(2)}) copy-start(bf16[512,1024]{1,0:T(8,128)(2,1)} %policy_in_ref.1) | copy-start | bytes 3145732
  20.2 5.2 %copy-start.2 = (bf16[1024,128]{1,0:T(8,128)(2,1)S(1)}, bf16[1024,128]{1,0:T(8,128)(2,1)}, u32[]{:S(2)}) copy-start(bf16[1024,128]{1,0:T(8,128)(2,1)} %policy_out_ref.1) | copy-start | bytes 786436
  24.8 7.2 %collective-permute-start.6 = (bf16[384,256]{1,0:T(8,128)(2,1)S(1)}, bf16[384,256]{1,0:T(8,128)(2,1)S(1)}, u32[]{:S(2)}, u32[]{:S(2)}) collective-permute-start(bf16[384,256]{1,0:T(8,128)(2,1)S(1)} %get-tuple-element.41), channel_id=1, source_target_pairs={{0,16},{16,0},{1,17},{17,1},{2,18},{18,2},{3,19},{19,3},{4,20},{20... | collective-permute-start | bytes 589832 | tf_op jit(solution)/shard_map/ppermute | solution.py:478

commit v5 on v4

--- a/solution.py
+++ b/solution.py
@@ -79,9 +79,9 @@
         pad_ref[first + b, LIVE:] = jnp.zeros((block_len - LIVE, width), pad_ref.dtype)
 
 
-def stage_kernel(place_ref, target_hbm, agents_hbm, off_ref, inn_ref, target_ref, sems):
+def stage_kernel(target_hbm, agents_hbm, off_ref, inn_ref, target_ref, sems):
     blocks_x, _, _, _ = agents_hbm.shape
-    core = place_ref[1] & 1
+    core = lax.axis_index("gy") & 1
     rows = REACH * LIVE
     targets = pltpu.make_async_copy(target_hbm, target_ref, sems.at[2, 0])
     targets.start()
@@ -115,7 +115,6 @@
 def local_kernel(
     fill_ref,
     near_ref,
-    place_ref,
     off_ref,
     inn_ref,
     weight_in_hbm,
@@ -137,9 +136,9 @@
         copy.start()
     capacity = own_rows_ref.shape[0]
     blocks, block_len, _ = pad_ref.shape
-    row_x = place_ref[0]
-    core = place_ref[1] & 1
-    place_of = (row_x, place_ref[1], blocks // (2 * REACH), 2 * REACH)
+    row_x = lax.axis_index("gx")
+    core = lax.axis_index("gy") & 1
+    place_of = (row_x, lax.axis_index("gy"), blocks // (2 * REACH), 2 * REACH)
     for half, first in enumerate((core * REACH, REACH - core * REACH)):
         for i in range(blocks // 2):
             b = half * (blocks // 2) + i
@@ -158,10 +157,10 @@
         copy.wait()
 
 
-def others_kernel(place_ref, other_off_ref, other_inn_ref, other_rows_ref, pad_ref):
+def others_kernel(other_off_ref, other_inn_ref, other_rows_ref, pad_ref):
     capacity = other_rows_ref.shape[0]
     blocks, block_len, _ = pad_ref.shape
-    row_x = place_ref[0]
+    row_x = lax.axis_index("gx")
     spread(pad_ref, 0, other_off_ref, blocks // 2)
     spread(pad_ref, blocks // 2, other_inn_ref, blocks // 2)
     pick = one_hot(
@@ -175,7 +174,6 @@
 
 def attention_kernel(
     table_ref,
-    place_ref,
     off_ref,
     inn_ref,
     other_off_ref,
@@ -201,7 +199,7 @@
     each = half_rows // LIVE
     blocks_x = each // REACH
     columns = 4 * REACH
-    core = place_ref[1] & 1
+    core = lax.axis_index("gy") & 1
     at_off = REACH + REACH * core
     at_inn = 2 * REACH - REACH * core
     at_side_off = 3 * REACH * core
@@ -272,7 +270,6 @@
 
 def policy_kernel(
     table_ref,
-    place_ref,
     off_ref,
     inn_ref,
     summary_ref,
@@ -290,8 +287,8 @@
 ):
     width = off_ref.shape[1]
     blocks_x, blocks_y, block_len, _ = actions_ref.shape
-    row_x = place_ref[0]
-    core = place_ref[1] & 1
+    row_x = lax.axis_index("gx")
+    core = lax.axis_index("gy") & 1
     capacity = batch_ref.shape[0] // 2
     half_rows = off_ref.shape[0]
     x_ref[:half_rows, :width] = off_ref[...]
@@ -368,7 +365,6 @@
     half_rows = slots // 2
     rows = owners * capacity
     block_fill, neighbours = in_hbm(block_fill, neighbours)
-    where = jnp.stack([row_x, lax.axis_index("gy")]).astype(jnp.int32)
 
     swap = [(0, 1), (1, 0)]
     across = [(i, i - 1) for i in range(2, count_y, 2)]
@@ -381,7 +377,7 @@
     off, inn = pl.pallas_call(
         stage_kernel,
         out_shape=(SDS((half_rows, width), BF16), SDS((half_rows + TARGET_ROWS, width), BF16)),
-        in_specs=[SMEM, HBM, HBM],
+        in_specs=[HBM, HBM],
         out_specs=(VMEM, VMEM),
         scratch_shapes=[
             pltpu.VMEM((blocks_x, blocks_y, block_len), jnp.int32),
@@ -389,7 +385,7 @@
         ],
         compiler_params=pltpu.CompilerParams(vmem_limit_bytes=4 * MIB),
         name="stage",
-    )(where, *in_hbm(target_slot, agents))
+    )(*in_hbm(target_slot, agents))
     other_inn = lax.ppermute(inn, "gx", swap)
     other_off = lax.ppermute(off, "gx", swap)
     side_off = lax.ppermute(off, "gy", across)
@@ -405,7 +401,7 @@
             SDS((all_blocks, 2 * neighbours.shape[2] + 2), jnp.int32),
             SDS((8, 128), F32),
         ),
-        in_specs=[SMEM] * 3 + [VMEM] * 2 + [HBM] * 2,
+        in_specs=[SMEM] * 2 + [VMEM] * 2 + [HBM] * 2,
         out_specs=(VMEM,) * 4 + (SMEM, VMEM),
         scratch_shapes=[
             pltpu.VMEM((all_blocks, block_len, width), BF16),
@@ -418,15 +414,15 @@
             transcendentals=0,
         ),
         name="local",
-    )(block_fill, neighbours, where, off, inn, *in_hbm(attention_in, attention_out))
-    token, other_side_off, side_inn, side_off, other_off, other_inn = lax.optimization_barrier(
-        (token, other_side_off, side_inn, side_off, other_off, other_inn)
+    )(block_fill, neighbours, off, inn, *in_hbm(attention_in, attention_out))
+    other_inn, other_off, side_off, side_inn, other_side_off, token = lax.optimization_barrier(
+        (other_inn, other_off, side_off, side_inn, other_side_off, token)
     )
     other_side_inn = lax.ppermute(other_inn, "gy", beside)
     other_rows = pl.pallas_call(
         others_kernel,
         out_shape=SDS((capacity, width), BF16),
-        in_specs=[SMEM, VMEM, VMEM],
+        in_specs=[VMEM, VMEM],
         out_specs=VMEM,
         scratch_shapes=[pltpu.VMEM((all_blocks, block_len, width), BF16)],
         compiler_params=pltpu.CompilerParams(vmem_limit_bytes=8 * MIB),
@@ -436,7 +432,7 @@
             transcendentals=0,
         ),
         name="others",
-    )(where, other_off, other_inn)
+    )(other_off, other_inn)
     other_rows, other_side_inn = lax.optimization_barrier((other_rows, other_side_inn))
 
     window = blocks_x * owners * (blocks_y + 2 * REACH)
@@ -444,7 +440,7 @@
     summary, packed = pl.pallas_call(
         attention_kernel,
         out_shape=(SDS((slots, width), BF16), SDS((capacity, width), BF16)),
-        in_specs=[SMEM] * 2 + [VMEM] * 12,
+        in_specs=[SMEM] + [VMEM] * 12,
         out_specs=(VMEM, VMEM),
         scratch_shapes=[
             pltpu.VMEM((window, LIVE, width), BF16),
@@ -461,7 +457,6 @@
         name="attention",
     )(
         table,
-        where,
         off,
         inn,
         other_off,
@@ -482,7 +477,7 @@
             SDS((blocks_x, blocks_y, block_len, acts), BF16),
             SDS((rows, 2 * width), BF16),
         ),
-        in_specs=[SMEM] * 2 + [VMEM] * 8,
+        in_specs=[SMEM] + [VMEM] * 8,
         out_specs=(VMEM, VMEM),
         scratch_shapes=[
             pltpu.VMEM((slots, 2 * width), BF16),
@@ -499,7 +494,6 @@
         name="policy",
     )(
         table,
-        where,
         off,
         inn,
         summary,

time: 33.1 us -> 32.5 us (0.982)
  Pallas kernels: 16.8 us -> 15.7 us
  waiting for transfers between devices: 5.22 us -> 5.76 us
    pallas_call x1, Pallas kernels: 0.91 us -> 0.37 us  [on_device(): pl.pallas_call(others_kernel, out_shape=SDS((capacity, width), BF16), in_...]
    ppermute x1, waiting for transfers between devices: 0.52 us -> 1.06 us  [on_device(): other_side_inn = lax.ppermute(other_inn, 'gy', beside)]
    pallas_call x1, Pallas kernels: 1.64 us -> 1.1 us  [on_device(): pl.pallas_call(stage_kernel, out_shape=(SDS((half_rows, width), BF16), SD...]
  transfers between devices with their start and end apart: 7 -> 7, of which waited for: 2 -> 2; matrix products, arithmetic and copies ran while one was open for 0% -> 0% of each run, Pallas kernels for 32% -> 31%
where the time goes in v5:
time: 32.5 us; the launch traced here: 32 us
  Pallas kernels  15.7 us (48%)
  starting transfers between devices  9.17 us (28%)
  waiting for transfers between devices  5.76 us (18%)
  between operations  0.71 us (2%)
  local copies, waits for them, and re-layouts  0.7 us (2%)
    pallas_call x1, Pallas kernels, on_device(): pl.pallas_call(policy_kernel, out_shape=(SDS((blocks_x, blocks_y, block_l...  6.58 us
    ppermute x1, waiting for transfers between devices, on_device(): other_side_off = lax.ppermute(off, ('gx', 'gy'), diagonal)  4.69 us
    pallas_call x1, Pallas kernels, on_device(): pl.pallas_call(attention_kernel, out_shape=(SDS((slots, width), BF16), SD...  4.6 us
    ppermute x1, starting transfers between devices, on_device(): other_side_off = lax.ppermute(off, ('gx', 'gy'), diagonal)  4.47 us
    pallas_call x1, Pallas kernels, on_device(): pl.pallas_call(local_kernel, out_shape=(SDS(attention_in.shape, BF16), SD...  3.01 us
    ppermute x1, starting transfers between devices, on_device(): side_off = lax.ppermute(off, 'gy', across)  2.04 us
    ppermute x1, starting transfers between devices, on_device(): other_inn = lax.ppermute(inn, 'gx', swap)  1.58 us
    pallas_call x1, Pallas kernels, on_device(): pl.pallas_call(stage_kernel, out_shape=(SDS((half_rows, width), BF16), SD...  1.1 us
  transfers between devices with their start and end apart: 7, of which 2 were waited for; matrix products, arithmetic and copies ran while one was open for 0% of the time, Pallas kernels for 31%

profile of v5, /device:TPU:2, one launch (start us, length us, event | category | flops | bytes accessed | tf_op | source)
XLA Modules:
  0.0 32.0 jit_solution(16485454978236764962)
XLA Ops:
  0.6 1.1 %stage.1 = (bf16[384,256]{1,0:T(8,128)(2,1)S(1)}, bf16[392,256]{1,0:T(8,128)(2,1)S(1)}) custom-call(s32[2,4,128]{2,1,0:T(4,128)} %target_hbm.1, bf16[2,4,128,256]{3,2,1,0:T(8,128)(2,1)} %agents_hbm.1), custom_call_target="tpu_custom_call" | custom-call | tf_op jit(solution)/shard_map/stage/pallas_call | solution.py:377
  1.7 1.6 %collective-permute-start = (bf16[392,256]{1,0:T(8,128)(2,1)S(1)}, bf16[392,256]{1,0:T(8,128)(2,1)S(1)}, u32[]{:S(2)}, u32[]{:S(2)}) collective-permute-start(bf16[392,256]{1,0:T(8,128)(2,1)S(1)} %get-tuple-element.23.inn_ref), channel_id=1, source_target_pairs={{0,16},{16,0},{1,17},{17,1},{2,18},{18,2},{3,19},{19,3},{4,20},{20... | collective-permute-start | bytes 602120 | tf_op jit(solution)/shard_map/ppermute | solution.py:389
  3.3 0.0 collective-permute-start.3
  3.3 0.5 %collective-permute-start.1 = (bf16[384,256]{1,0:T(8,128)(2,1)S(1)}, bf16[384,256]{1,0:T(8,128)(2,1)S(1)}, u32[]{:S(2)}, u32[]{:S(2)}) collective-permute-start(bf16[384,256]{1,0:T(8,128)(2,1)S(1)} %get-tuple-element.22.off_ref), channel_id=1, source_target_pairs={{0,16},{16,0},{1,17},{17,1},{2,18},{18,2},{3,19},{19,3},{4,20},{20... | collective-permute-start | bytes 589832 | tf_op jit(solution)/shard_map/ppermute | solution.py:390
  3.8 2.0 %collective-permute-start.2 = (bf16[384,256]{1,0:T(8,128)(2,1)S(1)}, bf16[384,256]{1,0:T(8,128)(2,1)S(1)}, u32[]{:S(2)}, u32[]{:S(2)}) collective-permute-start(bf16[384,256]{1,0:T(8,128)(2,1)S(1)} %get-tuple-element.22.off_ref), channel_id=1, source_target_pairs={{2,1},{4,3},{6,5},{8,7},{10,9},{12,11},{14,13},{1,2},{3,4},{5,6},{... | collective-permute-start | bytes 589832 | tf_op jit(solution)/shard_map/ppermute | solution.py:391
  5.9 4.5 %collective-permute-start.4 = (bf16[384,256]{1,0:T(8,128)(2,1)S(1)}, bf16[384,256]{1,0:T(8,128)(2,1)S(1)}, u32[]{:S(2)}, u32[]{:S(2)}) collective-permute-start(bf16[384,256]{1,0:T(8,128)(2,1)S(1)} %get-tuple-element.22.off_ref), channel_id=1, source_target_pairs={{2,17},{4,19},{6,21},{8,23},{10,25},{12,27},{14,29},{1,18},{3,20},... | collective-permute-start | bytes 589832 | tf_op jit(solution)/shard_map/ppermute | solution.py:393
  10.4 3.0 %local.1 = (bf16[256,768]{1,0:T(8,128)(2,1)S(1)}, bf16[256,256]{1,0:T(8,128)(2,1)S(1)}, bf16[384,256]{1,0:T(8,128)(2,1)S(1)}, bf16[384,1024]{1,0:T(8,128)(2,1)S(...) custom-call(s32[4,64]{1,0:T(4,128)} %fill_ref.1, s32[2,4,4]{2,1,0:T(4,128)} %near_ref.1, ...), custom_call_target="tpu_custom_call" | custom-call | flops 201326592 | bytes 8388608 | tf_op jit(solution)/shard_map/local/pallas_call | solution.py:394
  13.4 0.0 collective-permute-done.1.other_off_ref
  13.4 0.0 collective-permute-done.2.side_off_ref
  13.4 4.7 %collective-permute-done.4.other_side_off_ref = bf16[384,256]{1,0:T(8,128)(2,1)S(1)} collective-permute-done((bf16[384,256]{1,0:T(8,128)(2,1)S(1)}, bf16[384,256]{1,0:T(8,128)(2,1)S(1)}, u32[]{:S(2)}, u32[]{:S(2)}) %collective-permute-start.4) | collective-permute-done | bytes 196640 | tf_op jit(solution)/shard_map/ppermute | solution.py:393
  18.1 0.0 collective-permute-done.other_inn_ref
  18.1 0.0 collective-permute-done.3.side_inn_ref
  18.1 0.0 collective-permute-start.5
  18.1 0.4 %others.1.other_rows_ref = bf16[384,256]{1,0:T(8,128)(2,1)S(1)} custom-call(bf16[384,256]{1,0:T(8,128)(2,1)S(1)} %collective-permute-done.1.other_off_ref, bf16[392,256]{1,0:T(8,128)(2,1)S(1)} %collective-permute-done.other_inn_ref), custom_call_target="tpu_custom_call" | custom-call | flops 201326592 | bytes 2097152 | tf_op jit(solution)/shard_map/others/pallas_call | solution.py:422
  18.5 1.1 %collective-permute-done.5.other_side_inn_ref = bf16[392,256]{1,0:T(8,128)(2,1)S(1)} collective-permute-done((bf16[392,256]{1,0:T(8,128)(2,1)S(1)}, bf16[392,256]{1,0:T(8,128)(2,1)S(1)}, u32[]{:S(2)}, u32[]{:S(2)}) %collective-permute-start.5) | collective-permute-done | bytes 200736 | tf_op jit(solution)/shard_map/ppermute | solution.py:421
  19.5 0.0 copy-start
  19.5 0.0 copy-start.1
  19.6 0.0 copy-start.2
  19.6 4.6 %attention.1 = (bf16[768,256]{1,0:T(8,128)(2,1)S(1)}, bf16[384,256]{1,0:T(8,128)(2,1)S(1)}) custom-call(s32[8,10]{1,0:T(8,128)S(1)} %get-tuple-element.24.table_ref, bf16[384,256]{1,0:T(8,128)(2,1)S(1)} %get-tuple-element.22.off_ref, bf16[392,256]{1,0:T(8,128)(2,1)S(1)} %get-tuple-element.23.inn_ref, ...), custom_call_target="tpu_custom_call" | custom-call | flops 2315255808 | bytes 8388608 | tf_op jit(solution)/shard_map/attention/pallas_call | solution.py:440
  24.2 0.6 %collective-permute-start.6 = (bf16[384,256]{1,0:T(8,128)(2,1)S(1)}, bf16[384,256]{1,0:T(8,128)(2,1)S(1)}, u32[]{:S(2)}, u32[]{:S(2)}) collective-permute-start(bf16[384,256]{1,0:T(8,128)(2,1)S(1)} %get-tuple-element.41), channel_id=1, source_target_pairs={{0,16},{16,0},{1,17},{17,1},{2,18},{18,2},{3,19},{19,3},{4,20},{20... | collective-permute-start | bytes 589832 | tf_op jit(solution)/shard_map/ppermute | solution.py:473
  24.7 0.0 copy-done
  24.7 0.0 copy-done.1
  24.7 0.0 copy-done.2
  24.7 6.6 %policy.1 = (bf16[2,4,128,128]{3,2,1,0:T(8,128)(2,1)}, bf16[768,512]{1,0:T(8,128)(2,1)}) custom-call(s32[8,10]{1,0:T(8,128)S(1)} %get-tuple-element.24.table_ref, bf16[384,256]{1,0:T(8,128)(2,1)S(1)} %get-tuple-element.22.off_ref, bf16[392,256]{1,0:T(8,128)(2,1)S(1)} %get-tuple-element.23.inn_ref, bf16[768,256]{1,0:T(8,128)(2,1)S(1)} %get-tuple-element.36.summary_ref, ...), custom_call_target="tpu_custom_call" | custom-call | flops 4227858432 | bytes 12582912 | tf_op jit(solution)/shard_map/policy/pallas_call | solution.py:474
  31.3 0.0 collective-permute-done.6
  31.3 0.7 %bitcast_dynamic-update-slice_fusion = bf16[1,1,768,512]{3,2,1,0:T(8,128)(2,1)} fusion(bf16[1,1,768,512]{3,2,1,0:T(8,128)(2,1)} %bitcast.3, s32[]{:T(128)S(6)} %select_n.3, bf16[384,256]{1,0:T(8,128)(2,1)S(1)} %collective-permute-done.6), kind=kLoop, calls=%fused_computation | loop fusion | bytes 393220 | tf_op jit(solution)/shard_map/dynamic_update_slice | solution.py:506
Async XLA Ops:
  1.7 16.4 %collective-permute-start = (bf16[392,256]{1,0:T(8,128)(2,1)S(1)}, bf16[392,256]{1,0:T(8,128)(2,1)S(1)}, u32[]{:S(2)}, u32[]{:S(2)}) collective-permute-start(bf16[392,256]{1,0:T(8,128)(2,1)S(1)} %get-tuple-element.23.inn_ref), channel_id=1, source_target_pairs={{0,16},{16,0},{1,17},{17,1},{2,18},{18,2},{3,19},{19,3},{4,20},{20... | collective-permute-start | bytes 602120 | tf_op jit(solution)/shard_map/ppermute | solution.py:389
  3.3 14.8 %collective-permute-start.3 = (bf16[392,256]{1,0:T(8,128)(2,1)S(1)}, bf16[392,256]{1,0:T(8,128)(2,1)S(1)}, u32[]{:S(2)}, u32[]{:S(2)}) collective-permute-start(bf16[392,256]{1,0:T(8,128)(2,1)S(1)} %get-tuple-element.23.inn_ref), channel_id=1, source_target_pairs={{0,1},{1,0},{2,3},{3,2},{4,5},{5,4},{6,7},{7,6},{8,9},{9,8},{10,11... | collective-permute-start | bytes 602120 | tf_op jit(solution)/shard_map/ppermute | solution.py:392
  3.3 10.1 %collective-permute-start.1 = (bf16[384,256]{1,0:T(8,128)(2,1)S(1)}, bf16[384,256]{1,0:T(8,128)(2,1)S(1)}, u32[]{:S(2)}, u32[]{:S(2)}) collective-permute-start(bf16[384,256]{1,0:T(8,128)(2,1)S(1)} %get-tuple-element.22.off_ref), channel_id=1, source_target_pairs={{0,16},{16,0},{1,17},{17,1},{2,18},{18,2},{3,19},{19,3},{4,20},{20... | collective-permute-start | bytes 589832 | tf_op jit(solution)/shard_map/ppermute | solution.py:390
  3.8 9.6 %collective-permute-start.2 = (bf16[384,256]{1,0:T(8,128)(2,1)S(1)}, bf16[384,256]{1,0:T(8,128)(2,1)S(1)}, u32[]{:S(2)}, u32[]{:S(2)}) collective-permute-start(bf16[384,256]{1,0:T(8,128)(2,1)S(1)} %get-tuple-element.22.off_ref), channel_id=1, source_target_pairs={{2,1},{4,3},{6,5},{8,7},{10,9},{12,11},{14,13},{1,2},{3,4},{5,6},{... | collective-permute-start | bytes 589832 | tf_op jit(solution)/shard_map/ppermute | solution.py:391
  5.9 12.2 %collective-permute-start.4 = (bf16[384,256]{1,0:T(8,128)(2,1)S(1)}, bf16[384,256]{1,0:T(8,128)(2,1)S(1)}, u32[]{:S(2)}, u32[]{:S(2)}) collective-permute-start(bf16[384,256]{1,0:T(8,128)(2,1)S(1)} %get-tuple-element.22.off_ref), channel_id=1, source_target_pairs={{2,17},{4,19},{6,21},{8,23},{10,25},{12,27},{14,29},{1,18},{3,20},... | collective-permute-start | bytes 589832 | tf_op jit(solution)/shard_map/ppermute | solution.py:393
  18.1 1.4 %collective-permute-start.5 = (bf16[392,256]{1,0:T(8,128)(2,1)S(1)}, bf16[392,256]{1,0:T(8,128)(2,1)S(1)}, u32[]{:S(2)}, u32[]{:S(2)}) collective-permute-start(bf16[392,256]{1,0:T(8,128)(2,1)S(1)} %collective-permute-done.other_inn_ref), channel_id=1, source_target_pairs={{0,1},{1,0},{2,3},{3,2},{4,5},{5,4},{6,7},{7,6},{8,9},{9,8},{10,11... | collective-permute-start | bytes 602120 | tf_op jit(solution)/shard_map/ppermute | solution.py:421
  19.5 5.2 %copy-start = (bf16[2,1024,1024]{2,1,0:T(8,128)(2,1)S(1)}, bf16[2,1024,1024]{2,1,0:T(8,128)(2,1)}, u32[]{:S(2)}) copy-start(bf16[2,1024,1024]{2,1,0:T(8,128)(2,1)} %policy_mid_ref.1) | copy-start | bytes 12582916
  19.5 5.2 %copy-start.1 = (bf16[512,1024]{1,0:T(8,128)(2,1)S(1)}, bf16[512,1024]{1,0:T(8,128)(2,1)}, u32[]{:S(2)}) copy-start(bf16[512,1024]{1,0:T(8,128)(2,1)} %policy_in_ref.1) | copy-start | bytes 3145732
  19.6 5.2 %copy-start.2 = (bf16[1024,128]{1,0:T(8,128)(2,1)S(1)}, bf16[1024,128]{1,0:T(8,128)(2,1)}, u32[]{:S(2)}) copy-start(bf16[1024,128]{1,0:T(8,128)(2,1)} %policy_out_ref.1) | copy-start | bytes 786436
  24.2 7.2 %collective-permute-start.6 = (bf16[384,256]{1,0:T(8,128)(2,1)S(1)}, bf16[384,256]{1,0:T(8,128)(2,1)S(1)}, u32[]{:S(2)}, u32[]{:S(2)}) collective-permute-start(bf16[384,256]{1,0:T(8,128)(2,1)S(1)} %get-tuple-element.41), channel_id=1, source_target_pairs={{0,16},{16,0},{1,17},{17,1},{2,18},{18,2},{3,19},{19,3},{4,20},{20... | collective-permute-start | bytes 589832 | tf_op jit(solution)/shard_map/ppermute | solution.py:473

commit v6 on v5

--- a/solution.py
+++ b/solution.py
@@ -415,8 +415,8 @@
         ),
         name="local",
     )(block_fill, neighbours, off, inn, *in_hbm(attention_in, attention_out))
-    other_inn, other_off, side_off, side_inn, other_side_off, token = lax.optimization_barrier(
-        (other_inn, other_off, side_off, side_inn, other_side_off, token)
+    other_inn, side_off, other_off, side_inn, other_side_off, token = lax.optimization_barrier(
+        (other_inn, side_off, other_off, side_inn, other_side_off, token)
     )
     other_side_inn = lax.ppermute(other_inn, "gy", beside)
     other_rows = pl.pallas_call(

time: 32.5 us -> 32.2 us (level)
    ppermute x1, waiting for transfers between devices: 0.01 us -> 4.72 us  [on_device(): other_off = lax.ppermute(off, 'gx', swap)]
    ppermute x1, waiting for transfers between devices: 4.69 us -> 0.01 us  [on_device(): other_side_off = lax.ppermute(off, ('gx', 'gy'), diagonal)]
    ppermute x1, starting transfers between devices: 2.04 us -> 2.54 us  [on_device(): side_off = lax.ppermute(off, 'gy', across)]
    ppermute x1, starting transfers between devices: 4.47 us -> 4.1 us  [on_device(): other_side_off = lax.ppermute(off, ('gx', 'gy'), diagonal)]
    ppermute x1, starting transfers between devices: 0.51 us -> 0.14 us  [on_device(): other_off = lax.ppermute(off, 'gx', swap)]
where the time goes in v6:
time: 32.2 us; the launch traced here: 31.9 us
  Pallas kernels  15.7 us (49%)
  starting transfers between devices  9.14 us (28%)
  waiting for transfers between devices  5.69 us (18%)
  local copies, waits for them, and re-layouts  0.7 us (2%)
  between operations  0.7 us (2%)
    pallas_call x1, Pallas kernels, on_device(): pl.pallas_call(policy_kernel, out_shape=(SDS((blocks_x, blocks_y, block_l...  6.58 us
    ppermute x1, waiting for transfers between devices, on_device(): other_off = lax.ppermute(off, 'gx', swap)  4.72 us
    pallas_call x1, Pallas kernels, on_device(): pl.pallas_call(attention_kernel, out_shape=(SDS((slots, width), BF16), SD...  4.6 us
    ppermute x1, starting transfers between devices, on_device(): other_side_off = lax.ppermute(off, ('gx', 'gy'), diagonal)  4.1 us
    pallas_call x1, Pallas kernels, on_device(): pl.pallas_call(local_kernel, out_shape=(SDS(attention_in.shape, BF16), SD...  3.01 us
    ppermute x1, starting transfers between devices, on_device(): side_off = lax.ppermute(off, 'gy', across)  2.54 us
    ppermute x1, starting transfers between devices, on_device(): other_inn = lax.ppermute(inn, 'gx', swap)  1.58 us
    pallas_call x1, Pallas kernels, on_device(): pl.pallas_call(stage_kernel, out_shape=(SDS((half_rows, width), BF16), SD...  1.1 us
  transfers between devices with their start and end apart: 7, of which 2 were waited for; matrix products, arithmetic and copies ran while one was open for 0% of the time, Pallas kernels for 31%

profile of v6, /device:TPU:2, one launch (start us, length us, event | category | flops | bytes accessed | tf_op | source)
XLA Modules:
  0.0 31.9 jit_solution(4721418804871026826)
XLA Ops:
  0.6 1.1 %stage.1 = (bf16[384,256]{1,0:T(8,128)(2,1)S(1)}, bf16[392,256]{1,0:T(8,128)(2,1)S(1)}) custom-call(s32[2,4,128]{2,1,0:T(4,128)} %target_hbm.1, bf16[2,4,128,256]{3,2,1,0:T(8,128)(2,1)} %agents_hbm.1), custom_call_target="tpu_custom_call" | custom-call | tf_op jit(solution)/shard_map/stage/pallas_call | solution.py:377
  1.7 1.6 %collective-permute-start = (bf16[392,256]{1,0:T(8,128)(2,1)S(1)}, bf16[392,256]{1,0:T(8,128)(2,1)S(1)}, u32[]{:S(2)}, u32[]{:S(2)}) collective-permute-start(bf16[392,256]{1,0:T(8,128)(2,1)S(1)} %get-tuple-element.23.inn_ref), channel_id=1, source_target_pairs={{0,16},{16,0},{1,17},{17,1},{2,18},{18,2},{3,19},{19,3},{4,20},{20... | collective-permute-start | bytes 602120 | tf_op jit(solution)/shard_map/ppermute | solution.py:389
  3.3 0.0 collective-permute-start.3
  3.3 2.5 %collective-permute-start.1 = (bf16[384,256]{1,0:T(8,128)(2,1)S(1)}, bf16[384,256]{1,0:T(8,128)(2,1)S(1)}, u32[]{:S(2)}, u32[]{:S(2)}) collective-permute-start(bf16[384,256]{1,0:T(8,128)(2,1)S(1)} %get-tuple-element.22.off_ref), channel_id=1, source_target_pairs={{2,1},{4,3},{6,5},{8,7},{10,9},{12,11},{14,13},{1,2},{3,4},{5,6},{... | collective-permute-start | bytes 589832 | tf_op jit(solution)/shard_map/ppermute | solution.py:391
  5.9 0.1 collective-permute-start.2
  6.0 4.1 %collective-permute-start.4 = (bf16[384,256]{1,0:T(8,128)(2,1)S(1)}, bf16[384,256]{1,0:T(8,128)(2,1)S(1)}, u32[]{:S(2)}, u32[]{:S(2)}) collective-permute-start(bf16[384,256]{1,0:T(8,128)(2,1)S(1)} %get-tuple-element.22.off_ref), channel_id=1, source_target_pairs={{2,17},{4,19},{6,21},{8,23},{10,25},{12,27},{14,29},{1,18},{3,20},... | collective-permute-start | bytes 589832 | tf_op jit(solution)/shard_map/ppermute | solution.py:393
  10.1 3.0 %local.1 = (bf16[256,768]{1,0:T(8,128)(2,1)S(1)}, bf16[256,256]{1,0:T(8,128)(2,1)S(1)}, bf16[384,256]{1,0:T(8,128)(2,1)S(1)}, bf16[384,1024]{1,0:T(8,128)(2,1)S(...) custom-call(s32[4,64]{1,0:T(4,128)} %fill_ref.1, s32[2,4,4]{2,1,0:T(4,128)} %near_ref.1, ...), custom_call_target="tpu_custom_call" | custom-call | flops 201326592 | bytes 8388608 | tf_op jit(solution)/shard_map/local/pallas_call | solution.py:394
  13.2 0.0 collective-permute-done.1.side_off_ref
  13.2 4.7 %collective-permute-done.2.other_off_ref = bf16[384,256]{1,0:T(8,128)(2,1)S(1)} collective-permute-done((bf16[384,256]{1,0:T(8,128)(2,1)S(1)}, bf16[384,256]{1,0:T(8,128)(2,1)S(1)}, u32[]{:S(2)}, u32[]{:S(2)}) %collective-permute-start.2) | collective-permute-done | bytes 196640 | tf_op jit(solution)/shard_map/ppermute | solution.py:390
  17.9 0.0 collective-permute-done.4.other_side_off_ref
  17.9 0.0 collective-permute-done.other_inn_ref
  17.9 0.0 collective-permute-done.3.side_inn_ref
  17.9 0.2 collective-permute-start.5
  18.1 0.4 %others.1.other_rows_ref = bf16[384,256]{1,0:T(8,128)(2,1)S(1)} custom-call(bf16[384,256]{1,0:T(8,128)(2,1)S(1)} %collective-permute-done.2.other_off_ref, bf16[392,256]{1,0:T(8,128)(2,1)S(1)} %collective-permute-done.other_inn_ref), custom_call_target="tpu_custom_call" | custom-call | flops 201326592 | bytes 2097152 | tf_op jit(solution)/shard_map/others/pallas_call | solution.py:422
  18.5 1.0 %collective-permute-done.5.other_side_inn_ref = bf16[392,256]{1,0:T(8,128)(2,1)S(1)} collective-permute-done((bf16[392,256]{1,0:T(8,128)(2,1)S(1)}, bf16[392,256]{1,0:T(8,128)(2,1)S(1)}, u32[]{:S(2)}, u32[]{:S(2)}) %collective-permute-start.5) | collective-permute-done | bytes 200736 | tf_op jit(solution)/shard_map/ppermute | solution.py:421
  19.4 0.0 copy-start
  19.4 0.0 copy-start.1
  19.4 0.0 copy-start.2
  19.4 4.6 %attention.1 = (bf16[768,256]{1,0:T(8,128)(2,1)S(1)}, bf16[384,256]{1,0:T(8,128)(2,1)S(1)}) custom-call(s32[8,10]{1,0:T(8,128)S(1)} %get-tuple-element.24.table_ref, bf16[384,256]{1,0:T(8,128)(2,1)S(1)} %get-tuple-element.22.off_ref, bf16[392,256]{1,0:T(8,128)(2,1)S(1)} %get-tuple-element.23.inn_ref, ...), custom_call_target="tpu_custom_call" | custom-call | flops 2315255808 | bytes 8388608 | tf_op jit(solution)/shard_map/attention/pallas_call | solution.py:440
  24.0 0.6 %collective-permute-start.6 = (bf16[384,256]{1,0:T(8,128)(2,1)S(1)}, bf16[384,256]{1,0:T(8,128)(2,1)S(1)}, u32[]{:S(2)}, u32[]{:S(2)}) collective-permute-start(bf16[384,256]{1,0:T(8,128)(2,1)S(1)} %get-tuple-element.41), channel_id=1, source_target_pairs={{0,16},{16,0},{1,17},{17,1},{2,18},{18,2},{3,19},{19,3},{4,20},{20... | collective-permute-start | bytes 589832 | tf_op jit(solution)/shard_map/ppermute | solution.py:473
  24.6 0.0 copy-done
  24.6 0.0 copy-done.1
  24.6 0.0 copy-done.2
  24.6 6.6 %policy.1 = (bf16[2,4,128,128]{3,2,1,0:T(8,128)(2,1)}, bf16[768,512]{1,0:T(8,128)(2,1)}) custom-call(s32[8,10]{1,0:T(8,128)S(1)} %get-tuple-element.24.table_ref, bf16[384,256]{1,0:T(8,128)(2,1)S(1)} %get-tuple-element.22.off_ref, bf16[392,256]{1,0:T(8,128)(2,1)S(1)} %get-tuple-element.23.inn_ref, bf16[768,256]{1,0:T(8,128)(2,1)S(1)} %get-tuple-element.36.summary_ref, ...), custom_call_target="tpu_custom_call" | custom-call | flops 4227858432 | bytes 12582912 | tf_op jit(solution)/shard_map/policy/pallas_call | solution.py:474
  31.2 0.0 collective-permute-done.6
  31.2 0.7 %bitcast_dynamic-update-slice_fusion = bf16[1,1,768,512]{3,2,1,0:T(8,128)(2,1)} fusion(bf16[1,1,768,512]{3,2,1,0:T(8,128)(2,1)} %bitcast.3, s32[]{:T(128)S(6)} %select_n.3, bf16[384,256]{1,0:T(8,128)(2,1)S(1)} %collective-permute-done.6), kind=kLoop, calls=%fused_computation | loop fusion | bytes 393220 | tf_op jit(solution)/shard_map/dynamic_update_slice | solution.py:506
Async XLA Ops:
  1.7 16.2 %collective-permute-start = (bf16[392,256]{1,0:T(8,128)(2,1)S(1)}, bf16[392,256]{1,0:T(8,128)(2,1)S(1)}, u32[]{:S(2)}, u32[]{:S(2)}) collective-permute-start(bf16[392,256]{1,0:T(8,128)(2,1)S(1)} %get-tuple-element.23.inn_ref), channel_id=1, source_target_pairs={{0,16},{16,0},{1,17},{17,1},{2,18},{18,2},{3,19},{19,3},{4,20},{20... | collective-permute-start | bytes 602120 | tf_op jit(solution)/shard_map/ppermute | solution.py:389
  3.3 14.6 %collective-permute-start.3 = (bf16[392,256]{1,0:T(8,128)(2,1)S(1)}, bf16[392,256]{1,0:T(8,128)(2,1)S(1)}, u32[]{:S(2)}, u32[]{:S(2)}) collective-permute-start(bf16[392,256]{1,0:T(8,128)(2,1)S(1)} %get-tuple-element.23.inn_ref), channel_id=1, source_target_pairs={{0,1},{1,0},{2,3},{3,2},{4,5},{5,4},{6,7},{7,6},{8,9},{9,8},{10,11... | collective-permute-start | bytes 602120 | tf_op jit(solution)/shard_map/ppermute | solution.py:392
  3.3 9.8 %collective-permute-start.1 = (bf16[384,256]{1,0:T(8,128)(2,1)S(1)}, bf16[384,256]{1,0:T(8,128)(2,1)S(1)}, u32[]{:S(2)}, u32[]{:S(2)}) collective-permute-start(bf16[384,256]{1,0:T(8,128)(2,1)S(1)} %get-tuple-element.22.off_ref), channel_id=1, source_target_pairs={{2,1},{4,3},{6,5},{8,7},{10,9},{12,11},{14,13},{1,2},{3,4},{5,6},{... | collective-permute-start | bytes 589832 | tf_op jit(solution)/shard_map/ppermute | solution.py:391
  5.9 12.0 %collective-permute-start.2 = (bf16[384,256]{1,0:T(8,128)(2,1)S(1)}, bf16[384,256]{1,0:T(8,128)(2,1)S(1)}, u32[]{:S(2)}, u32[]{:S(2)}) collective-permute-start(bf16[384,256]{1,0:T(8,128)(2,1)S(1)} %get-tuple-element.22.off_ref), channel_id=1, source_target_pairs={{0,16},{16,0},{1,17},{17,1},{2,18},{18,2},{3,19},{19,3},{4,20},{20... | collective-permute-start | bytes 589832 | tf_op jit(solution)/shard_map/ppermute | solution.py:390
  6.0 11.9 %collective-permute-start.4 = (bf16[384,256]{1,0:T(8,128)(2,1)S(1)}, bf16[384,256]{1,0:T(8,128)(2,1)S(1)}, u32[]{:S(2)}, u32[]{:S(2)}) collective-permute-start(bf16[384,256]{1,0:T(8,128)(2,1)S(1)} %get-tuple-element.22.off_ref), channel_id=1, source_target_pairs={{2,17},{4,19},{6,21},{8,23},{10,25},{12,27},{14,29},{1,18},{3,20},... | collective-permute-start | bytes 589832 | tf_op jit(solution)/shard_map/ppermute | solution.py:393
  17.9 1.5 %collective-permute-start.5 = (bf16[392,256]{1,0:T(8,128)(2,1)S(1)}, bf16[392,256]{1,0:T(8,128)(2,1)S(1)}, u32[]{:S(2)}, u32[]{:S(2)}) collective-permute-start(bf16[392,256]{1,0:T(8,128)(2,1)S(1)} %collective-permute-done.other_inn_ref), channel_id=1, source_target_pairs={{0,1},{1,0},{2,3},{3,2},{4,5},{5,4},{6,7},{7,6},{8,9},{9,8},{10,11... | collective-permute-start | bytes 602120 | tf_op jit(solution)/shard_map/ppermute | solution.py:421
  19.4 5.2 %copy-start = (bf16[2,1024,1024]{2,1,0:T(8,128)(2,1)S(1)}, bf16[2,1024,1024]{2,1,0:T(8,128)(2,1)}, u32[]{:S(2)}) copy-start(bf16[2,1024,1024]{2,1,0:T(8,128)(2,1)} %policy_mid_ref.1) | copy-start | bytes 12582916
  19.4 5.2 %copy-start.1 = (bf16[512,1024]{1,0:T(8,128)(2,1)S(1)}, bf16[512,1024]{1,0:T(8,128)(2,1)}, u32[]{:S(2)}) copy-start(bf16[512,1024]{1,0:T(8,128)(2,1)} %policy_in_ref.1) | copy-start | bytes 3145732
  19.4 5.2 %copy-start.2 = (bf16[1024,128]{1,0:T(8,128)(2,1)S(1)}, bf16[1024,128]{1,0:T(8,128)(2,1)}, u32[]{:S(2)}) copy-start(bf16[1024,128]{1,0:T(8,128)(2,1)} %policy_out_ref.1) | copy-start | bytes 786436
  24.0 7.2 %collective-permute-start.6 = (bf16[384,256]{1,0:T(8,128)(2,1)S(1)}, bf16[384,256]{1,0:T(8,128)(2,1)S(1)}, u32[]{:S(2)}, u32[]{:S(2)}) collective-permute-start(bf16[384,256]{1,0:T(8,128)(2,1)S(1)} %get-tuple-element.41), channel_id=1, source_target_pairs={{0,16},{16,0},{1,17},{17,1},{2,18},{18,2},{3,19},{19,3},{4,20},{20... | collective-permute-start | bytes 589832 | tf_op jit(solution)/shard_map/ppermute | solution.py:473

commit v7 on v6

--- a/solution.py
+++ b/solution.py
@@ -214,14 +214,17 @@
         (1, at_side_off, other_side_off_ref),
         (1, at_side_inn, other_side_inn_ref),
     )
-    for o, column, ref in sources:
-        rows = ref[:half_rows]
+    for s in range(0, len(sources), 4):
+        group = sources[s : s + 4]
+        rows = jnp.concatenate([ref[:half_rows] for _, _, ref in group], axis=0)
         both = jnp.dot(rows, weight_in_ref[:, width:], preferred_element_type=F32).astype(BF16)
-        both = both.reshape(each, LIVE, 2 * width)
-        for x in range(blocks_x):
-            at = (o * blocks_x + x) * columns + column
-            keys_ref[pl.ds(at, REACH)] = both[x * REACH : (x + 1) * REACH, :, :width]
-            values_ref[pl.ds(at, REACH)] = both[x * REACH : (x + 1) * REACH, :, width:]
+        both = both.reshape(len(group) * each, LIVE, 2 * width)
+        for g, (o, column, _) in enumerate(group):
+            for x in range(blocks_x):
+                at = (o * blocks_x + x) * columns + column
+                first = g * each + x * REACH
+                keys_ref[pl.ds(at, REACH)] = both[first : first + REACH, :, :width]
+                values_ref[pl.ds(at, REACH)] = both[first : first + REACH, :, width:]
 
     key_blocks = table_ref.shape[1] // 2
     lane = lax.broadcasted_iota(jnp.int32, (1, key_blocks * LIVE), 1)

time: 32.2 us -> 32.1 us (level)
  no operation moved by 1% of the time
where the time goes in v7:
time: 32.1 us; the launch traced here: 31.9 us
  Pallas kernels  15.6 us (49%)
  starting transfers between devices  9.14 us (28%)
  waiting for transfers between devices  5.69 us (18%)
  local copies, waits for them, and re-layouts  0.7 us (2%)
  between operations  0.7 us (2%)
    pallas_call x1, Pallas kernels, on_device(): pl.pallas_call(policy_kernel, out_shape=(SDS((blocks_x, blocks_y, block_l...  6.58 us
    ppermute x1, waiting for transfers between devices, on_device(): other_off = lax.ppermute(off, 'gx', swap)  4.72 us
    pallas_call x1, Pallas kernels, on_device(): pl.pallas_call(attention_kernel, out_shape=(SDS((slots, width), BF16), SD...  4.58 us
    ppermute x1, starting transfers between devices, on_device(): other_side_off = lax.ppermute(off, ('gx', 'gy'), diagonal)  4.1 us
    pallas_call x1, Pallas kernels, on_device(): pl.pallas_call(local_kernel, out_shape=(SDS(attention_in.shape, BF16), SD...  3.01 us
    ppermute x1, starting transfers between devices, on_device(): side_off = lax.ppermute(off, 'gy', across)  2.54 us
    ppermute x1, starting transfers between devices, on_device(): other_inn = lax.ppermute(inn, 'gx', swap)  1.58 us
    pallas_call x1, Pallas kernels, on_device(): pl.pallas_call(stage_kernel, out_shape=(SDS((half_rows, width), BF16), SD...  1.1 us
  transfers between devices with their start and end apart: 7, of which 2 were waited for; matrix products, arithmetic and copies ran while one was open for 0% of the time, Pallas kernels for 31%

profile of v7, /device:TPU:2, one launch (start us, length us, event | category | flops | bytes accessed | tf_op | source)
XLA Modules:
  0.0 31.9 jit_solution(405337058421749304)
XLA Ops:
  0.6 1.1 %stage.1 = (bf16[384,256]{1,0:T(8,128)(2,1)S(1)}, bf16[392,256]{1,0:T(8,128)(2,1)S(1)}) custom-call(s32[2,4,128]{2,1,0:T(4,128)} %target_hbm.1, bf16[2,4,128,256]{3,2,1,0:T(8,128)(2,1)} %agents_hbm.1), custom_call_target="tpu_custom_call" | custom-call | tf_op jit(solution)/shard_map/stage/pallas_call | solution.py:380
  1.7 1.6 %collective-permute-start = (bf16[392,256]{1,0:T(8,128)(2,1)S(1)}, bf16[392,256]{1,0:T(8,128)(2,1)S(1)}, u32[]{:S(2)}, u32[]{:S(2)}) collective-permute-start(bf16[392,256]{1,0:T(8,128)(2,1)S(1)} %get-tuple-element.23.inn_ref), channel_id=1, source_target_pairs={{0,16},{16,0},{1,17},{17,1},{2,18},{18,2},{3,19},{19,3},{4,20},{20... | collective-permute-start | bytes 602120 | tf_op jit(solution)/shard_map/ppermute | solution.py:392
  3.3 0.0 collective-permute-start.3
  3.3 2.5 %collective-permute-start.1 = (bf16[384,256]{1,0:T(8,128)(2,1)S(1)}, bf16[384,256]{1,0:T(8,128)(2,1)S(1)}, u32[]{:S(2)}, u32[]{:S(2)}) collective-permute-start(bf16[384,256]{1,0:T(8,128)(2,1)S(1)} %get-tuple-element.22.off_ref), channel_id=1, source_target_pairs={{2,1},{4,3},{6,5},{8,7},{10,9},{12,11},{14,13},{1,2},{3,4},{5,6},{... | collective-permute-start | bytes 589832 | tf_op jit(solution)/shard_map/ppermute | solution.py:394
  5.9 0.1 collective-permute-start.2
  6.0 4.1 %collective-permute-start.4 = (bf16[384,256]{1,0:T(8,128)(2,1)S(1)}, bf16[384,256]{1,0:T(8,128)(2,1)S(1)}, u32[]{:S(2)}, u32[]{:S(2)}) collective-permute-start(bf16[384,256]{1,0:T(8,128)(2,1)S(1)} %get-tuple-element.22.off_ref), channel_id=1, source_target_pairs={{2,17},{4,19},{6,21},{8,23},{10,25},{12,27},{14,29},{1,18},{3,20},... | collective-permute-start | bytes 589832 | tf_op jit(solution)/shard_map/ppermute | solution.py:396
  10.1 3.0 %local.1 = (bf16[256,768]{1,0:T(8,128)(2,1)S(1)}, bf16[256,256]{1,0:T(8,128)(2,1)S(1)}, bf16[384,256]{1,0:T(8,128)(2,1)S(1)}, bf16[384,1024]{1,0:T(8,128)(2,1)S(...) custom-call(s32[4,64]{1,0:T(4,128)} %fill_ref.1, s32[2,4,4]{2,1,0:T(4,128)} %near_ref.1, ...), custom_call_target="tpu_custom_call" | custom-call | flops 201326592 | bytes 8388608 | tf_op jit(solution)/shard_map/local/pallas_call | solution.py:397
  13.2 0.0 collective-permute-done.1.side_off_ref
  13.2 4.7 %collective-permute-done.2.other_off_ref = bf16[384,256]{1,0:T(8,128)(2,1)S(1)} collective-permute-done((bf16[384,256]{1,0:T(8,128)(2,1)S(1)}, bf16[384,256]{1,0:T(8,128)(2,1)S(1)}, u32[]{:S(2)}, u32[]{:S(2)}) %collective-permute-start.2) | collective-permute-done | bytes 196640 | tf_op jit(solution)/shard_map/ppermute | solution.py:393
  17.9 0.0 collective-permute-done.4.other_side_off_ref
  17.9 0.0 collective-permute-done.other_inn_ref
  17.9 0.0 collective-permute-done.3.side_inn_ref
  17.9 0.2 collective-permute-start.5
  18.1 0.4 %others.1.other_rows_ref = bf16[384,256]{1,0:T(8,128)(2,1)S(1)} custom-call(bf16[384,256]{1,0:T(8,128)(2,1)S(1)} %collective-permute-done.2.other_off_ref, bf16[392,256]{1,0:T(8,128)(2,1)S(1)} %collective-permute-done.other_inn_ref), custom_call_target="tpu_custom_call" | custom-call | flops 201326592 | bytes 2097152 | tf_op jit(solution)/shard_map/others/pallas_call | solution.py:425
  18.5 1.0 %collective-permute-done.5.other_side_inn_ref = bf16[392,256]{1,0:T(8,128)(2,1)S(1)} collective-permute-done((bf16[392,256]{1,0:T(8,128)(2,1)S(1)}, bf16[392,256]{1,0:T(8,128)(2,1)S(1)}, u32[]{:S(2)}, u32[]{:S(2)}) %collective-permute-start.5) | collective-permute-done | bytes 200736 | tf_op jit(solution)/shard_map/ppermute | solution.py:424
  19.4 0.0 copy-start
  19.4 0.0 copy-start.1
  19.4 0.0 copy-start.2
  19.4 4.6 %attention.1 = (bf16[768,256]{1,0:T(8,128)(2,1)S(1)}, bf16[384,256]{1,0:T(8,128)(2,1)S(1)}) custom-call(s32[8,10]{1,0:T(8,128)S(1)} %get-tuple-element.24.table_ref, bf16[384,256]{1,0:T(8,128)(2,1)S(1)} %get-tuple-element.22.off_ref, bf16[392,256]{1,0:T(8,128)(2,1)S(1)} %get-tuple-element.23.inn_ref, ...), custom_call_target="tpu_custom_call" | custom-call | flops 2315255808 | bytes 8388608 | tf_op jit(solution)/shard_map/attention/pallas_call | solution.py:443
  24.0 0.6 %collective-permute-start.6 = (bf16[384,256]{1,0:T(8,128)(2,1)S(1)}, bf16[384,256]{1,0:T(8,128)(2,1)S(1)}, u32[]{:S(2)}, u32[]{:S(2)}) collective-permute-start(bf16[384,256]{1,0:T(8,128)(2,1)S(1)} %get-tuple-element.41), channel_id=1, source_target_pairs={{0,16},{16,0},{1,17},{17,1},{2,18},{18,2},{3,19},{19,3},{4,20},{20... | collective-permute-start | bytes 589832 | tf_op jit(solution)/shard_map/ppermute | solution.py:476
  24.6 0.0 copy-done
  24.6 0.0 copy-done.1
  24.6 0.0 copy-done.2
  24.6 6.6 %policy.1 = (bf16[2,4,128,128]{3,2,1,0:T(8,128)(2,1)}, bf16[768,512]{1,0:T(8,128)(2,1)}) custom-call(s32[8,10]{1,0:T(8,128)S(1)} %get-tuple-element.24.table_ref, bf16[384,256]{1,0:T(8,128)(2,1)S(1)} %get-tuple-element.22.off_ref, bf16[392,256]{1,0:T(8,128)(2,1)S(1)} %get-tuple-element.23.inn_ref, bf16[768,256]{1,0:T(8,128)(2,1)S(1)} %get-tuple-element.36.summary_ref, ...), custom_call_target="tpu_custom_call" | custom-call | flops 4227858432 | bytes 12582912 | tf_op jit(solution)/shard_map/policy/pallas_call | solution.py:477
  31.2 0.0 collective-permute-done.6
  31.2 0.7 %bitcast_dynamic-update-slice_fusion = bf16[1,1,768,512]{3,2,1,0:T(8,128)(2,1)} fusion(bf16[1,1,768,512]{3,2,1,0:T(8,128)(2,1)} %bitcast.3, s32[]{:T(128)S(6)} %select_n.3, bf16[384,256]{1,0:T(8,128)(2,1)S(1)} %collective-permute-done.6), kind=kLoop, calls=%fused_computation | loop fusion | bytes 393220 | tf_op jit(solution)/shard_map/dynamic_update_slice | solution.py:509
Async XLA Ops:
  1.7 16.2 %collective-permute-start = (bf16[392,256]{1,0:T(8,128)(2,1)S(1)}, bf16[392,256]{1,0:T(8,128)(2,1)S(1)}, u32[]{:S(2)}, u32[]{:S(2)}) collective-permute-start(bf16[392,256]{1,0:T(8,128)(2,1)S(1)} %get-tuple-element.23.inn_ref), channel_id=1, source_target_pairs={{0,16},{16,0},{1,17},{17,1},{2,18},{18,2},{3,19},{19,3},{4,20},{20... | collective-permute-start | bytes 602120 | tf_op jit(solution)/shard_map/ppermute | solution.py:392
  3.3 14.6 %collective-permute-start.3 = (bf16[392,256]{1,0:T(8,128)(2,1)S(1)}, bf16[392,256]{1,0:T(8,128)(2,1)S(1)}, u32[]{:S(2)}, u32[]{:S(2)}) collective-permute-start(bf16[392,256]{1,0:T(8,128)(2,1)S(1)} %get-tuple-element.23.inn_ref), channel_id=1, source_target_pairs={{0,1},{1,0},{2,3},{3,2},{4,5},{5,4},{6,7},{7,6},{8,9},{9,8},{10,11... | collective-permute-start | bytes 602120 | tf_op jit(solution)/shard_map/ppermute | solution.py:395
  3.3 9.8 %collective-permute-start.1 = (bf16[384,256]{1,0:T(8,128)(2,1)S(1)}, bf16[384,256]{1,0:T(8,128)(2,1)S(1)}, u32[]{:S(2)}, u32[]{:S(2)}) collective-permute-start(bf16[384,256]{1,0:T(8,128)(2,1)S(1)} %get-tuple-element.22.off_ref), channel_id=1, source_target_pairs={{2,1},{4,3},{6,5},{8,7},{10,9},{12,11},{14,13},{1,2},{3,4},{5,6},{... | collective-permute-start | bytes 589832 | tf_op jit(solution)/shard_map/ppermute | solution.py:394
  5.9 12.0 %collective-permute-start.2 = (bf16[384,256]{1,0:T(8,128)(2,1)S(1)}, bf16[384,256]{1,0:T(8,128)(2,1)S(1)}, u32[]{:S(2)}, u32[]{:S(2)}) collective-permute-start(bf16[384,256]{1,0:T(8,128)(2,1)S(1)} %get-tuple-element.22.off_ref), channel_id=1, source_target_pairs={{0,16},{16,0},{1,17},{17,1},{2,18},{18,2},{3,19},{19,3},{4,20},{20... | collective-permute-start | bytes 589832 | tf_op jit(solution)/shard_map/ppermute | solution.py:393
  6.0 11.9 %collective-permute-start.4 = (bf16[384,256]{1,0:T(8,128)(2,1)S(1)}, bf16[384,256]{1,0:T(8,128)(2,1)S(1)}, u32[]{:S(2)}, u32[]{:S(2)}) collective-permute-start(bf16[384,256]{1,0:T(8,128)(2,1)S(1)} %get-tuple-element.22.off_ref), channel_id=1, source_target_pairs={{2,17},{4,19},{6,21},{8,23},{10,25},{12,27},{14,29},{1,18},{3,20},... | collective-permute-start | bytes 589832 | tf_op jit(solution)/shard_map/ppermute | solution.py:396
  17.9 1.5 %collective-permute-start.5 = (bf16[392,256]{1,0:T(8,128)(2,1)S(1)}, bf16[392,256]{1,0:T(8,128)(2,1)S(1)}, u32[]{:S(2)}, u32[]{:S(2)}) collective-permute-start(bf16[392,256]{1,0:T(8,128)(2,1)S(1)} %collective-permute-done.other_inn_ref), channel_id=1, source_target_pairs={{0,1},{1,0},{2,3},{3,2},{4,5},{5,4},{6,7},{7,6},{8,9},{9,8},{10,11... | collective-permute-start | bytes 602120 | tf_op jit(solution)/shard_map/ppermute | solution.py:424
  19.4 5.2 %copy-start = (bf16[2,1024,1024]{2,1,0:T(8,128)(2,1)S(1)}, bf16[2,1024,1024]{2,1,0:T(8,128)(2,1)}, u32[]{:S(2)}) copy-start(bf16[2,1024,1024]{2,1,0:T(8,128)(2,1)} %policy_mid_ref.1) | copy-start | bytes 12582916
  19.4 5.2 %copy-start.1 = (bf16[512,1024]{1,0:T(8,128)(2,1)S(1)}, bf16[512,1024]{1,0:T(8,128)(2,1)}, u32[]{:S(2)}) copy-start(bf16[512,1024]{1,0:T(8,128)(2,1)} %policy_in_ref.1) | copy-start | bytes 3145732
  19.4 5.2 %copy-start.2 = (bf16[1024,128]{1,0:T(8,128)(2,1)S(1)}, bf16[1024,128]{1,0:T(8,128)(2,1)}, u32[]{:S(2)}) copy-start(bf16[1024,128]{1,0:T(8,128)(2,1)} %policy_out_ref.1) | copy-start | bytes 786436
  24.0 7.2 %collective-permute-start.6 = (bf16[384,256]{1,0:T(8,128)(2,1)S(1)}, bf16[384,256]{1,0:T(8,128)(2,1)S(1)}, u32[]{:S(2)}, u32[]{:S(2)}) collective-permute-start(bf16[384,256]{1,0:T(8,128)(2,1)S(1)} %get-tuple-element.41), channel_id=1, source_target_pairs={{0,16},{16,0},{1,17},{17,1},{2,18},{18,2},{3,19},{19,3},{4,20},{20... | collective-permute-start | bytes 589832 | tf_op jit(solution)/shard_map/ppermute | solution.py:476
